TPU v7x, 256 devices: a whole 4x4x8 slice. The times are simulated.
256 devices in a mesh: seq: 32 (over x, y, core), head: 8 (over z).
Axes of the slice: x: 4, y: 4, z: 8, core: 2. Of those that a mesh axis runs over, the one named last changes fastest.
Arguments:
- hidden: bfloat16 [49152, 4096], P('seq', 'head'), may hold values from -6 to 6
- norm_gain: float32 [4096], replicated, may hold values from 0.1 to 1.9
- w_query: bfloat16 [4096, 4096], P(None, 'head'), may hold values from -0.09375 to 0.09375
- w_out: bfloat16 [4096, 4096], P('head'), may hold values from -0.5 to 0.5
- keys: bfloat16 [49152, 1024], P('seq', 'head'), may hold values from -240 to 240
- values: bfloat16 [49152, 1024], P('seq', 'head'), may hold values from -6 to 6
- cand_count: int32 [32], P('seq'), may hold values from 1 to 384, 3072 in all
- cand_pos: int32 [12288], P('seq'), may hold values from 0 to 1535, as said below
Outputs:
- slot_update: bfloat16 [12288, 4096], P('seq', 'head')
Inputs may be any that keep to these rules, and one draw needn't show every extreme that they name: `cand_pos`: each shard's 384 slots hold distinct positions within that shard; its first cand_count slots are the used ones. `cand_count`: the counts sum to 3072.
All inputs are finite; a program needn't handle non-finite values. No bound on the sum of `cand_count` on one device may be relied on, other than what follows from the above.
Results may differ from a plain program's by a relative error of at most 0.019.
The roundings to bfloat16 on the way count: a program that leaves them out, or rounds other values in their place, can miss the bound.
Values may be sent and summed in bfloat16 or wider, within the bound.
No kernel may reach another device: no remote copies, remote signals or barrier semaphores. Data moves between devices by JAX's collectives and lax.ppermute only.
A program may use at most 128 MiB of HBM per device.

v0:
```python
import functools
import math

import jax
import jax.numpy as jnp
from jax import lax
from jax.experimental import pallas as pl
from jax.experimental.pallas import tpu as pltpu
from jax.sharding import Mesh
from jax.sharding import PartitionSpec as P

HEAD = 128
HEADS = 4
ROWS = 128
GROUP = 16
META = 128
TILE = 32
SEQ = ("seq_0", "seq_1", "seq_2")
EPS = 1e-05
ROPE_BASE = 500000.0
NEG = -1e30
BF = jnp.bfloat16
F32 = jnp.float32
VM = pl.BlockSpec(memory_space=pltpu.VMEM)
SM = pl.BlockSpec(memory_space=pltpu.SMEM)
ANY = pl.BlockSpec(memory_space=pl.ANY)
HB = pl.BlockSpec(memory_space=pltpu.HBM)


def iota(shape, dim):
    return lax.broadcasted_iota(jnp.int32, shape, dim)


def onehot(mask):
    return jnp.where(mask, 1.0, 0.0).astype(BF)


def call(kernel, out, specs, *args, flops=0, moved=0, limit=20, **kw):
    return pl.pallas_call(
        kernel,
        out_shape=out,
        in_specs=specs,
        out_specs=jax.tree.map(lambda _: VM, out),
        cost_estimate=pl.CostEstimate(flops=flops, bytes_accessed=moved, transcendentals=0),
        compiler_params=pltpu.CompilerParams(vmem_limit_bytes=limit << 20),
        **kw,
    )(*args)


def seq_place():
    place = jnp.int32(0)
    for a in SEQ:
        place = place * lax.axis_size(a) + lax.axis_index(a)
    return place


def pack_kernel(shards, count, pos, hidden, out):
    s, count = seq_place(), count[0]
    slots, tokens, width = pos.shape[0], hidden.shape[0], hidden.shape[1]
    where = pos[...].reshape(1, slots)
    block = 128
    for b in range(shards * GROUP // block):
        o = iota((block, slots), 0) + b * block
        k = o & (GROUP - 1)
        slot = k * shards + (((o // GROUP) - s + shards) & (shards - 1))
        at = jnp.sum(
            jnp.where(iota((block, slots), 1) == slot, where, 0).astype(F32),
            axis=1,
            keepdims=True,
        ).astype(jnp.int32)
        oc = iota((block, 1), 0) + b * block
        kc = oc & (GROUP - 1)
        slot_c = kc * shards + (((oc // GROUP) - s + shards) & (shards - 1))
        live = (kc < slots // shards) & (slot_c < count)
        pick = onehot((iota((block, tokens), 1) == at) & live)
        rows = slice(b * block, (b + 1) * block)
        out[rows, :width] = jnp.dot(pick, hidden[...], preferred_element_type=F32).astype(BF)
        token = at + s * tokens
        lane = iota((block, META), 1)
        meta = jnp.where(lane == 0, token // 256, jnp.where(lane == 1, token & 255, 1))
        meta = jnp.where((lane < 3) & live, meta, 0)
        out[rows, width:] = meta.astype(F32).astype(BF)


def turn_kernel(values, out):
    out[...] = values[...].T


def compact_kernel(got, rows_out, meta_out, back_out):
    n = got.shape[0]
    width = got.shape[1] - META
    meta = got[:, width:]
    lower = onehot(iota((n, n), 0) >= iota((n, n), 1))
    running = jnp.dot(lower, meta, preferred_element_type=F32)[:, 2:3]
    live = meta.astype(F32)[:, 2:3]
    spare = ROWS - running[n - 1 : n, :]
    target = jnp.where(live > 0.5, running - 1.0 + spare, -1.0)
    back = jnp.where(iota((n, ROWS), 1).astype(F32) == target, 1.0, 0.0)
    back_out[...] = back.astype(BF)
    place = back.T.astype(BF)
    rows_out[...] = jnp.dot(place, got[:, :width], preferred_element_type=F32).astype(BF)
    meta_out[...] = jnp.dot(place, meta, preferred_element_type=F32).astype(BF)


def project_kernel(order, z, meta, gain, cosine, sine, weight, *refs):
    sources, (out, held, xs, sem, xsem) = refs[:-5], refs[-5:]
    width = xs.shape[2]
    n = len(sources)
    for k, x in enumerate(sources):
        pltpu.make_async_copy(x, xs.at[k], xsem.at[k]).start()
    spots = []
    for k, delta in enumerate(order):
        block = (z[0] + delta + n) & (n - 1)
        at = pl.ds(pl.multiple_of(block * width, width), width)
        pltpu.make_async_copy(weight.at[at], held.at[k], sem.at[k]).start()
        spots.append(at)
    total = jnp.zeros((ROWS, 1), F32)
    for k, x in enumerate(sources):
        pltpu.make_async_copy(x, xs.at[k], xsem.at[k]).wait()
        w = xs[k].astype(F32)
        total += jnp.sum(w * w, axis=1, keepdims=True)
    inv = lax.rsqrt(total / (n * width) + EPS)
    acc = jnp.zeros((ROWS, weight.shape[1]), F32)
    for k in range(n):
        normed = (xs[k].astype(F32) * inv * gain[:, spots[k]]).astype(BF)
        pltpu.make_async_copy(weight.at[spots[k]], held.at[k], sem.at[k]).wait()
        acc += jnp.dot(normed, held[k], preferred_element_type=F32)
    scale = 1.0 / math.sqrt(HEAD)
    for h in range(HEADS):
        at = slice(h * HEAD, (h + 1) * HEAD)
        part = acc[:, at]
        turned = part * cosine[...] + pltpu.roll(part, HEAD // 2, 1) * sine[...]
        out[:, at] = (turned * scale).astype(BF)
    out[:, HEADS * HEAD :] = meta[...]


def three(x):
    a = x.astype(BF).astype(F32)
    b = (x - a).astype(BF).astype(F32)
    return a, b, x - a - b


def collect_kernel(*refs):
    n = (len(refs) - 3) // 2
    keys, values = refs[:n], refs[n : 2 * n]
    kbuf, vbuf, sem = refs[2 * n :]
    copies = []
    for i in range(n):
        copies.append(pltpu.make_async_copy(keys[i], kbuf.at[i], sem.at[0, i]))
        copies.append(
            pltpu.make_async_copy(values[i], vbuf.at[i, pl.ds(0, HEAD)], sem.at[1, i])
        )
    for copy in copies:
        copy.start()
    vbuf[:, HEAD:, :] = jnp.ones((n, vbuf.shape[1] - HEAD, vbuf.shape[2]), BF)
    for copy in copies:
        copy.wait()


def collect(all_k, all_v):
    n = len(all_k)
    tokens = all_k[0].shape[0]
    return call(
        collect_kernel,
        (
            jax.ShapeDtypeStruct((n, tokens, HEAD), BF),
            jax.ShapeDtypeStruct((n, HEAD + 16, tokens), BF),
        ),
        [ANY] * (2 * n),
        *all_k,
        *all_v,
        scratch_shapes=[pltpu.SemaphoreType.DMA((2, n))],
    )


def attend_kernel(
    shard_ids, first_q, second_q, kbuf, vbuf, first_out, second_out,
    qbuf, place, even, odd, acc, peak, tops, steps,
):
    n, tokens = kbuf.shape[0], kbuf.shape[1]
    tiles = ROWS // TILE
    side = TILE * HEADS
    big = 2 * side
    lane = iota((8, ROWS), 1)
    spots = []
    for c, query in enumerate((first_q, second_q)):
        meta = query[:, HEADS * HEAD :].astype(F32).T
        row_pos = meta[0:1, :] * 256.0 + meta[1:2, :]
        row_pos = jnp.where(meta[2:3, :] > 0.5, row_pos, -1.0)
        spots.append(row_pos)
        wide = jnp.broadcast_to(row_pos, (8, ROWS))
        for t in range(tiles):
            rows = slice(t * TILE, (t + 1) * TILE)
            spot = jnp.zeros((8, ROWS), F32)
            for h in range(HEADS):
                into = slice(c * side + h * TILE, c * side + (h + 1) * TILE)
                qbuf[t, into, :] = query[rows, h * HEAD : (h + 1) * HEAD]
                moved = pltpu.roll(wide, (h * TILE - t * TILE) % ROWS, 1)
                spot = jnp.where((lane >= h * TILE) & (lane < (h + 1) * TILE), moved, spot)
            place[t, :, c * side : (c + 1) * side] = spot.astype(jnp.int32)
    acc[...] = jnp.zeros_like(acc)
    peak[...] = jnp.full_like(peak, NEG)

    def below(limit):
        found = [jnp.sum(jnp.where(p < limit, 1.0, 0.0)).astype(jnp.int32) for p in spots]
        return jnp.minimum(*found), jnp.maximum(*found)

    bounds = []
    for i in range(n):
        start = (shard_ids[i] * tokens).astype(F32)
        bounds.append((below(start)[0], below(start + tokens)[1]))
    count = jnp.int32(0)
    clear = count
    for masked in (False, True):
        for i in range(n):
            least, most = bounds[i]
            for t in range(tiles):
                steps[count] = i * tiles + t
                cut = t * TILE < most
                here = (t >= least // TILE) & (cut if masked else ~cut)
                count += here.astype(jnp.int32)
        if not masked:
            clear = count
    for k in range(3):
        steps[count + k] = n * tiles

    def parts(code):
        none = code >= n * tiles
        i = jnp.where(none, 0, code // tiles)
        return i, jnp.where(none, 0, code % tiles), none

    span = 2 * HEAD

    def advance(made, into, made_top, used_step, source, top, masked):
        if made is not None:
            i, t, none = parts(made)
            start = jnp.where(none, 1 << 30, shard_ids[i] * tokens)
            rel = place[t] - start - iota((8, big), 0)
            best = jnp.full((8, big), -jnp.inf, F32)
        if used_step is not None:
            ui, ut, _ = parts(used_step)
            before = peak[ut][0:1, :]
            now = jnp.maximum(before, jnp.max(top[...], axis=0, keepdims=True))
            peak[ut] = jnp.broadcast_to(now, (8, big))
            summed = acc[ut] * jnp.exp(before - now)
        for k in range(tokens // span):
            at = slice(k * span, (k + 1) * span)
            if made is not None:
                s = lax.dot_general(
                    kbuf[i, at, :], qbuf[t], (((1,), (1,)), ((), ())), preferred_element_type=F32
                ).reshape(span // 8, 8, big)
                if masked:
                    keep = rel[None] >= 8 * iota((span // 8, 8, big), 0) + k * span
                    s = jnp.where(keep, s, -jnp.inf)
                best = jnp.maximum(best, jnp.max(s, axis=0))
                into[at, :] = s.reshape(span, big)
            if used_step is not None:
                weight = jnp.exp(source[at, :] - now).astype(BF)
                summed += jnp.dot(vbuf[ui, :, at], weight, preferred_element_type=F32)
        if used_step is not None:
            acc[ut] = summed
        if made is not None:
            made_top[...] = best

    def run(first, last, masked):
        def pair(j, _):
            a, b, c = steps[2 * j], steps[2 * j + 1], steps[2 * j + 2]
            advance(b, odd, tops.at[1], a, even, tops.at[0], masked)
            advance(c, even, tops.at[0], b, odd, tops.at[1], masked)
            return 0

        advance(steps[2 * first], even, tops.at[0], None, None, None, masked)
        lax.fori_loop(first, last, pair, 0)

    run(0, clear // 2, False)
    run(clear // 2, (count + 1) // 2, True)

    for c, out in enumerate((first_out, second_out)):
        lanes = slice(c * side, (c + 1) * side)
        for t in range(tiles):
            rows = slice(t * TILE, (t + 1) * TILE)
            numer = acc[t, :HEAD, lanes].T.astype(BF)
            pieces = three(peak[t, 0:1, lanes]) + three(acc[t, HEAD : HEAD + 1, lanes])
            block = jnp.zeros((META, side), F32)
            row = iota((META, side), 0)
            for k, piece in enumerate(pieces):
                block = jnp.where(row == k, piece, block)
            block = block.T
            stats = jnp.zeros((TILE, META), F32)
            for h in range(HEADS):
                out[rows, h * HEAD : (h + 1) * HEAD] = numer[h * TILE : (h + 1) * TILE, :]
                part = block[h * TILE : (h + 1) * TILE, :]
                stats += pltpu.roll(part, 8 * h, 1) if h else part
            out[rows, HEADS * HEAD :] = stats.astype(BF)


def attend(shard_ids, first_q, second_q, kbuf, vbuf):
    n, tokens = kbuf.shape[0], kbuf.shape[1]
    big = 2 * TILE * HEADS
    tiles = ROWS // TILE
    return call(
        attend_kernel,
        (jax.ShapeDtypeStruct((ROWS, HEADS * HEAD + META), BF),) * 2,
        [SM, VM, VM, VM, VM],
        shard_ids,
        first_q,
        second_q,
        kbuf,
        vbuf,
        flops=10**10,
        moved=7 * 10**6,
        scratch_shapes=[
            pltpu.VMEM((tiles, big, HEAD), BF),
            pltpu.VMEM((tiles, 8, big), jnp.int32),
            pltpu.VMEM((tokens, big), F32),
            pltpu.VMEM((tokens, big), F32),
            pltpu.VMEM((tiles, HEAD + 16, big), F32),
            pltpu.VMEM((tiles, 8, big), F32),
            pltpu.VMEM((2, 8, big), F32),
            pltpu.SMEM((n * tiles + 8,), jnp.int32),
        ],
    )


def output_kernel(weight, *refs):
    parts, out = refs[:-1], refs[-1]
    peaks, totals = [], []
    for part in parts:
        meta = part[:, HEADS * HEAD :].astype(F32)
        shifted = [meta] + [pltpu.roll(meta, META - c, 1) for c in range(1, 6)]
        peaks.append(shifted[0] + shifted[1] + shifted[2])
        totals.append(shifted[3] + shifted[4] + shifted[5])
    top = functools.reduce(jnp.maximum, peaks)
    fades = [jnp.exp(p - top) for p in peaks]
    denom = sum(f * t for f, t in zip(fades, totals))
    cols = []
    for h in range(HEADS):
        at = slice(h * HEAD, (h + 1) * HEAD)
        col = slice(8 * h, 8 * h + 1)
        numer = sum(f[:, col] * p[:, at].astype(F32) for f, p in zip(fades, parts))
        d = denom[:, col]
        cols.append((numer / jnp.where(d > 0.0, d, 1.0)).astype(BF))
    mixed = jnp.concatenate(cols, axis=1)
    width = out.shape[2]
    for z in range(out.shape[0]):
        out[z] = jnp.dot(
            mixed, weight[:, z * width : (z + 1) * width], preferred_element_type=F32
        ).astype(BF)


def spread_kernel(back, parts, out):
    total = parts[0].astype(F32)
    for z in range(1, parts.shape[0]):
        total += parts[z].astype(F32)
    out[...] = jnp.dot(back[...], total.astype(BF), preferred_element_type=F32).astype(BF)


def unpack_kernel(shards, count, got, out):
    s, count = seq_place(), count[0]
    slots, n = out.shape[0], got.shape[0]
    slot = iota((slots, n), 0)
    source = ((slot + s) & (shards - 1)) * GROUP + slot // shards
    pick = onehot((iota((slots, n), 1) == source) & (slot < count))
    out[...] = jnp.dot(pick, got[...], preferred_element_type=F32).astype(BF)


def shift(n, k):
    return [(i, (i + k) % n) for i in range(n)]


def body(hidden, norm_gain, w_query, w_out, keys, values, cand_count, cand_pos):
    x, y, c = (lax.axis_index(a) for a in SEQ)
    z = lax.axis_index("head")
    nx, ny, nc, nz = (lax.axis_size(a) for a in (*SEQ, "head"))
    shards = nx * ny * nc
    slots = cand_pos.shape[0]
    width = hidden.shape[1]
    lanes = shards * GROUP

    send = call(
        functools.partial(pack_kernel, shards),
        jax.ShapeDtypeStruct((lanes, width + META), BF),
        [SM, VM, VM],
        cand_count,
        cand_pos,
        hidden,
    )
    swap = [(0, 1), (1, 0)]
    keys, values, send = lax.optimization_barrier((keys, values, send))
    values = call(turn_kernel, jax.ShapeDtypeStruct(values.shape[::-1], BF), [VM], values)
    got = lax.all_to_all(send.reshape(shards, GROUP, -1), SEQ, 0, 0, tiled=True)
    got = got.reshape(lanes, -1)
    k_left, v_left = (
        lax.ppermute(a, SEQ[0], shift(nx, 1)) for a in (keys, values)
    )
    k_right, v_right = (
        lax.ppermute(a, SEQ[0], shift(nx, -1)) for a in (keys, values)
    )
    rows, meta, back = call(
        compact_kernel,
        (
            jax.ShapeDtypeStruct((ROWS, width), BF),
            jax.ShapeDtypeStruct((ROWS, META), BF),
            jax.ShapeDtypeStruct((lanes, ROWS), BF),
        ),
        [VM],
        got,
        flops=5 * 10**9,
        moved=10**6,
    )
    up, down = rows, rows
    slices, order = [rows], [0]
    for k in range(1, nz // 2 + 1):
        up = lax.ppermute(up, "head", shift(nz, 1))
        slices.append(up)
        order.append(-k)
        if k < nz // 2:
            down = lax.ppermute(down, "head", shift(nz, -1))
            slices.append(down)
            order.append(k)
            up, down = lax.optimization_barrier((up, down))

    k_far = lax.ppermute(k_left, SEQ[0], shift(nx, 1))
    v_far = lax.ppermute(v_right, SEQ[0], shift(nx, -1))
    near_k, near_v = [keys, k_left, k_right, k_far], [values, v_left, v_right, v_far]
    all_k = near_k + [lax.ppermute(a, SEQ[2], swap) for a in near_k[:3]]
    all_v = near_v + [lax.ppermute(a, SEQ[2], swap) for a in near_v[:3]]
    all_k.append(lax.ppermute(k_far, SEQ[2], swap))
    all_v.append(lax.ppermute(v_far, SEQ[2], swap))
    places = [((x + d) % nx, cc) for cc in (c, 1 - c) for d in (0, nx - 1, 1, 2)]
    shard_ids = jnp.stack([(px * ny + y) * nc + pc for px, pc in places]).astype(jnp.int32)

    half = HEAD // 2
    freq = jnp.exp(-math.log(ROPE_BASE) * 2.0 * jnp.arange(half, dtype=F32) / HEAD)
    meta_f = meta[:, :2].astype(F32)
    angle = (meta_f[:, 0:1] * 256.0 + meta_f[:, 1:2]) * freq[None, :]
    cosine, sine = jnp.cos(angle), jnp.sin(angle)
    cosine = jnp.concatenate([cosine, cosine], axis=1)
    sine = jnp.concatenate([-sine, sine], axis=1)

    w_query = pltpu.with_memory_space_constraint(w_query, pltpu.HBM)
    slices = [pltpu.with_memory_space_constraint(a, pltpu.HBM) for a in slices]
    query = call(
        functools.partial(project_kernel, tuple(order)),
        jax.ShapeDtypeStruct((ROWS, HEADS * HEAD + META), BF),
        [SM, VM, VM, VM, VM, HB] + [HB] * nz,
        z.reshape(1).astype(jnp.int32),
        meta,
        norm_gain.reshape(1, -1),
        cosine,
        sine,
        w_query,
        *slices,
        scratch_shapes=[
            pltpu.VMEM((nz, width, w_query.shape[1]), BF),
            pltpu.VMEM((nz, ROWS, width), BF),
            pltpu.SemaphoreType.DMA((nz,)),
            pltpu.SemaphoreType.DMA((nz,)),
        ],
    )

    asked = [(k, lax.ppermute(query, SEQ[1], shift(ny, k))) for k in (1, ny - 1, 2)]
    kbuf, vbuf = collect(all_k, all_v)
    (ka, qa), (kb, qb), (kc, qc) = asked
    own, ra = attend(shard_ids, query, qa, kbuf, vbuf)
    qb, qc, ra = lax.optimization_barrier((qb, qc, ra))
    ra = lax.ppermute(ra, SEQ[1], shift(ny, -ka))
    rb, rc = attend(shard_ids, qb, qc, kbuf, vbuf)
    parts = [own, ra]
    for k, r in ((kb, rb), (kc, rc)):
        parts.append(lax.ppermute(r, SEQ[1], shift(ny, -k)))

    partial = call(
        output_kernel,
        jax.ShapeDtypeStruct((nz, ROWS, width), BF),
        [VM] * (1 + ny),
        w_out,
        *parts,
    )
    arrived = lax.all_to_all(partial, "head", 0, 0, tiled=True)
    to_send = call(
        spread_kernel, jax.ShapeDtypeStruct((lanes, width), BF), [VM, VM], back, arrived
    )
    returned = lax.all_to_all(to_send.reshape(shards, GROUP, width), SEQ, 0, 0, tiled=True)
    return call(
        functools.partial(unpack_kernel, shards),
        jax.ShapeDtypeStruct((slots, width), BF),
        [SM, VM],
        cand_count,
        returned.reshape(lanes, width),
    )


def solution(mesh):
    split = Mesh(
        mesh.devices.reshape(4, 4, 2, mesh.shape["head"]), ("seq_0", "seq_1", "seq_2", "head")
    )
    placed = (
        P(SEQ, "head"),
        P(),
        P(None, "head"),
        P("head", None),
        P(SEQ, "head"),
        P(SEQ, "head"),
        P(SEQ),
        P(SEQ),
    )

    return jax.shard_map(
        body, mesh=split, in_specs=placed, out_specs=P(SEQ, "head"), check_vma=False
    )
```

profile of v0, /device:TPU:1, one launch (start us, length us, event | category | flops | bytes accessed | tf_op | source)
XLA Modules:
  0.0 173.6 jit_solution(14335126742360998607)
XLA Ops:
  0.7 1.4 copy-done.1
  2.7 1.2 shard_map.82
  3.9 21.3 %all_to_all.15 = bf16[32,16,640]{2,1,0:T(8,128)(2,1)S(1)} all-to-all(bf16[32,16,640]{2,1,0:T(8,128)(2,1)S(1)} %bitcast.14), channel_id=1, replica_groups=mesh['seq_0'=4,'seq_1'=4,'seq_2'=2,'head'=8] {'seq_0','seq_1','seq_2'}, dimensions={0} | all-to-all | bytes 1310720 | tf_op jit(solution)/shard_map/all_to_all | solution.py:391
  26.0 1.7 collective-permute-start
  27.7 4.0 %collective-permute-start.1 = (bf16[128,512]{1,0:T(8,128)(2,1)S(1)}, bf16[128,512]{1,0:T(8,128)(2,1)S(1)}, u32[]{:S(2)}, u32[]{:S(2)}) collective-permute-start(bf16[128,512]{1,0:T(8,128)(2,1)S(1)} %get-tuple-element.28.refs_0_), channel_id=1, source_target_pairs={{0,7},{1,0},{2,1},{3,2},{4,3},{5,4},{6,5},{7,6},{8,15},{9,8},{10,9... | collective-permute-start | bytes 393224 | tf_op jit(solution)/shard_map/ppermute | solution.py:418
  31.8 3.9 %collective-permute-done.refs_1_ = bf16[128,512]{1,0:T(8,128)(2,1)S(1)} collective-permute-done((bf16[128,512]{1,0:T(8,128)(2,1)S(1)}, bf16[128,512]{1,0:T(8,128)(2,1)S(1)}, u32[]{:S(2)}, u32[]{:S(2)}) %collective-permute-start) | collective-permute-done | bytes 131104 | tf_op jit(solution)/shard_map/ppermute | solution.py:414
  37.1 2.9 %collective-permute-start.3 = (bf16[128,512]{1,0:T(8,128)(2,1)S(1)}, bf16[128,512]{1,0:T(8,128)(2,1)S(1)}, u32[]{:S(2)}, u32[]{:S(2)}) collective-permute-start(bf16[128,512]{1,0:T(8,128)(2,1)S(1)} %collective-permute-done.1.refs_2_), channel_id=1, source_target_pairs={{0,7},{1,0},{2,1},{3,2},{4,3},{5,4},{6,5},{7,6},{8,15},{9,8},{10,9... | collective-permute-start | bytes 393224 | tf_op jit(solution)/shard_map/ppermute | solution.py:418
  40.1 1.4 collective-permute-done.2.refs_3_
  41.7 1.6 collective-permute-done.3.refs_4_
  44.2 2.7 %collective-permute-start.4 = (bf16[128,512]{1,0:T(8,128)(2,1)S(1)}, bf16[128,512]{1,0:T(8,128)(2,1)S(1)}, u32[]{:S(2)}, u32[]{:S(2)}) collective-permute-start(bf16[128,512]{1,0:T(8,128)(2,1)S(1)} %collective-permute-done.2.refs_3_), channel_id=1, source_target_pairs={{0,1},{1,2},{2,3},{3,4},{4,5},{5,6},{6,7},{7,0},{8,9},{9,10},{10,1... | collective-permute-start | bytes 393224 | tf_op jit(solution)/shard_map/ppermute | solution.py:414
  46.8 1.5 collective-permute-start.5
  48.4 3.0 %collective-permute-start.18 = (bf16[128,1536]{1,0:T(8,128)(2,1)S(1)}, bf16[128,1536]{1,0:T(8,128)(2,1)S(1)}, u32[]{:S(2)}, u32[]{:S(2)}) collective-permute-start(bf16[128,1536]{1,0:T(8,128)(2,1)S(1)} %shard_map.85.refs_8_), channel_id=1, source_target_pairs={{0,8},{8,0},{1,9},{9,1},{2,10},{10,2},{3,11},{11,3},{4,12},{12,4},... | collective-permute-start | bytes 1179656 | tf_op jit(solution)/shard_map/ppermute | solution.py:427
  51.4 3.1 %collective-permute-done.16.refs_10_ = bf16[128,1536]{1,0:T(8,128)(2,1)S(1)} collective-permute-done((bf16[128,1536]{1,0:T(8,128)(2,1)S(1)}, bf16[128,1536]{1,0:T(8,128)(2,1)S(1)}, u32[]{:S(2)}, u32[]{:S(2)}) %collective-permute-start.16) | collective-permute-done | bytes 393248 | tf_op jit(solution)/shard_map/ppermute | solution.py:397
  54.5 1.6 collective-permute-start.12
  56.7 2.7 %collective-permute-start.17 = (bf16[128,1536]{1,0:T(8,128)(2,1)S(1)}, bf16[128,1536]{1,0:T(8,128)(2,1)}, u32[]{:S(2)}, u32[]{:S(2)}) collective-permute-start(bf16[128,1536]{1,0:T(8,128)(2,1)S(1)} %collective-permute-done.16.refs_10_), channel_id=1, source_target_pairs={{0,192},{64,0},{128,64},{192,128},{1,193},{65,1},{129,65},{193,129... | collective-permute-start | bytes 1179656 | tf_op jit(solution)/shard_map/ppermute | solution.py:424
  60.0 1.7 collective-permute-start.6
  62.5 1.3 collective-permute-start.13
  63.9 1.1 collective-permute-done.10.refs_3_
  65.1 2.2 %collective-permute-start.20 = (bf16[128,1536]{1,0:T(8,128)(2,1)S(1)}, bf16[128,1536]{1,0:T(8,128)(2,1)}, u32[]{:S(2)}, u32[]{:S(2)}) collective-permute-start(bf16[128,1536]{1,0:T(8,128)(2,1)S(1)} %collective-permute-done.16.refs_10_), channel_id=1, source_target_pairs={{0,8},{8,0},{1,9},{9,1},{2,10},{10,2},{3,11},{11,3},{4,12},{12,4},... | collective-permute-start | bytes 1179656 | tf_op jit(solution)/shard_map/ppermute | solution.py:427
  67.2 1.5 collective-permute-start.14
  70.7 4.5 %shard_map.84.first_q = bf16[128,640]{1,0:T(8,128)(2,1)} custom-call(s32[1]{0:T(128)} %bitcast.10.z, bf16[128,128]{1,0:T(8,128)(2,1)S(1)} %copy-done.7, f32[1,4096]{1,0:T(1,128)S(1)} %bitcast.18, f32[128,128]{1,0:T(8,128)S(1)} %get-tuple-element.48.cosine, f32[128,128]{1,0:T(8,128)S(1)} %get-tuple-element.49.sine, bf16[4096,512]{1,0:T(8,128)(2,1)} %weight.2, ...), custom_call_target="tpu_custom_call" | custom-call | tf_op jit(solution)/shard_map/pallas_call | solution.py:39
  76.0 2.8 %collective-permute-start.22 = (bf16[128,640]{1,0:T(8,128)(2,1)}, bf16[128,640]{1,0:T(8,128)(2,1)S(1)}, u32[]{:S(2)}, u32[]{:S(2)}) collective-permute-start(bf16[128,640]{1,0:T(8,128)(2,1)} %shard_map.84.first_q), channel_id=1, source_target_pairs={{0,48},{16,0},{32,16},{48,32},{1,49},{17,1},{33,17},{49,33},{2,50}... | collective-permute-start | bytes 491528 | tf_op jit(solution)/shard_map/ppermute | solution.py:462
  79.8 3.4 %shard_map.86 = (bf16[8,1536,128]{2,1,0:T(8,128)(2,1)S(1)}, bf16[8,144,1536]{2,1,0:T(8,128)(2,1)S(1)}) custom-call(bf16[1536,128]{1,0:T(8,128)(2,1)S(1)} %copy-done.2, bf16[1536,128]{1,0:T(8,128)(2,1)S(1)} %collective-permute-done.8.refs_1_, bf16[1536,128]{1,0:T(8,128)(2,1)S(1)} %collective-permute-done.9.refs_2_, ...), custom_call_target="tpu_custom_call" | custom-call | tf_op jit(solution)/shard_map/pallas_call | solution.py:39
  83.3 11.7 %shard_map.87 = (bf16[128,640]{1,0:T(8,128)(2,1)S(1)}, bf16[128,640]{1,0:T(8,128)(2,1)S(1)}) custom-call(s32[8]{0:T(128)S(1)} %stack.35.shard_ids, bf16[128,640]{1,0:T(8,128)(2,1)} %shard_map.84.first_q, bf16[128,640]{1,0:T(8,128)(2,1)} %collective-permute-done.7.second_q, bf16[8,1536,128]{2,1,0:T(8,128)(2,1)S(1)} %get-tuple-element.36.kbuf, ...), custom_call_target="tpu_custom_call" | custom-call | flops 10000000000 | bytes 7000000 | tf_op jit(solution)/shard_map/pallas_call | solution.py:39
  95.5 12.2 %shard_map.88 = (bf16[128,640]{1,0:T(8,128)(2,1)S(1)}, bf16[128,640]{1,0:T(8,128)(2,1)S(1)}) custom-call(s32[8]{0:T(128)S(1)} %stack.35.shard_ids, bf16[128,640]{1,0:T(8,128)(2,1)S(1)} %collective-permute-done.22.first_q, bf16[128,640]{1,0:T(8,128)(2,1)S(1)} %collective-permute-done.23.second_q, bf16[8,1536,128]{2,1,0:T(8,128)(2,1)S(1)} %get-tuple-element.36.kbuf, ...), custom_call_target="tpu_custom_call" | custom-call | flops 10000000000 | bytes 7000000 | tf_op jit(solution)/shard_map/pallas_call | solution.py:39
  108.0 3.1 %collective-permute-start.26 = (bf16[128,640]{1,0:T(8,128)(2,1)S(1)}, bf16[128,640]{1,0:T(8,128)(2,1)S(1)}, u32[]{:S(2)}, u32[]{:S(2)}) collective-permute-start(bf16[128,640]{1,0:T(8,128)(2,1)S(1)} %get-tuple-element.44), channel_id=1, source_target_pairs={{0,32},{16,48},{32,0},{48,16},{1,33},{17,49},{33,1},{49,17},{2,34}... | collective-permute-start | bytes 491528 | tf_op jit(solution)/shard_map/ppermute | solution.py:471
  111.1 2.1 %collective-permute-done.25.refs_2_ = bf16[128,640]{1,0:T(8,128)(2,1)S(1)} collective-permute-done((bf16[128,640]{1,0:T(8,128)(2,1)S(1)}, bf16[128,640]{1,0:T(8,128)(2,1)S(1)}, u32[]{:S(2)}, u32[]{:S(2)}) %collective-permute-start.25) | collective-permute-done | bytes 163872 | tf_op jit(solution)/shard_map/ppermute | solution.py:471
  113.2 3.8 %collective-permute-done.26.refs_3_ = bf16[128,640]{1,0:T(8,128)(2,1)S(1)} collective-permute-done((bf16[128,640]{1,0:T(8,128)(2,1)S(1)}, bf16[128,640]{1,0:T(8,128)(2,1)S(1)}, u32[]{:S(2)}, u32[]{:S(2)}) %collective-permute-start.26) | collective-permute-done | bytes 163872 | tf_op jit(solution)/shard_map/ppermute | solution.py:471
  117.0 1.4 shard_map.89
  118.5 29.3 %all_to_all.16.parts = bf16[8,128,512]{2,1,0:T(8,128)(2,1)S(1)} all-to-all(bf16[8,128,512]{2,1,0:T(8,128)(2,1)S(1)} %shard_map.89), channel_id=1, replica_groups=mesh['seq_0'=4,'seq_1'=4,'seq_2'=2,'head'=8] {'head'}, dimensions={0} | all-to-all | bytes 2097152 | tf_op jit(solution)/shard_map/all_to_all | solution.py:480
  148.1 24.3 %all_to_all.17 = bf16[32,16,512]{2,1,0:T(8,128)(2,1)S(1)} all-to-all(bf16[32,16,512]{2,1,0:T(8,128)(2,1)S(1)} %bitcast.15), channel_id=1, replica_groups=mesh['seq_0'=4,'seq_1'=4,'seq_2'=2,'head'=8] {'seq_0','seq_1','seq_2'}, dimensions={0} | all-to-all | bytes 1048576 | tf_op jit(solution)/shard_map/all_to_all | solution.py:484
  172.5 1.1 shard_map.91
  (81 shorter events, 11.1 us)
Async XLA Ops:
  25.2 44.6 %copy-start.11 = (f32[4096]{0:T(1024)S(1)}, f32[4096]{0:T(1024)}, u32[]{:S(2)}) copy-start(f32[4096]{0:T(1024)} %param.9) | copy-start | bytes 49156
  25.9 22.4 %copy-start.8 = (bf16[128,512]{1,0:T(8,128)(2,1)}, bf16[128,512]{1,0:T(8,128)(2,1)S(1)}, u32[]{:S(2)}) copy-start(bf16[128,512]{1,0:T(8,128)(2,1)S(1)} %get-tuple-element.28.refs_0_) | copy-start | bytes 393220
  26.0 25.4 %copy-start.6 = (bf16[128,128]{1,0:T(8,128)(2,1)}, bf16[128,128]{1,0:T(8,128)(2,1)S(1)}, u32[]{:S(2)}) copy-start(bf16[128,128]{1,0:T(8,128)(2,1)S(1)} %get-tuple-element.27.meta) | copy-start | bytes 98308
  26.0 25.4 %copy-start.9 = (bf16[512,128]{1,0:T(8,128)(2,1)}, bf16[512,128]{1,0:T(8,128)(2,1)S(1)}, u32[]{:S(2)}) copy-start(bf16[512,128]{1,0:T(8,128)(2,1)S(1)} %get-tuple-element.26.back) | copy-start | bytes 393220
  26.0 9.7 %collective-permute-start = (bf16[128,512]{1,0:T(8,128)(2,1)S(1)}, bf16[128,512]{1,0:T(8,128)(2,1)S(1)}, u32[]{:S(2)}, u32[]{:S(2)}) collective-permute-start(bf16[128,512]{1,0:T(8,128)(2,1)S(1)} %get-tuple-element.28.refs_0_), channel_id=1, source_target_pairs={{0,1},{1,2},{2,3},{3,4},{4,5},{5,6},{6,7},{7,0},{8,9},{9,10},{10,1... | collective-permute-start | bytes 393224 | tf_op jit(solution)/shard_map/ppermute | solution.py:414
  27.7 8.0 %collective-permute-start.1 = (bf16[128,512]{1,0:T(8,128)(2,1)S(1)}, bf16[128,512]{1,0:T(8,128)(2,1)S(1)}, u32[]{:S(2)}, u32[]{:S(2)}) collective-permute-start(bf16[128,512]{1,0:T(8,128)(2,1)S(1)} %get-tuple-element.28.refs_0_), channel_id=1, source_target_pairs={{0,7},{1,0},{2,1},{3,2},{4,3},{5,4},{6,5},{7,6},{8,15},{9,8},{10,9... | collective-permute-start | bytes 393224 | tf_op jit(solution)/shard_map/ppermute | solution.py:418
  31.7 12.4 %collective-permute-start.8 = (bf16[1536,128]{1,0:T(8,128)(2,1)S(1)}, bf16[1536,128]{1,0:T(8,128)(2,1)S(1)}, u32[]{:S(2)}, u32[]{:S(2)}) collective-permute-start(bf16[1536,128]{1,0:T(8,128)(2,1)S(1)} %copy-done.2), channel_id=1, source_target_pairs={{0,64},{64,128},{128,192},{192,0},{1,65},{65,129},{129,193},{193,1... | collective-permute-start | bytes 1179656 | tf_op jit(solution)/shard_map/ppermute | solution.py:394
  35.7 5.9 %collective-permute-start.2 = (bf16[128,512]{1,0:T(8,128)(2,1)S(1)}, bf16[128,512]{1,0:T(8,128)(2,1)S(1)}, u32[]{:S(2)}, u32[]{:S(2)}) collective-permute-start(bf16[128,512]{1,0:T(8,128)(2,1)S(1)} %collective-permute-done.refs_1_), channel_id=1, source_target_pairs={{0,1},{1,2},{2,3},{3,4},{4,5},{5,6},{6,7},{7,0},{8,9},{9,10},{10,1... | collective-permute-start | bytes 393224 | tf_op jit(solution)/shard_map/ppermute | solution.py:414
  35.7 11.1 %collective-permute-start.9 = (bf16[1536,128]{1,0:T(8,128)(2,1)S(1)}, bf16[1536,128]{1,0:T(8,128)(2,1)S(1)}, u32[]{:S(2)}, u32[]{:S(2)}) collective-permute-start(bf16[1536,128]{1,0:T(8,128)(2,1)S(1)} %copy-done.2), channel_id=1, source_target_pairs={{0,192},{64,0},{128,64},{192,128},{1,193},{65,1},{129,65},{193,129... | collective-permute-start | bytes 1179656 | tf_op jit(solution)/shard_map/ppermute | solution.py:397
  36.2 12.2 %collective-permute-start.11 = (bf16[1536,128]{1,0:T(8,128)(2,1)S(1)}, bf16[1536,128]{1,0:T(8,128)(2,1)S(1)}, u32[]{:S(2)}, u32[]{:S(2)}) collective-permute-start(bf16[1536,128]{1,0:T(8,128)(2,1)S(1)} %copy-done.2), channel_id=1, source_target_pairs={{0,8},{8,0},{1,9},{9,1},{2,10},{10,2},{3,11},{11,3},{4,12},{12,4},... | collective-permute-start | bytes 1179656 | tf_op jit(solution)/shard_map/ppermute | solution.py:426
  37.1 6.2 %collective-permute-start.3 = (bf16[128,512]{1,0:T(8,128)(2,1)S(1)}, bf16[128,512]{1,0:T(8,128)(2,1)S(1)}, u32[]{:S(2)}, u32[]{:S(2)}) collective-permute-start(bf16[128,512]{1,0:T(8,128)(2,1)S(1)} %collective-permute-done.1.refs_2_), channel_id=1, source_target_pairs={{0,7},{1,0},{2,1},{3,2},{4,3},{5,4},{6,5},{7,6},{8,15},{9,8},{10,9... | collective-permute-start | bytes 393224 | tf_op jit(solution)/shard_map/ppermute | solution.py:418
  41.6 12.9 %collective-permute-start.16 = (bf16[128,1536]{1,0:T(8,128)(2,1)S(1)}, bf16[128,1536]{1,0:T(8,128)(2,1)S(1)}, u32[]{:S(2)}, u32[]{:S(2)}) collective-permute-start(bf16[128,1536]{1,0:T(8,128)(2,1)S(1)} %shard_map.85.refs_8_), channel_id=1, source_target_pairs={{0,192},{64,0},{128,64},{192,128},{1,193},{65,1},{129,65},{193,129... | collective-permute-start | bytes 1179656 | tf_op jit(solution)/shard_map/ppermute | solution.py:397
  43.3 16.7 %collective-permute-start.15 = (bf16[128,1536]{1,0:T(8,128)(2,1)S(1)}, bf16[128,1536]{1,0:T(8,128)(2,1)S(1)}, u32[]{:S(2)}, u32[]{:S(2)}) collective-permute-start(bf16[128,1536]{1,0:T(8,128)(2,1)S(1)} %shard_map.85.refs_8_), channel_id=1, source_target_pairs={{0,64},{64,128},{128,192},{192,0},{1,65},{65,129},{129,193},{193,1... | collective-permute-start | bytes 1179656 | tf_op jit(solution)/shard_map/ppermute | solution.py:394
  44.2 10.3 %collective-permute-start.4 = (bf16[128,512]{1,0:T(8,128)(2,1)S(1)}, bf16[128,512]{1,0:T(8,128)(2,1)S(1)}, u32[]{:S(2)}, u32[]{:S(2)}) collective-permute-start(bf16[128,512]{1,0:T(8,128)(2,1)S(1)} %collective-permute-done.2.refs_3_), channel_id=1, source_target_pairs={{0,1},{1,2},{2,3},{3,4},{4,5},{5,6},{6,7},{7,0},{8,9},{9,10},{10,1... | collective-permute-start | bytes 393224 | tf_op jit(solution)/shard_map/ppermute | solution.py:414
  46.8 9.2 %collective-permute-start.5 = (bf16[128,512]{1,0:T(8,128)(2,1)S(1)}, bf16[128,512]{1,0:T(8,128)(2,1)S(1)}, u32[]{:S(2)}, u32[]{:S(2)}) collective-permute-start(bf16[128,512]{1,0:T(8,128)(2,1)S(1)} %collective-permute-done.3.refs_4_), channel_id=1, source_target_pairs={{0,7},{1,0},{2,1},{3,2},{4,3},{5,4},{6,5},{7,6},{8,15},{9,8},{10,9... | collective-permute-start | bytes 393224 | tf_op jit(solution)/shard_map/ppermute | solution.py:418
  48.4 14.1 %collective-permute-start.18 = (bf16[128,1536]{1,0:T(8,128)(2,1)S(1)}, bf16[128,1536]{1,0:T(8,128)(2,1)S(1)}, u32[]{:S(2)}, u32[]{:S(2)}) collective-permute-start(bf16[128,1536]{1,0:T(8,128)(2,1)S(1)} %shard_map.85.refs_8_), channel_id=1, source_target_pairs={{0,8},{8,0},{1,9},{9,1},{2,10},{10,2},{3,11},{11,3},{4,12},{12,4},... | collective-permute-start | bytes 1179656 | tf_op jit(solution)/shard_map/ppermute | solution.py:427
  54.5 10.6 %collective-permute-start.10 = (bf16[1536,128]{1,0:T(8,128)(2,1)S(1)}, bf16[1536,128]{1,0:T(8,128)(2,1)S(1)}, u32[]{:S(2)}, u32[]{:S(2)}) collective-permute-start(bf16[1536,128]{1,0:T(8,128)(2,1)S(1)} %collective-permute-done.8.refs_1_), channel_id=1, source_target_pairs={{0,64},{64,128},{128,192},{192,0},{1,65},{65,129},{129,193},{193,1... | collective-permute-start | bytes 1179656 | tf_op jit(solution)/shard_map/ppermute | solution.py:423
  54.5 12.7 %collective-permute-start.12 = (bf16[1536,128]{1,0:T(8,128)(2,1)S(1)}, bf16[1536,128]{1,0:T(8,128)(2,1)}, u32[]{:S(2)}, u32[]{:S(2)}) collective-permute-start(bf16[1536,128]{1,0:T(8,128)(2,1)S(1)} %collective-permute-done.8.refs_1_), channel_id=1, source_target_pairs={{0,8},{8,0},{1,9},{9,1},{2,10},{10,2},{3,11},{11,3},{4,12},{12,4},... | collective-permute-start | bytes 1179656 | tf_op jit(solution)/shard_map/ppermute | solution.py:426
  56.7 10.5 %collective-permute-start.17 = (bf16[128,1536]{1,0:T(8,128)(2,1)S(1)}, bf16[128,1536]{1,0:T(8,128)(2,1)}, u32[]{:S(2)}, u32[]{:S(2)}) collective-permute-start(bf16[128,1536]{1,0:T(8,128)(2,1)S(1)} %collective-permute-done.16.refs_10_), channel_id=1, source_target_pairs={{0,192},{64,0},{128,64},{192,128},{1,193},{65,1},{129,65},{193,129... | collective-permute-start | bytes 1179656 | tf_op jit(solution)/shard_map/ppermute | solution.py:424
  60.0 8.8 %collective-permute-start.6 = (bf16[128,512]{1,0:T(8,128)(2,1)}, bf16[128,512]{1,0:T(8,128)(2,1)S(1)}, u32[]{:S(2)}, u32[]{:S(2)}) collective-permute-start(bf16[128,512]{1,0:T(8,128)(2,1)} %copy-done.17), channel_id=1, source_target_pairs={{0,1},{1,2},{2,3},{3,4},{4,5},{5,6},{6,7},{7,0},{8,9},{9,10},{10,1... | collective-permute-start | bytes 393224 | tf_op jit(solution)/shard_map/ppermute | solution.py:414
  62.5 12.7 %collective-permute-start.13 = (bf16[1536,128]{1,0:T(8,128)(2,1)S(1)}, bf16[1536,128]{1,0:T(8,128)(2,1)S(1)}, u32[]{:S(2)}, u32[]{:S(2)}) collective-permute-start(bf16[1536,128]{1,0:T(8,128)(2,1)S(1)} %collective-permute-done.9.refs_2_), channel_id=1, source_target_pairs={{0,8},{8,0},{1,9},{9,1},{2,10},{10,2},{3,11},{11,3},{4,12},{12,4},... | collective-permute-start | bytes 1179656 | tf_op jit(solution)/shard_map/ppermute | solution.py:426
  65.1 13.7 %collective-permute-start.20 = (bf16[128,1536]{1,0:T(8,128)(2,1)S(1)}, bf16[128,1536]{1,0:T(8,128)(2,1)}, u32[]{:S(2)}, u32[]{:S(2)}) collective-permute-start(bf16[128,1536]{1,0:T(8,128)(2,1)S(1)} %collective-permute-done.16.refs_10_), channel_id=1, source_target_pairs={{0,8},{8,0},{1,9},{9,1},{2,10},{10,2},{3,11},{11,3},{4,12},{12,4},... | collective-permute-start | bytes 1179656 | tf_op jit(solution)/shard_map/ppermute | solution.py:427
  67.2 8.8 %collective-permute-start.19 = (bf16[128,1536]{1,0:T(8,128)(2,1)S(1)}, bf16[128,1536]{1,0:T(8,128)(2,1)}, u32[]{:S(2)}, u32[]{:S(2)}) collective-permute-start(bf16[128,1536]{1,0:T(8,128)(2,1)S(1)} %collective-permute-done.15.refs_9_), channel_id=1, source_target_pairs={{0,8},{8,0},{1,9},{9,1},{2,10},{10,2},{3,11},{11,3},{4,12},{12,4},... | collective-permute-start | bytes 1179656 | tf_op jit(solution)/shard_map/ppermute | solution.py:427
  67.2 11.6 %collective-permute-start.14 = (bf16[1536,128]{1,0:T(8,128)(2,1)S(1)}, bf16[1536,128]{1,0:T(8,128)(2,1)}, u32[]{:S(2)}, u32[]{:S(2)}) collective-permute-start(bf16[1536,128]{1,0:T(8,128)(2,1)S(1)} %collective-permute-done.10.refs_3_), channel_id=1, source_target_pairs={{0,8},{8,0},{1,9},{9,1},{2,10},{10,2},{3,11},{11,3},{4,12},{12,4},... | collective-permute-start | bytes 1179656 | tf_op jit(solution)/shard_map/ppermute | solution.py:428
  68.7 10.1 %collective-permute-start.21 = (bf16[128,1536]{1,0:T(8,128)(2,1)}, bf16[128,1536]{1,0:T(8,128)(2,1)}, u32[]{:S(2)}, u32[]{:S(2)}) collective-permute-start(bf16[128,1536]{1,0:T(8,128)(2,1)} %collective-permute-done.17.refs_11_), channel_id=1, source_target_pairs={{0,8},{8,0},{1,9},{9,1},{2,10},{10,2},{3,11},{11,3},{4,12},{12,4},... | collective-permute-start | bytes 1179656 | tf_op jit(solution)/shard_map/ppermute | solution.py:429
  76.0 7.3 %collective-permute-start.7 = (bf16[128,640]{1,0:T(8,128)(2,1)}, bf16[128,640]{1,0:T(8,128)(2,1)}, u32[]{:S(2)}, u32[]{:S(2)}) collective-permute-start(bf16[128,640]{1,0:T(8,128)(2,1)} %shard_map.84.first_q), channel_id=1, source_target_pairs={{0,16},{16,32},{32,48},{48,0},{1,17},{17,33},{33,49},{49,1},{2,18}... | collective-permute-start | bytes 491528 | tf_op jit(solution)/shard_map/ppermute | solution.py:462
  76.0 18.9 %collective-permute-start.22 = (bf16[128,640]{1,0:T(8,128)(2,1)}, bf16[128,640]{1,0:T(8,128)(2,1)S(1)}, u32[]{:S(2)}, u32[]{:S(2)}) collective-permute-start(bf16[128,640]{1,0:T(8,128)(2,1)} %shard_map.84.first_q), channel_id=1, source_target_pairs={{0,48},{16,0},{32,16},{48,32},{1,49},{17,1},{33,17},{49,33},{2,50}... | collective-permute-start | bytes 491528 | tf_op jit(solution)/shard_map/ppermute | solution.py:462
  78.8 16.1 %collective-permute-start.23 = (bf16[128,640]{1,0:T(8,128)(2,1)}, bf16[128,640]{1,0:T(8,128)(2,1)S(1)}, u32[]{:S(2)}, u32[]{:S(2)}) collective-permute-start(bf16[128,640]{1,0:T(8,128)(2,1)} %shard_map.84.first_q), channel_id=1, source_target_pairs={{0,32},{16,48},{32,0},{48,16},{1,33},{17,49},{33,1},{49,17},{2,34}... | collective-permute-start | bytes 491528 | tf_op jit(solution)/shard_map/ppermute | solution.py:462
  95.0 16.1 %collective-permute-start.24 = (bf16[128,640]{1,0:T(8,128)(2,1)S(1)}, bf16[128,640]{1,0:T(8,128)(2,1)S(1)}, u32[]{:S(2)}, u32[]{:S(2)}) collective-permute-start(bf16[128,640]{1,0:T(8,128)(2,1)S(1)} %get-tuple-element.40), channel_id=1, source_target_pairs={{0,48},{16,0},{32,16},{48,32},{1,49},{17,1},{33,17},{49,33},{2,50}... | collective-permute-start | bytes 491528 | tf_op jit(solution)/shard_map/ppermute | solution.py:467
  107.8 5.5 %collective-permute-start.25 = (bf16[128,640]{1,0:T(8,128)(2,1)S(1)}, bf16[128,640]{1,0:T(8,128)(2,1)S(1)}, u32[]{:S(2)}, u32[]{:S(2)}) collective-permute-start(bf16[128,640]{1,0:T(8,128)(2,1)S(1)} %get-tuple-element.43), channel_id=1, source_target_pairs={{0,16},{16,32},{32,48},{48,0},{1,17},{17,33},{33,49},{49,1},{2,18}... | collective-permute-start | bytes 491528 | tf_op jit(solution)/shard_map/ppermute | solution.py:471
  108.0 9.0 %collective-permute-start.26 = (bf16[128,640]{1,0:T(8,128)(2,1)S(1)}, bf16[128,640]{1,0:T(8,128)(2,1)S(1)}, u32[]{:S(2)}, u32[]{:S(2)}) collective-permute-start(bf16[128,640]{1,0:T(8,128)(2,1)S(1)} %get-tuple-element.44), channel_id=1, source_target_pairs={{0,32},{16,48},{32,0},{48,16},{1,33},{17,49},{33,1},{49,17},{2,34}... | collective-permute-start | bytes 491528 | tf_op jit(solution)/shard_map/ppermute | solution.py:471
  117.0 30.7 %copy-start.10 = (bf16[512,128]{1,0:T(8,128)(2,1)S(1)}, bf16[512,128]{1,0:T(8,128)(2,1)}, u32[]{:S(2)}) copy-start(bf16[512,128]{1,0:T(8,128)(2,1)} %copy-done.9) | copy-start | bytes 393220
  (15 other events, 100.4 us)
where the time goes:
time: 174 us
  blocking collectives  74.9 us (43%)
  Pallas kernels  36.8 us (21%)
  starting transfers between devices  36 us (21%)
  waiting for transfers between devices  17.1 us (10%)
  local copies, waits for them, and re-layouts  5.35 us (3%)
  other arithmetic  2.51 us (1%)
    pallas_call x10, Pallas kernels, call(): pl.pallas_call(kernel, out_shape=out, in_specs=specs, out_specs=jax.tree....  36.8 us
    all_to_all x1, blocking collectives, body(): arrived = lax.all_to_all(partial, 'head', 0, 0, tiled=True)  29.3 us
    all_to_all x1, blocking collectives, body(): lax.all_to_all(to_send.reshape(shards, GROUP, width), SEQ, 0, 0, tiled=True)  24.3 us
    all_to_all x1, blocking collectives, body(): got = lax.all_to_all(send.reshape(shards, GROUP, -1), SEQ, 0, 0, tiled=True)  21.3 us
    ppermute x3, starting transfers between devices, body(): down = lax.ppermute(down, 'head', shift(nz, -1))  8.41 us
    ppermute x4, starting transfers between devices, body(): up = lax.ppermute(up, 'head', shift(nz, 1))  6.2 us
    ppermute x2, waiting for transfers between devices, body(): parts.append(lax.ppermute(r, SEQ[1], shift(ny, -k)))  5.95 us
    ppermute x4, waiting for transfers between devices, body(): up = lax.ppermute(up, 'head', shift(nz, 1))  5.32 us
  transfers between devices with their start and end apart: 27, of which 7 were waited for; matrix products, arithmetic and copies ran while one was open for 1% of the time, Pallas kernels for 18%

commit v1 on v0

--- a/solution.py
+++ b/solution.py
@@ -459,16 +459,15 @@
         ],
     )
 
-    asked = [(k, lax.ppermute(query, SEQ[1], shift(ny, k))) for k in (1, ny - 1, 2)]
+    asked = [lax.ppermute(query, SEQ[1], shift(ny, k)) for k in (1, ny - 1)]
+    far = lax.ppermute(query, SEQ[1], shift(ny, 2))
     kbuf, vbuf = collect(all_k, all_v)
-    (ka, qa), (kb, qb), (kc, qc) = asked
-    own, ra = attend(shard_ids, query, qa, kbuf, vbuf)
-    qb, qc, ra = lax.optimization_barrier((qb, qc, ra))
-    ra = lax.ppermute(ra, SEQ[1], shift(ny, -ka))
-    rb, rc = attend(shard_ids, qb, qc, kbuf, vbuf)
-    parts = [own, ra]
-    for k, r in ((kb, rb), (kc, rc)):
-        parts.append(lax.ppermute(r, SEQ[1], shift(ny, -k)))
+    ra, rb = attend(shard_ids, *asked, kbuf, vbuf)
+    query, far, ra, rb = lax.optimization_barrier((query, far, ra, rb))
+    ra = lax.ppermute(ra, SEQ[1], shift(ny, -1))
+    rb = lax.ppermute(rb, SEQ[1], shift(ny, 1))
+    own, rc = attend(shard_ids, query, far, kbuf, vbuf)
+    parts = [own, ra, rb, lax.ppermute(rc, SEQ[1], shift(ny, -2))]
 
     partial = call(
         output_kernel,

time: 174 us -> 179 us (1.029)
  waiting for transfers between devices: 17.1 us -> 24.7 us
  starting transfers between devices: 36 us -> 31.3 us
  local copies, waits for them, and re-layouts: 5.35 us -> 8.68 us
  blocking collectives: 74.9 us -> 72.7 us
    ppermute x2, waiting for transfers between devices: 0.01 us -> 4.79 us  [body(): lax.ppermute(a, SEQ[0], shift(nx, 1))]
    ppermute x1, waiting for transfers between devices: 0.01 us -> 3.98 us  [body(): v_far = lax.ppermute(v_right, SEQ[0], shift(nx, -1))]
    all_to_all x1, blocking collectives: 24.3 us -> 20.6 us  [body(): lax.all_to_all(to_send.reshape(shards, GROUP, width), SEQ, 0, 0, tiled=True)]
    unnamed x40 -> x44, local copies, waits for them, and re-layouts: 5.26 us -> 8.6 us
    ppermute x2, waiting for transfers between devices: 3.08 us -> 0.01 us  [body(): lax.ppermute(a, SEQ[0], shift(nx, -1))]
    ppermute x1, starting transfers between devices: 2.68 us -> 0.01 us  [body(): v_far = lax.ppermute(v_right, SEQ[0], shift(nx, -1))]
    ppermute x2, starting transfers between devices: 0.52 us -> 3.07 us  [body(): lax.ppermute(a, SEQ[0], shift(nx, -1))]
    ppermute x3, starting transfers between devices: 8.41 us -> 6.12 us  [body(): down = lax.ppermute(down, 'head', shift(nz, -1))]
  transfers between devices with their start and end apart: 27 -> 27, of which waited for: 7 -> 9; matrix products, arithmetic and copies ran while one was open for 1% -> 1% of each run, Pallas kernels for 18% -> 11%
where the time goes in v1:
time: 179 us
  blocking collectives  72.7 us (41%)
  Pallas kernels  37.8 us (21%)
  starting transfers between devices  31.3 us (17%)
  waiting for transfers between devices  24.7 us (14%)
  local copies, waits for them, and re-layouts  8.68 us (5%)
  other arithmetic  2.48 us (1%)
    pallas_call x10, Pallas kernels, call(): pl.pallas_call(kernel, out_shape=out, in_specs=specs, out_specs=jax.tree....  37.8 us
    all_to_all x1, blocking collectives, body(): arrived = lax.all_to_all(partial, 'head', 0, 0, tiled=True)  30.8 us
    all_to_all x1, blocking collectives, body(): got = lax.all_to_all(send.reshape(shards, GROUP, -1), SEQ, 0, 0, tiled=True)  21.3 us
    all_to_all x1, blocking collectives, body(): lax.all_to_all(to_send.reshape(shards, GROUP, width), SEQ, 0, 0, tiled=True)  20.6 us
    unnamed x44, local copies, waits for them, and re-layouts  8.6 us
    ppermute x3, starting transfers between devices, body(): down = lax.ppermute(down, 'head', shift(nz, -1))  6.12 us
    ppermute x4, starting transfers between devices, body(): up = lax.ppermute(up, 'head', shift(nz, 1))  5.63 us
    ppermute x4, waiting for transfers between devices, body(): up = lax.ppermute(up, 'head', shift(nz, 1))  5.43 us
  transfers between devices with their start and end apart: 27, of which 9 were waited for; matrix products, arithmetic and copies ran while one was open for 1% of the time, Pallas kernels for 11%

profile of v1, /device:TPU:1, one launch (start us, length us, event | category | flops | bytes accessed | tf_op | source)
XLA Modules:
  0.0 178.5 jit_solution(15412955119594050625)
XLA Ops:
  0.7 1.4 copy-done.1
  2.7 1.2 shard_map.82
  3.9 21.3 %all_to_all.15 = bf16[32,16,640]{2,1,0:T(8,128)(2,1)S(1)} all-to-all(bf16[32,16,640]{2,1,0:T(8,128)(2,1)S(1)} %bitcast.14), channel_id=1, replica_groups=mesh['seq_0'=4,'seq_1'=4,'seq_2'=2,'head'=8] {'seq_0','seq_1','seq_2'}, dimensions={0} | all-to-all | bytes 1310720 | tf_op jit(solution)/shard_map/all_to_all | solution.py:391
  27.2 1.6 collective-permute-start
  28.8 3.9 %collective-permute-start.1 = (bf16[128,512]{1,0:T(8,128)(2,1)S(1)}, bf16[128,512]{1,0:T(8,128)(2,1)S(1)}, u32[]{:S(2)}, u32[]{:S(2)}) collective-permute-start(bf16[128,512]{1,0:T(8,128)(2,1)S(1)} %get-tuple-element.29.refs_0_), channel_id=1, source_target_pairs={{0,7},{1,0},{2,1},{3,2},{4,3},{5,4},{6,5},{7,6},{8,15},{9,8},{10,9... | collective-permute-start | bytes 393224 | tf_op jit(solution)/shard_map/ppermute | solution.py:418
  32.8 4.0 %collective-permute-done.refs_1_ = bf16[128,512]{1,0:T(8,128)(2,1)S(1)} collective-permute-done((bf16[128,512]{1,0:T(8,128)(2,1)S(1)}, bf16[128,512]{1,0:T(8,128)(2,1)S(1)}, u32[]{:S(2)}, u32[]{:S(2)}) %collective-permute-start) | collective-permute-done | bytes 131104 | tf_op jit(solution)/shard_map/ppermute | solution.py:414
  37.5 1.1 collective-permute-start.10
  38.6 2.7 %collective-permute-start.11 = (bf16[1536,128]{1,0:T(8,128)(2,1)S(1)}, bf16[1536,128]{1,0:T(8,128)(2,1)S(1)}, u32[]{:S(2)}, u32[]{:S(2)}) collective-permute-start(bf16[1536,128]{1,0:T(8,128)(2,1)S(1)} %copy-done.2), channel_id=1, source_target_pairs={{0,192},{64,0},{128,64},{192,128},{1,193},{65,1},{129,65},{193,129... | collective-permute-start | bytes 1179656 | tf_op jit(solution)/shard_map/ppermute | solution.py:397
  41.3 1.4 collective-permute-done.2.refs_3_
  42.7 1.2 collective-permute-start.3
  44.0 2.9 %collective-permute-done.3.refs_4_ = bf16[128,512]{1,0:T(8,128)(2,1)S(1)} collective-permute-done((bf16[128,512]{1,0:T(8,128)(2,1)S(1)}, bf16[128,512]{1,0:T(8,128)(2,1)S(1)}, u32[]{:S(2)}, u32[]{:S(2)}) %collective-permute-start.3) | collective-permute-done | bytes 131104 | tf_op jit(solution)/shard_map/ppermute | solution.py:418
  46.8 2.1 %collective-permute-start.20 = (bf16[128,1536]{1,0:T(8,128)(2,1)S(1)}, bf16[128,1536]{1,0:T(8,128)(2,1)S(1)}, u32[]{:S(2)}, u32[]{:S(2)}) collective-permute-start(bf16[128,1536]{1,0:T(8,128)(2,1)S(1)} %shard_map.85.refs_8_), channel_id=1, source_target_pairs={{0,8},{8,0},{1,9},{9,1},{2,10},{10,2},{3,11},{11,3},{4,12},{12,4},... | collective-permute-start | bytes 1179656 | tf_op jit(solution)/shard_map/ppermute | solution.py:427
  49.0 2.1 %collective-permute-start.4 = (bf16[128,512]{1,0:T(8,128)(2,1)S(1)}, bf16[128,512]{1,0:T(8,128)(2,1)S(1)}, u32[]{:S(2)}, u32[]{:S(2)}) collective-permute-start(bf16[128,512]{1,0:T(8,128)(2,1)S(1)} %collective-permute-done.2.refs_3_), channel_id=1, source_target_pairs={{0,1},{1,2},{2,3},{3,4},{4,5},{5,6},{6,7},{7,0},{8,9},{9,10},{10,1... | collective-permute-start | bytes 393224 | tf_op jit(solution)/shard_map/ppermute | solution.py:414
  52.1 4.8 %collective-permute-done.17.refs_9_ = bf16[128,1536]{1,0:T(8,128)(2,1)S(1)} collective-permute-done((bf16[128,1536]{1,0:T(8,128)(2,1)S(1)}, bf16[128,1536]{1,0:T(8,128)(2,1)S(1)}, u32[]{:S(2)}, u32[]{:S(2)}) %collective-permute-start.17) | collective-permute-done | bytes 393248 | tf_op jit(solution)/shard_map/ppermute | solution.py:394
  56.9 1.8 %collective-permute-start.13 = (bf16[1536,128]{1,0:T(8,128)(2,1)S(1)}, bf16[1536,128]{1,0:T(8,128)(2,1)S(1)}, u32[]{:S(2)}, u32[]{:S(2)}) collective-permute-start(bf16[1536,128]{1,0:T(8,128)(2,1)S(1)} %copy-done.2), channel_id=1, source_target_pairs={{0,8},{8,0},{1,9},{9,1},{2,10},{10,2},{3,11},{11,3},{4,12},{12,4},... | collective-permute-start | bytes 1179656 | tf_op jit(solution)/shard_map/ppermute | solution.py:426
  60.0 1.5 collective-permute-start.12
  62.0 1.8 %collective-permute-start.6 = (bf16[128,512]{1,0:T(8,128)(2,1)}, bf16[128,512]{1,0:T(8,128)(2,1)S(1)}, u32[]{:S(2)}, u32[]{:S(2)}) collective-permute-start(bf16[128,512]{1,0:T(8,128)(2,1)} %copy-done.19), channel_id=1, source_target_pairs={{0,1},{1,2},{2,3},{3,4},{4,5},{5,6},{6,7},{7,0},{8,9},{9,10},{10,1... | collective-permute-start | bytes 393224 | tf_op jit(solution)/shard_map/ppermute | solution.py:414
  65.5 4.0 %collective-permute-done.19.refs_11_ = bf16[128,1536]{1,0:T(8,128)(2,1)S(1)} collective-permute-done((bf16[128,1536]{1,0:T(8,128)(2,1)S(1)}, bf16[128,1536]{1,0:T(8,128)(2,1)S(1)}, u32[]{:S(2)}, u32[]{:S(2)}) %collective-permute-start.19) | collective-permute-done | bytes 393248 | tf_op jit(solution)/shard_map/ppermute | solution.py:424
  70.4 1.3 collective-permute-done.12.refs_3_
  75.1 4.5 %shard_map.84.first_q = bf16[128,640]{1,0:T(8,128)(2,1)} custom-call(s32[1]{0:T(128)} %bitcast.10.z, bf16[128,128]{1,0:T(8,128)(2,1)S(1)} %copy-done.9, f32[1,4096]{1,0:T(1,128)S(1)} %bitcast.18, f32[128,128]{1,0:T(8,128)S(1)} %get-tuple-element.50.cosine, f32[128,128]{1,0:T(8,128)S(1)} %get-tuple-element.51.sine, bf16[4096,512]{1,0:T(8,128)(2,1)} %weight.2, ...), custom_call_target="tpu_custom_call" | custom-call | tf_op jit(solution)/shard_map/pallas_call | solution.py:39
  82.0 1.9 %collective-permute-start.9 = (bf16[128,640]{1,0:T(8,128)(2,1)}, bf16[128,640]{1,0:T(8,128)(2,1)}, u32[]{:S(2)}, u32[]{:S(2)}) collective-permute-start(bf16[128,640]{1,0:T(8,128)(2,1)} %shard_map.84.first_q), channel_id=1, source_target_pairs={{0,48},{16,0},{32,16},{48,32},{1,49},{17,1},{33,17},{49,33},{2,50}... | collective-permute-start | bytes 491528 | tf_op jit(solution)/shard_map/ppermute | solution.py:462
  86.1 3.6 %shard_map.86 = (bf16[8,1536,128]{2,1,0:T(8,128)(2,1)S(1)}, bf16[8,144,1536]{2,1,0:T(8,128)(2,1)S(1)}) custom-call(bf16[1536,128]{1,0:T(8,128)(2,1)S(1)} %copy-done.2, bf16[1536,128]{1,0:T(8,128)(2,1)S(1)} %collective-permute-done.10.refs_1_, bf16[1536,128]{1,0:T(8,128)(2,1)S(1)} %collective-permute-done.11.refs_2_, ...), custom_call_target="tpu_custom_call" | custom-call | tf_op jit(solution)/shard_map/pallas_call | solution.py:39
  89.7 11.9 %shard_map.87 = (bf16[128,640]{1,0:T(8,128)(2,1)S(1)}, bf16[128,640]{1,0:T(8,128)(2,1)S(1)}) custom-call(s32[8]{0:T(128)S(1)} %stack.35.shard_ids, bf16[128,640]{1,0:T(8,128)(2,1)} %collective-permute-done.8.first_q, bf16[128,640]{1,0:T(8,128)(2,1)} %collective-permute-done.9.second_q, bf16[8,1536,128]{2,1,0:T(8,128)(2,1)S(1)} %get-tuple-element.37.kbuf, ...), custom_call_target="tpu_custom_call" | custom-call | flops 10000000000 | bytes 7000000 | tf_op jit(solution)/shard_map/pallas_call | solution.py:39
  101.6 12.8 %shard_map.88 = (bf16[128,640]{1,0:T(8,128)(2,1)S(1)}, bf16[128,640]{1,0:T(8,128)(2,1)S(1)}) custom-call(s32[8]{0:T(128)S(1)} %stack.35.shard_ids, bf16[128,640]{1,0:T(8,128)(2,1)} %shard_map.84.first_q, bf16[128,640]{1,0:T(8,128)(2,1)S(1)} %collective-permute-done.7.second_q, bf16[8,1536,128]{2,1,0:T(8,128)(2,1)S(1)} %get-tuple-element.37.kbuf, ...), custom_call_target="tpu_custom_call" | custom-call | flops 10000000000 | bytes 7000000 | tf_op jit(solution)/shard_map/pallas_call | solution.py:39
  114.4 2.1 %collective-permute-start.26 = (bf16[128,640]{1,0:T(8,128)(2,1)S(1)}, bf16[128,640]{1,0:T(8,128)(2,1)S(1)}, u32[]{:S(2)}, u32[]{:S(2)}) collective-permute-start(bf16[128,640]{1,0:T(8,128)(2,1)S(1)} %get-tuple-element.46), channel_id=1, source_target_pairs={{0,32},{16,48},{32,0},{48,16},{1,33},{17,49},{33,1},{49,17},{2,34}... | collective-permute-start | bytes 491528 | tf_op jit(solution)/shard_map/ppermute | solution.py:470
  116.7 1.2 collective-permute-start.25
  118.0 2.2 %collective-permute-done.26.refs_3_ = bf16[128,640]{1,0:T(8,128)(2,1)S(1)} collective-permute-done((bf16[128,640]{1,0:T(8,128)(2,1)S(1)}, bf16[128,640]{1,0:T(8,128)(2,1)S(1)}, u32[]{:S(2)}, u32[]{:S(2)}) %collective-permute-start.26) | collective-permute-done | bytes 163872 | tf_op jit(solution)/shard_map/ppermute | solution.py:470
  120.8 3.4 %collective-permute-done.25.refs_2_ = bf16[128,640]{1,0:T(8,128)(2,1)S(1)} collective-permute-done((bf16[128,640]{1,0:T(8,128)(2,1)S(1)}, bf16[128,640]{1,0:T(8,128)(2,1)S(1)}, u32[]{:S(2)}, u32[]{:S(2)}) %collective-permute-start.25) | collective-permute-done | bytes 163872 | tf_op jit(solution)/shard_map/ppermute | solution.py:468
  124.2 1.4 shard_map.89
  125.6 30.8 %all_to_all.16.parts = bf16[8,128,512]{2,1,0:T(8,128)(2,1)S(1)} all-to-all(bf16[8,128,512]{2,1,0:T(8,128)(2,1)S(1)} %shard_map.89), channel_id=1, replica_groups=mesh['seq_0'=4,'seq_1'=4,'seq_2'=2,'head'=8] {'head'}, dimensions={0} | all-to-all | bytes 2097152 | tf_op jit(solution)/shard_map/all_to_all | solution.py:479
  156.8 20.6 %all_to_all.17 = bf16[32,16,512]{2,1,0:T(8,128)(2,1)S(1)} all-to-all(bf16[32,16,512]{2,1,0:T(8,128)(2,1)S(1)} %bitcast.15), channel_id=1, replica_groups=mesh['seq_0'=4,'seq_1'=4,'seq_2'=2,'head'=8] {'seq_0','seq_1','seq_2'}, dimensions={0} | all-to-all | bytes 1048576 | tf_op jit(solution)/shard_map/all_to_all | solution.py:483
  177.4 1.1 shard_map.91
  (85 shorter events, 17.9 us)
Async XLA Ops:
  25.2 12.3 %copy-start.2 = (bf16[1536,128]{1,0:T(8,128)(2,1)S(1)}, bf16[1536,128]{1,0:T(8,128)(2,1)}, u32[]{:S(2)}) copy-start(bf16[1536,128]{1,0:T(8,128)(2,1)} %refs_0_) | copy-start | bytes 1179652
  25.2 49.1 %copy-start.13 = (f32[4096]{0:T(1024)S(1)}, f32[4096]{0:T(1024)}, u32[]{:S(2)}) copy-start(f32[4096]{0:T(1024)} %param.9) | copy-start | bytes 49156
  27.2 9.6 %collective-permute-start = (bf16[128,512]{1,0:T(8,128)(2,1)S(1)}, bf16[128,512]{1,0:T(8,128)(2,1)S(1)}, u32[]{:S(2)}, u32[]{:S(2)}) collective-permute-start(bf16[128,512]{1,0:T(8,128)(2,1)S(1)} %get-tuple-element.29.refs_0_), channel_id=1, source_target_pairs={{0,1},{1,2},{2,3},{3,4},{4,5},{5,6},{6,7},{7,0},{8,9},{9,10},{10,1... | collective-permute-start | bytes 393224 | tf_op jit(solution)/shard_map/ppermute | solution.py:414
  28.8 8.0 %collective-permute-start.1 = (bf16[128,512]{1,0:T(8,128)(2,1)S(1)}, bf16[128,512]{1,0:T(8,128)(2,1)S(1)}, u32[]{:S(2)}, u32[]{:S(2)}) collective-permute-start(bf16[128,512]{1,0:T(8,128)(2,1)S(1)} %get-tuple-element.29.refs_0_), channel_id=1, source_target_pairs={{0,7},{1,0},{2,1},{3,2},{4,3},{5,4},{6,5},{7,6},{8,15},{9,8},{10,9... | collective-permute-start | bytes 393224 | tf_op jit(solution)/shard_map/ppermute | solution.py:418
  36.8 5.9 %collective-permute-start.2 = (bf16[128,512]{1,0:T(8,128)(2,1)S(1)}, bf16[128,512]{1,0:T(8,128)(2,1)S(1)}, u32[]{:S(2)}, u32[]{:S(2)}) collective-permute-start(bf16[128,512]{1,0:T(8,128)(2,1)S(1)} %collective-permute-done.refs_1_), channel_id=1, source_target_pairs={{0,1},{1,2},{2,3},{3,4},{4,5},{5,6},{6,7},{7,0},{8,9},{9,10},{10,1... | collective-permute-start | bytes 393224 | tf_op jit(solution)/shard_map/ppermute | solution.py:414
  37.1 11.9 %collective-permute-start.18 = (bf16[128,1536]{1,0:T(8,128)(2,1)S(1)}, bf16[128,1536]{1,0:T(8,128)(2,1)S(1)}, u32[]{:S(2)}, u32[]{:S(2)}) collective-permute-start(bf16[128,1536]{1,0:T(8,128)(2,1)S(1)} %shard_map.85.refs_8_), channel_id=1, source_target_pairs={{0,192},{64,0},{128,64},{192,128},{1,193},{65,1},{129,65},{193,129... | collective-permute-start | bytes 1179656 | tf_op jit(solution)/shard_map/ppermute | solution.py:397
  37.5 13.6 %collective-permute-start.10 = (bf16[1536,128]{1,0:T(8,128)(2,1)S(1)}, bf16[1536,128]{1,0:T(8,128)(2,1)S(1)}, u32[]{:S(2)}, u32[]{:S(2)}) collective-permute-start(bf16[1536,128]{1,0:T(8,128)(2,1)S(1)} %copy-done.2), channel_id=1, source_target_pairs={{0,64},{64,128},{128,192},{192,0},{1,65},{65,129},{129,193},{193,1... | collective-permute-start | bytes 1179656 | tf_op jit(solution)/shard_map/ppermute | solution.py:394
  38.6 18.2 %collective-permute-start.17 = (bf16[128,1536]{1,0:T(8,128)(2,1)S(1)}, bf16[128,1536]{1,0:T(8,128)(2,1)S(1)}, u32[]{:S(2)}, u32[]{:S(2)}) collective-permute-start(bf16[128,1536]{1,0:T(8,128)(2,1)S(1)} %shard_map.85.refs_8_), channel_id=1, source_target_pairs={{0,64},{64,128},{128,192},{192,0},{1,65},{65,129},{129,193},{193,1... | collective-permute-start | bytes 1179656 | tf_op jit(solution)/shard_map/ppermute | solution.py:394
  38.6 20.0 %collective-permute-start.11 = (bf16[1536,128]{1,0:T(8,128)(2,1)S(1)}, bf16[1536,128]{1,0:T(8,128)(2,1)S(1)}, u32[]{:S(2)}, u32[]{:S(2)}) collective-permute-start(bf16[1536,128]{1,0:T(8,128)(2,1)S(1)} %copy-done.2), channel_id=1, source_target_pairs={{0,192},{64,0},{128,64},{192,128},{1,193},{65,1},{129,65},{193,129... | collective-permute-start | bytes 1179656 | tf_op jit(solution)/shard_map/ppermute | solution.py:397
  42.7 16.2 %copy-start.17 = (bf16[128,512]{1,0:T(8,128)(2,1)}, bf16[128,512]{1,0:T(8,128)(2,1)S(1)}, u32[]{:S(2)}) copy-start(bf16[128,512]{1,0:T(8,128)(2,1)S(1)} %collective-permute-done.2.refs_3_) | copy-start | bytes 393220
  42.7 4.1 %collective-permute-start.3 = (bf16[128,512]{1,0:T(8,128)(2,1)S(1)}, bf16[128,512]{1,0:T(8,128)(2,1)S(1)}, u32[]{:S(2)}, u32[]{:S(2)}) collective-permute-start(bf16[128,512]{1,0:T(8,128)(2,1)S(1)} %collective-permute-done.1.refs_2_), channel_id=1, source_target_pairs={{0,7},{1,0},{2,1},{3,2},{4,3},{5,4},{6,5},{7,6},{8,15},{9,8},{10,9... | collective-permute-start | bytes 393224 | tf_op jit(solution)/shard_map/ppermute | solution.py:418
  46.8 15.1 %collective-permute-start.20 = (bf16[128,1536]{1,0:T(8,128)(2,1)S(1)}, bf16[128,1536]{1,0:T(8,128)(2,1)S(1)}, u32[]{:S(2)}, u32[]{:S(2)}) collective-permute-start(bf16[128,1536]{1,0:T(8,128)(2,1)S(1)} %shard_map.85.refs_8_), channel_id=1, source_target_pairs={{0,8},{8,0},{1,9},{9,1},{2,10},{10,2},{3,11},{11,3},{4,12},{12,4},... | collective-permute-start | bytes 1179656 | tf_op jit(solution)/shard_map/ppermute | solution.py:427
  49.0 9.7 %collective-permute-start.4 = (bf16[128,512]{1,0:T(8,128)(2,1)S(1)}, bf16[128,512]{1,0:T(8,128)(2,1)S(1)}, u32[]{:S(2)}, u32[]{:S(2)}) collective-permute-start(bf16[128,512]{1,0:T(8,128)(2,1)S(1)} %collective-permute-done.2.refs_3_), channel_id=1, source_target_pairs={{0,1},{1,2},{2,3},{3,4},{4,5},{5,6},{6,7},{7,0},{8,9},{9,10},{10,1... | collective-permute-start | bytes 393224 | tf_op jit(solution)/shard_map/ppermute | solution.py:414
  51.1 7.9 %collective-permute-start.5 = (bf16[128,512]{1,0:T(8,128)(2,1)S(1)}, bf16[128,512]{1,0:T(8,128)(2,1)S(1)}, u32[]{:S(2)}, u32[]{:S(2)}) collective-permute-start(bf16[128,512]{1,0:T(8,128)(2,1)S(1)} %collective-permute-done.3.refs_4_), channel_id=1, source_target_pairs={{0,7},{1,0},{2,1},{3,2},{4,3},{5,4},{6,5},{7,6},{8,15},{9,8},{10,9... | collective-permute-start | bytes 393224 | tf_op jit(solution)/shard_map/ppermute | solution.py:418
  56.9 7.7 %collective-permute-start.13 = (bf16[1536,128]{1,0:T(8,128)(2,1)S(1)}, bf16[1536,128]{1,0:T(8,128)(2,1)S(1)}, u32[]{:S(2)}, u32[]{:S(2)}) collective-permute-start(bf16[1536,128]{1,0:T(8,128)(2,1)S(1)} %copy-done.2), channel_id=1, source_target_pairs={{0,8},{8,0},{1,9},{9,1},{2,10},{10,2},{3,11},{11,3},{4,12},{12,4},... | collective-permute-start | bytes 1179656 | tf_op jit(solution)/shard_map/ppermute | solution.py:426
  58.7 10.8 %collective-permute-start.19 = (bf16[128,1536]{1,0:T(8,128)(2,1)S(1)}, bf16[128,1536]{1,0:T(8,128)(2,1)S(1)}, u32[]{:S(2)}, u32[]{:S(2)}) collective-permute-start(bf16[128,1536]{1,0:T(8,128)(2,1)S(1)} %collective-permute-done.18.refs_10_), channel_id=1, source_target_pairs={{0,192},{64,0},{128,64},{192,128},{1,193},{65,1},{129,65},{193,129... | collective-permute-start | bytes 1179656 | tf_op jit(solution)/shard_map/ppermute | solution.py:424
  58.7 14.1 %collective-permute-start.22 = (bf16[128,1536]{1,0:T(8,128)(2,1)S(1)}, bf16[128,1536]{1,0:T(8,128)(2,1)}, u32[]{:S(2)}, u32[]{:S(2)}) collective-permute-start(bf16[128,1536]{1,0:T(8,128)(2,1)S(1)} %collective-permute-done.18.refs_10_), channel_id=1, source_target_pairs={{0,8},{8,0},{1,9},{9,1},{2,10},{10,2},{3,11},{11,3},{4,12},{12,4},... | collective-permute-start | bytes 1179656 | tf_op jit(solution)/shard_map/ppermute | solution.py:427
  60.0 11.7 %collective-permute-start.12 = (bf16[1536,128]{1,0:T(8,128)(2,1)S(1)}, bf16[1536,128]{1,0:T(8,128)(2,1)}, u32[]{:S(2)}, u32[]{:S(2)}) collective-permute-start(bf16[1536,128]{1,0:T(8,128)(2,1)S(1)} %collective-permute-done.10.refs_1_), channel_id=1, source_target_pairs={{0,64},{64,128},{128,192},{192,0},{1,65},{65,129},{129,193},{193,1... | collective-permute-start | bytes 1179656 | tf_op jit(solution)/shard_map/ppermute | solution.py:423
  62.0 10.9 %collective-permute-start.6 = (bf16[128,512]{1,0:T(8,128)(2,1)}, bf16[128,512]{1,0:T(8,128)(2,1)S(1)}, u32[]{:S(2)}, u32[]{:S(2)}) collective-permute-start(bf16[128,512]{1,0:T(8,128)(2,1)} %copy-done.19), channel_id=1, source_target_pairs={{0,1},{1,2},{2,3},{3,4},{4,5},{5,6},{6,7},{7,0},{8,9},{9,10},{10,1... | collective-permute-start | bytes 393224 | tf_op jit(solution)/shard_map/ppermute | solution.py:414
  64.5 15.2 %collective-permute-start.14 = (bf16[1536,128]{1,0:T(8,128)(2,1)S(1)}, bf16[1536,128]{1,0:T(8,128)(2,1)S(1)}, u32[]{:S(2)}, u32[]{:S(2)}) collective-permute-start(bf16[1536,128]{1,0:T(8,128)(2,1)S(1)} %collective-permute-done.10.refs_1_), channel_id=1, source_target_pairs={{0,8},{8,0},{1,9},{9,1},{2,10},{10,2},{3,11},{11,3},{4,12},{12,4},... | collective-permute-start | bytes 1179656 | tf_op jit(solution)/shard_map/ppermute | solution.py:426
  69.4 11.8 %collective-permute-start.21 = (bf16[128,1536]{1,0:T(8,128)(2,1)S(1)}, bf16[128,1536]{1,0:T(8,128)(2,1)S(1)}, u32[]{:S(2)}, u32[]{:S(2)}) collective-permute-start(bf16[128,1536]{1,0:T(8,128)(2,1)S(1)} %collective-permute-done.17.refs_9_), channel_id=1, source_target_pairs={{0,8},{8,0},{1,9},{9,1},{2,10},{10,2},{3,11},{11,3},{4,12},{12,4},... | collective-permute-start | bytes 1179656 | tf_op jit(solution)/shard_map/ppermute | solution.py:427
  71.7 12.3 %collective-permute-start.15 = (bf16[1536,128]{1,0:T(8,128)(2,1)S(1)}, bf16[1536,128]{1,0:T(8,128)(2,1)}, u32[]{:S(2)}, u32[]{:S(2)}) collective-permute-start(bf16[1536,128]{1,0:T(8,128)(2,1)S(1)} %collective-permute-done.11.refs_2_), channel_id=1, source_target_pairs={{0,8},{8,0},{1,9},{9,1},{2,10},{10,2},{3,11},{11,3},{4,12},{12,4},... | collective-permute-start | bytes 1179656 | tf_op jit(solution)/shard_map/ppermute | solution.py:426
  72.8 11.3 %collective-permute-start.23 = (bf16[128,1536]{1,0:T(8,128)(2,1)S(1)}, bf16[128,1536]{1,0:T(8,128)(2,1)}, u32[]{:S(2)}, u32[]{:S(2)}) collective-permute-start(bf16[128,1536]{1,0:T(8,128)(2,1)S(1)} %collective-permute-done.19.refs_11_), channel_id=1, source_target_pairs={{0,8},{8,0},{1,9},{9,1},{2,10},{10,2},{3,11},{11,3},{4,12},{12,4},... | collective-permute-start | bytes 1179656 | tf_op jit(solution)/shard_map/ppermute | solution.py:429
  72.8 11.3 %collective-permute-start.16 = (bf16[1536,128]{1,0:T(8,128)(2,1)}, bf16[1536,128]{1,0:T(8,128)(2,1)}, u32[]{:S(2)}, u32[]{:S(2)}) collective-permute-start(bf16[1536,128]{1,0:T(8,128)(2,1)} %collective-permute-done.12.refs_3_), channel_id=1, source_target_pairs={{0,8},{8,0},{1,9},{9,1},{2,10},{10,2},{3,11},{11,3},{4,12},{12,4},... | collective-permute-start | bytes 1179656 | tf_op jit(solution)/shard_map/ppermute | solution.py:428
  80.4 9.3 %collective-permute-start.8 = (bf16[128,640]{1,0:T(8,128)(2,1)}, bf16[128,640]{1,0:T(8,128)(2,1)}, u32[]{:S(2)}, u32[]{:S(2)}) collective-permute-start(bf16[128,640]{1,0:T(8,128)(2,1)} %shard_map.84.first_q), channel_id=1, source_target_pairs={{0,16},{16,32},{32,48},{48,0},{1,17},{17,33},{33,49},{49,1},{2,18}... | collective-permute-start | bytes 491528 | tf_op jit(solution)/shard_map/ppermute | solution.py:462
  82.0 7.7 %collective-permute-start.9 = (bf16[128,640]{1,0:T(8,128)(2,1)}, bf16[128,640]{1,0:T(8,128)(2,1)}, u32[]{:S(2)}, u32[]{:S(2)}) collective-permute-start(bf16[128,640]{1,0:T(8,128)(2,1)} %shard_map.84.first_q), channel_id=1, source_target_pairs={{0,48},{16,0},{32,16},{48,32},{1,49},{17,1},{33,17},{49,33},{2,50}... | collective-permute-start | bytes 491528 | tf_op jit(solution)/shard_map/ppermute | solution.py:462
  84.0 17.6 %collective-permute-start.7 = (bf16[128,640]{1,0:T(8,128)(2,1)}, bf16[128,640]{1,0:T(8,128)(2,1)S(1)}, u32[]{:S(2)}, u32[]{:S(2)}) collective-permute-start(bf16[128,640]{1,0:T(8,128)(2,1)} %shard_map.84.first_q), channel_id=1, source_target_pairs={{0,32},{16,48},{32,0},{48,16},{1,33},{17,49},{33,1},{49,17},{2,34}... | collective-permute-start | bytes 491528 | tf_op jit(solution)/shard_map/ppermute | solution.py:463
  101.6 22.6 %copy-start = (bf16[512,4096]{1,0:T(8,128)(2,1)S(1)}, bf16[512,4096]{1,0:T(8,128)(2,1)}, u32[]{:S(2)}) copy-start(bf16[512,4096]{1,0:T(8,128)(2,1)} %weight.3) | copy-start | bytes 12582916
  114.4 5.8 %collective-permute-start.26 = (bf16[128,640]{1,0:T(8,128)(2,1)S(1)}, bf16[128,640]{1,0:T(8,128)(2,1)S(1)}, u32[]{:S(2)}, u32[]{:S(2)}) collective-permute-start(bf16[128,640]{1,0:T(8,128)(2,1)S(1)} %get-tuple-element.46), channel_id=1, source_target_pairs={{0,32},{16,48},{32,0},{48,16},{1,33},{17,49},{33,1},{49,17},{2,34}... | collective-permute-start | bytes 491528 | tf_op jit(solution)/shard_map/ppermute | solution.py:470
  116.5 4.3 %collective-permute-start.24 = (bf16[128,640]{1,0:T(8,128)(2,1)S(1)}, bf16[128,640]{1,0:T(8,128)(2,1)S(1)}, u32[]{:S(2)}, u32[]{:S(2)}) collective-permute-start(bf16[128,640]{1,0:T(8,128)(2,1)S(1)} %get-tuple-element.44), channel_id=1, source_target_pairs={{0,48},{16,0},{32,16},{48,32},{1,49},{17,1},{33,17},{49,33},{2,50}... | collective-permute-start | bytes 491528 | tf_op jit(solution)/shard_map/ppermute | solution.py:467
  116.7 7.5 %collective-permute-start.25 = (bf16[128,640]{1,0:T(8,128)(2,1)S(1)}, bf16[128,640]{1,0:T(8,128)(2,1)S(1)}, u32[]{:S(2)}, u32[]{:S(2)}) collective-permute-start(bf16[128,640]{1,0:T(8,128)(2,1)S(1)} %get-tuple-element.45), channel_id=1, source_target_pairs={{0,16},{16,32},{32,48},{48,0},{1,17},{17,33},{33,49},{49,1},{2,18}... | collective-permute-start | bytes 491528 | tf_op jit(solution)/shard_map/ppermute | solution.py:468
  124.2 32.2 %copy-start.12 = (bf16[512,128]{1,0:T(8,128)(2,1)S(1)}, bf16[512,128]{1,0:T(8,128)(2,1)}, u32[]{:S(2)}) copy-start(bf16[512,128]{1,0:T(8,128)(2,1)} %copy-done.11) | copy-start | bytes 393220
  (17 other events, 58.2 us)

commit v2 on v1

--- a/solution.py
+++ b/solution.py
@@ -140,47 +140,38 @@
     return a, b, x - a - b
 
 
-def collect_kernel(*refs):
-    n = (len(refs) - 3) // 2
+def attend_kernel(n, shard_ids, first_q, second_q, *refs):
+    loads = len(refs) > 2 * n
     keys, values = refs[:n], refs[n : 2 * n]
-    kbuf, vbuf, sem = refs[2 * n :]
-    copies = []
-    for i in range(n):
-        copies.append(pltpu.make_async_copy(keys[i], kbuf.at[i], sem.at[0, i]))
-        copies.append(
-            pltpu.make_async_copy(values[i], vbuf.at[i, pl.ds(0, HEAD)], sem.at[1, i])
-        )
-    for copy in copies:
-        copy.start()
-    vbuf[:, HEAD:, :] = jnp.ones((n, vbuf.shape[1] - HEAD, vbuf.shape[2]), BF)
-    for copy in copies:
-        copy.wait()
-
-
-def collect(all_k, all_v):
-    n = len(all_k)
-    tokens = all_k[0].shape[0]
-    return call(
-        collect_kernel,
-        (
-            jax.ShapeDtypeStruct((n, tokens, HEAD), BF),
-            jax.ShapeDtypeStruct((n, HEAD + 16, tokens), BF),
-        ),
-        [ANY] * (2 * n),
-        *all_k,
-        *all_v,
-        scratch_shapes=[pltpu.SemaphoreType.DMA((2, n))],
-    )
-
-
-def attend_kernel(
-    shard_ids, first_q, second_q, kbuf, vbuf, first_out, second_out,
-    qbuf, place, even, odd, acc, peak, tops, steps,
-):
-    n, tokens = kbuf.shape[0], kbuf.shape[1]
+    if loads:
+        first_out, second_out, kbuf, vbuf, *scratch, sem = refs[2 * n :]
+        for i in range(n):
+            pltpu.make_async_copy(keys[i], kbuf.at[i], sem.at[0, i]).start()
+            pltpu.make_async_copy(values[i], vbuf.at[i, pl.ds(0, HEAD)], sem.at[1, i]).start()
+        vbuf[:, HEAD:, :] = jnp.ones((n, vbuf.shape[1] - HEAD, vbuf.shape[2]), BF)
+    else:
+        kbuf, vbuf, first_out, second_out, *scratch = refs
+    qbuf, place, even, odd, acc, peak, tops, steps = scratch
+    tokens = kbuf.shape[1]
     tiles = ROWS // TILE
     side = TILE * HEADS
     big = 2 * side
+
+    def arrive(done, *codes):
+        if not loads:
+            return done
+        upto = done
+        for code in codes:
+            upto = jnp.maximum(upto, parts(code)[0] + 1)
+
+        def wait(i, _):
+            pltpu.make_async_copy(keys[0], kbuf.at[i], sem.at[0, i]).wait()
+            pltpu.make_async_copy(values[0], vbuf.at[i, pl.ds(0, HEAD)], sem.at[1, i]).wait()
+            return 0
+
+        lax.fori_loop(done, upto, wait, 0)
+        return upto
+
     lane = iota((8, ROWS), 1)
     spots = []
     for c, query in enumerate((first_q, second_q)):
@@ -262,18 +253,21 @@
         if made is not None:
             made_top[...] = best
 
-    def run(first, last, masked):
-        def pair(j, _):
+    def run(done, first, last, masked):
+        def pair(j, done):
             a, b, c = steps[2 * j], steps[2 * j + 1], steps[2 * j + 2]
+            done = arrive(done, b, c)
             advance(b, odd, tops.at[1], a, even, tops.at[0], masked)
             advance(c, even, tops.at[0], b, odd, tops.at[1], masked)
-            return 0
-
+            return done
+
+        done = arrive(done, steps[2 * first])
         advance(steps[2 * first], even, tops.at[0], None, None, None, masked)
-        lax.fori_loop(first, last, pair, 0)
-
-    run(0, clear // 2, False)
-    run(clear // 2, (count + 1) // 2, True)
+        return lax.fori_loop(first, last, pair, done)
+
+    done = run(jnp.int32(0), 0, clear // 2, False)
+    done = run(done, clear // 2, (count + 1) // 2, True)
+    arrive(done, jnp.int32(n * tiles - 1))
 
     for c, out in enumerate((first_out, second_out)):
         lanes = slice(c * side, (c + 1) * side)
@@ -294,19 +288,25 @@
             out[rows, HEADS * HEAD :] = stats.astype(BF)
 
 
-def attend(shard_ids, first_q, second_q, kbuf, vbuf):
-    n, tokens = kbuf.shape[0], kbuf.shape[1]
+def attend(shard_ids, first_q, second_q, all_k, all_v):
+    loads = isinstance(all_k, list)
+    n = len(all_k) if loads else all_k.shape[0]
+    tokens = all_k[0].shape[0]
     big = 2 * TILE * HEADS
     tiles = ROWS // TILE
+    held = (
+        jax.ShapeDtypeStruct((n, tokens, HEAD), BF),
+        jax.ShapeDtypeStruct((n, HEAD + 16, tokens), BF),
+    )
+    sources = [*all_k, *all_v] if loads else [all_k, all_v]
     return call(
-        attend_kernel,
-        (jax.ShapeDtypeStruct((ROWS, HEADS * HEAD + META), BF),) * 2,
-        [SM, VM, VM, VM, VM],
+        functools.partial(attend_kernel, n),
+        (jax.ShapeDtypeStruct((ROWS, HEADS * HEAD + META), BF),) * 2 + (held if loads else ()),
+        [SM, VM, VM] + ([ANY] * (2 * n) if loads else [VM, VM]),
         shard_ids,
         first_q,
         second_q,
-        kbuf,
-        vbuf,
+        *sources,
         flops=10**10,
         moved=7 * 10**6,
         scratch_shapes=[
@@ -318,7 +318,8 @@
             pltpu.VMEM((tiles, 8, big), F32),
             pltpu.VMEM((2, 8, big), F32),
             pltpu.SMEM((n * tiles + 8,), jnp.int32),
-        ],
+        ]
+        + ([pltpu.SemaphoreType.DMA((2, n))] if loads else []),
     )
 
 
@@ -439,11 +440,12 @@
     sine = jnp.concatenate([-sine, sine], axis=1)
 
     w_query = pltpu.with_memory_space_constraint(w_query, pltpu.HBM)
-    slices = [pltpu.with_memory_space_constraint(a, pltpu.HBM) for a in slices]
+    slices[:-1] = [pltpu.with_memory_space_constraint(a, pltpu.HBM) for a in slices[:-1]]
+    back = pltpu.with_memory_space_constraint(back, pltpu.HBM)
     query = call(
         functools.partial(project_kernel, tuple(order)),
         jax.ShapeDtypeStruct((ROWS, HEADS * HEAD + META), BF),
-        [SM, VM, VM, VM, VM, HB] + [HB] * nz,
+        [SM, VM, VM, VM, VM, HB] + [HB] * (nz - 1) + [ANY],
         z.reshape(1).astype(jnp.int32),
         meta,
         norm_gain.reshape(1, -1),
@@ -461,8 +463,7 @@
 
     asked = [lax.ppermute(query, SEQ[1], shift(ny, k)) for k in (1, ny - 1)]
     far = lax.ppermute(query, SEQ[1], shift(ny, 2))
-    kbuf, vbuf = collect(all_k, all_v)
-    ra, rb = attend(shard_ids, *asked, kbuf, vbuf)
+    ra, rb, kbuf, vbuf = attend(shard_ids, *asked, all_k, all_v)
     query, far, ra, rb = lax.optimization_barrier((query, far, ra, rb))
     ra = lax.ppermute(ra, SEQ[1], shift(ny, -1))
     rb = lax.ppermute(rb, SEQ[1], shift(ny, 1))

time: 179 us -> 175 us (0.978)
  waiting for transfers between devices: 24.7 us -> 27.6 us
  Pallas kernels: 37.8 us -> 35.6 us
  local copies, waits for them, and re-layouts: 8.68 us -> 6.59 us
  other arithmetic: 2.48 us -> 0.6 us
    all_to_all x1, blocking collectives: 30.8 us -> 27.3 us  [body(): arrived = lax.all_to_all(partial, 'head', 0, 0, tiled=True)]
    ppermute x2, waiting for transfers between devices: 0.01 us -> 3.4 us  [body(): asked = [lax.ppermute(query, SEQ[1], shift(ny, k)) for k in (1, ny - 1)]]
    all_to_all x1, blocking collectives: 20.6 us -> 24 us  [body(): lax.all_to_all(to_send.reshape(shards, GROUP, width), SEQ, 0, 0, tiled=True)]
    ppermute x1, waiting for transfers between devices: 3.36 us -> 0.41 us  [body(): rb = lax.ppermute(rb, SEQ[1], shift(ny, 1))]
    pallas_call x10 -> x9, Pallas kernels: 37.8 us -> 35.6 us  [call(): pl.pallas_call(kernel, out_shape=out, in_specs=specs, out_specs=jax.tree....]
    unnamed x44 -> x36, local copies, waits for them, and re-layouts: 8.6 us -> 6.51 us
  transfers between devices with their start and end apart: 27 -> 27, of which waited for: 9 -> 11; matrix products, arithmetic and copies ran while one was open for 1% -> 0% of each run, Pallas kernels for 11% -> 10%
where the time goes in v2:
time: 175 us
  blocking collectives  72.6 us (41%)
  Pallas kernels  35.6 us (20%)
  starting transfers between devices  31 us (18%)
  waiting for transfers between devices  27.6 us (16%)
  local copies, waits for them, and re-layouts  6.59 us (4%)
    pallas_call x9, Pallas kernels, call(): pl.pallas_call(kernel, out_shape=out, in_specs=specs, out_specs=jax.tree....  35.6 us
    all_to_all x1, blocking collectives, body(): arrived = lax.all_to_all(partial, 'head', 0, 0, tiled=True)  27.3 us
    all_to_all x1, blocking collectives, body(): lax.all_to_all(to_send.reshape(shards, GROUP, width), SEQ, 0, 0, tiled=True)  24 us
    all_to_all x1, blocking collectives, body(): got = lax.all_to_all(send.reshape(shards, GROUP, -1), SEQ, 0, 0, tiled=True)  21.3 us
    unnamed x36, local copies, waits for them, and re-layouts  6.51 us
    ppermute x3, starting transfers between devices, body(): down = lax.ppermute(down, 'head', shift(nz, -1))  6.2 us
    ppermute x4, starting transfers between devices, body(): up = lax.ppermute(up, 'head', shift(nz, 1))  5.81 us
    ppermute x4, waiting for transfers between devices, body(): up = lax.ppermute(up, 'head', shift(nz, 1))  5.35 us
  transfers between devices with their start and end apart: 27, of which 11 were waited for; matrix products, arithmetic and copies ran while one was open for 0% of the time, Pallas kernels for 10%

profile of v2, /device:TPU:1, one launch (start us, length us, event | category | flops | bytes accessed | tf_op | source)
XLA Modules:
  0.0 174.9 jit_solution(9038261810338467149)
XLA Ops:
  0.7 1.4 copy-done.1
  2.7 1.2 shard_map.82
  3.9 21.3 %all_to_all.15 = bf16[32,16,640]{2,1,0:T(8,128)(2,1)S(1)} all-to-all(bf16[32,16,640]{2,1,0:T(8,128)(2,1)S(1)} %bitcast.14), channel_id=1, replica_groups=mesh['seq_0'=4,'seq_1'=4,'seq_2'=2,'head'=8] {'seq_0','seq_1','seq_2'}, dimensions={0} | all-to-all | bytes 1310720 | tf_op jit(solution)/shard_map/all_to_all | solution.py:392
  26.0 1.7 collective-permute-start
  27.7 4.0 %collective-permute-start.1 = (bf16[128,512]{1,0:T(8,128)(2,1)S(1)}, bf16[128,512]{1,0:T(8,128)(2,1)S(1)}, u32[]{:S(2)}, u32[]{:S(2)}) collective-permute-start(bf16[128,512]{1,0:T(8,128)(2,1)S(1)} %get-tuple-element.29.refs_0_), channel_id=1, source_target_pairs={{0,7},{1,0},{2,1},{3,2},{4,3},{5,4},{6,5},{7,6},{8,15},{9,8},{10,9... | collective-permute-start | bytes 393224 | tf_op jit(solution)/shard_map/ppermute | solution.py:419
  31.7 3.9 %collective-permute-done.refs_1_ = bf16[128,512]{1,0:T(8,128)(2,1)S(1)} collective-permute-done((bf16[128,512]{1,0:T(8,128)(2,1)S(1)}, bf16[128,512]{1,0:T(8,128)(2,1)S(1)}, u32[]{:S(2)}, u32[]{:S(2)}) %collective-permute-start) | collective-permute-done | bytes 131104 | tf_op jit(solution)/shard_map/ppermute | solution.py:415
  36.3 1.1 collective-permute-start.10
  37.5 2.7 %collective-permute-start.11 = (bf16[1536,128]{1,0:T(8,128)(2,1)S(1)}, bf16[1536,128]{1,0:T(8,128)(2,1)S(1)}, u32[]{:S(2)}, u32[]{:S(2)}) collective-permute-start(bf16[1536,128]{1,0:T(8,128)(2,1)S(1)} %copy-done.7), channel_id=1, source_target_pairs={{0,192},{64,0},{128,64},{192,128},{1,193},{65,1},{129,65},{193,129... | collective-permute-start | bytes 1179656 | tf_op jit(solution)/shard_map/ppermute | solution.py:398
  40.1 1.4 collective-permute-done.2.refs_3_
  41.5 1.2 collective-permute-start.3
  42.8 2.9 %collective-permute-done.3.refs_4_ = bf16[128,512]{1,0:T(8,128)(2,1)S(1)} collective-permute-done((bf16[128,512]{1,0:T(8,128)(2,1)S(1)}, bf16[128,512]{1,0:T(8,128)(2,1)S(1)}, u32[]{:S(2)}, u32[]{:S(2)}) %collective-permute-start.3) | collective-permute-done | bytes 131104 | tf_op jit(solution)/shard_map/ppermute | solution.py:419
  45.7 2.1 %collective-permute-start.20 = (bf16[128,1536]{1,0:T(8,128)(2,1)S(1)}, bf16[128,1536]{1,0:T(8,128)(2,1)S(1)}, u32[]{:S(2)}, u32[]{:S(2)}) collective-permute-start(bf16[128,1536]{1,0:T(8,128)(2,1)S(1)} %shard_map.85.refs_8_), channel_id=1, source_target_pairs={{0,8},{8,0},{1,9},{9,1},{2,10},{10,2},{3,11},{11,3},{4,12},{12,4},... | collective-permute-start | bytes 1179656 | tf_op jit(solution)/shard_map/ppermute | solution.py:428
  47.8 2.1 %collective-permute-start.4 = (bf16[128,512]{1,0:T(8,128)(2,1)S(1)}, bf16[128,512]{1,0:T(8,128)(2,1)S(1)}, u32[]{:S(2)}, u32[]{:S(2)}) collective-permute-start(bf16[128,512]{1,0:T(8,128)(2,1)S(1)} %collective-permute-done.2.refs_3_), channel_id=1, source_target_pairs={{0,1},{1,2},{2,3},{3,4},{4,5},{5,6},{6,7},{7,0},{8,9},{9,10},{10,1... | collective-permute-start | bytes 393224 | tf_op jit(solution)/shard_map/ppermute | solution.py:415
  50.9 4.8 %collective-permute-done.17.refs_9_ = bf16[128,1536]{1,0:T(8,128)(2,1)S(1)} collective-permute-done((bf16[128,1536]{1,0:T(8,128)(2,1)S(1)}, bf16[128,1536]{1,0:T(8,128)(2,1)S(1)}, u32[]{:S(2)}, u32[]{:S(2)}) %collective-permute-start.17) | collective-permute-done | bytes 393248 | tf_op jit(solution)/shard_map/ppermute | solution.py:395
  55.7 1.8 %collective-permute-start.13 = (bf16[1536,128]{1,0:T(8,128)(2,1)S(1)}, bf16[1536,128]{1,0:T(8,128)(2,1)S(1)}, u32[]{:S(2)}, u32[]{:S(2)}) collective-permute-start(bf16[1536,128]{1,0:T(8,128)(2,1)S(1)} %copy-done.7), channel_id=1, source_target_pairs={{0,8},{8,0},{1,9},{9,1},{2,10},{10,2},{3,11},{11,3},{4,12},{12,4},... | collective-permute-start | bytes 1179656 | tf_op jit(solution)/shard_map/ppermute | solution.py:427
  58.8 1.5 collective-permute-start.12
  60.3 1.9 %collective-permute-start.6 = (bf16[128,512]{1,0:T(8,128)(2,1)}, bf16[128,512]{1,0:T(8,128)(2,1)S(1)}, u32[]{:S(2)}, u32[]{:S(2)}) collective-permute-start(bf16[128,512]{1,0:T(8,128)(2,1)} %copy-done.16), channel_id=1, source_target_pairs={{0,1},{1,2},{2,3},{3,4},{4,5},{5,6},{6,7},{7,0},{8,9},{9,10},{10,1... | collective-permute-start | bytes 393224 | tf_op jit(solution)/shard_map/ppermute | solution.py:415
  63.2 5.0 %collective-permute-done.19.refs_11_ = bf16[128,1536]{1,0:T(8,128)(2,1)} collective-permute-done((bf16[128,1536]{1,0:T(8,128)(2,1)S(1)}, bf16[128,1536]{1,0:T(8,128)(2,1)}, u32[]{:S(2)}, u32[]{:S(2)}) %collective-permute-start.19) | collective-permute-done | bytes 393248 | tf_op jit(solution)/shard_map/ppermute | solution.py:425
  69.3 1.2 collective-permute-done.12.refs_3_
  70.5 1.1 collective-permute-start.15
  72.6 3.2 %shard_map.84.first_q = bf16[128,640]{1,0:T(8,128)(2,1)S(1)} custom-call(s32[1]{0:T(128)} %bitcast.10.z, bf16[128,128]{1,0:T(8,128)(2,1)S(1)} %get-tuple-element.28.meta, f32[1,4096]{1,0:T(1,128)S(1)} %bitcast.18, f32[128,128]{1,0:T(8,128)S(1)} %get-tuple-element.50.cosine, f32[128,128]{1,0:T(8,128)S(1)} %get-tuple-element.51.sine, ...), custom_call_target="tpu_custom_call" | custom-call | tf_op jit(solution)/shard_map/pallas_call | solution.py:39
  78.1 1.9 %collective-permute-start.9 = (bf16[128,640]{1,0:T(8,128)(2,1)S(1)}, bf16[128,640]{1,0:T(8,128)(2,1)}, u32[]{:S(2)}, u32[]{:S(2)}) collective-permute-start(bf16[128,640]{1,0:T(8,128)(2,1)S(1)} %shard_map.84.first_q), channel_id=1, source_target_pairs={{0,48},{16,0},{32,16},{48,32},{1,49},{17,1},{33,17},{49,33},{2,50}... | collective-permute-start | bytes 491528 | tf_op jit(solution)/shard_map/ppermute | solution.py:464
  80.2 3.2 %collective-permute-done.8.first_q = bf16[128,640]{1,0:T(8,128)(2,1)S(1)} collective-permute-done((bf16[128,640]{1,0:T(8,128)(2,1)S(1)}, bf16[128,640]{1,0:T(8,128)(2,1)S(1)}, u32[]{:S(2)}, u32[]{:S(2)}) %collective-permute-start.8) | collective-permute-done | bytes 163872 | tf_op jit(solution)/shard_map/ppermute | solution.py:464
  85.6 14.3 %shard_map.86 = (bf16[128,640]{1,0:T(8,128)(2,1)S(1)}, bf16[128,640]{1,0:T(8,128)(2,1)S(1)}, bf16[8,1536,128]{2,1,0:T(8,128)(2,1)S(1)}, bf16[8,144,1536]{2,1,0:T(8,128)(2,1)S(1)}) custom-call(s32[8]{0:T(128)S(1)} %stack.35.shard_ids, bf16[128,640]{1,0:T(8,128)(2,1)S(1)} %collective-permute-done.8.first_q, bf16[128,640]{1,0:T(8,128)(2,1)} %collective-permute-done.9.second_q, ...), custom_call_target="tpu_custom_call" | custom-call | flops 10000000000 | bytes 7000000 | tf_op jit(solution)/shard_map/pallas_call | solution.py:39
  99.9 12.2 %shard_map.87 = (bf16[128,640]{1,0:T(8,128)(2,1)S(1)}, bf16[128,640]{1,0:T(8,128)(2,1)S(1)}) custom-call(s32[8]{0:T(128)S(1)} %stack.35.shard_ids, bf16[128,640]{1,0:T(8,128)(2,1)S(1)} %shard_map.84.first_q, bf16[128,640]{1,0:T(8,128)(2,1)S(1)} %collective-permute-done.7.second_q, bf16[8,1536,128]{2,1,0:T(8,128)(2,1)S(1)} %get-tuple-element.41.refs_0_, ...), custom_call_target="tpu_custom_call" | custom-call | flops 10000000000 | bytes 7000000 | tf_op jit(solution)/shard_map/pallas_call | solution.py:39
  114.8 3.2 %collective-permute-done.26.refs_3_ = bf16[128,640]{1,0:T(8,128)(2,1)S(1)} collective-permute-done((bf16[128,640]{1,0:T(8,128)(2,1)S(1)}, bf16[128,640]{1,0:T(8,128)(2,1)S(1)}, u32[]{:S(2)}, u32[]{:S(2)}) %collective-permute-start.26) | collective-permute-done | bytes 163872 | tf_op jit(solution)/shard_map/ppermute | solution.py:471
  117.9 1.3 collective-permute-done.24.refs_1_
  119.7 1.4 shard_map.88
  121.1 27.3 %all_to_all.16.parts = bf16[8,128,512]{2,1,0:T(8,128)(2,1)S(1)} all-to-all(bf16[8,128,512]{2,1,0:T(8,128)(2,1)S(1)} %shard_map.88), channel_id=1, replica_groups=mesh['seq_0'=4,'seq_1'=4,'seq_2'=2,'head'=8] {'head'}, dimensions={0} | all-to-all | bytes 2097152 | tf_op jit(solution)/shard_map/all_to_all | solution.py:480
  148.5 1.3 shard_map.89
  149.8 24.0 %all_to_all.17 = bf16[32,16,512]{2,1,0:T(8,128)(2,1)S(1)} all-to-all(bf16[32,16,512]{2,1,0:T(8,128)(2,1)S(1)} %bitcast.15), channel_id=1, replica_groups=mesh['seq_0'=4,'seq_1'=4,'seq_2'=2,'head'=8] {'seq_0','seq_1','seq_2'}, dimensions={0} | all-to-all | bytes 1048576 | tf_op jit(solution)/shard_map/all_to_all | solution.py:484
  173.7 1.1 shard_map.90
  (76 shorter events, 15.1 us)
Async XLA Ops:
  25.2 47.3 %copy-start.5 = (f32[4096]{0:T(1024)S(1)}, f32[4096]{0:T(1024)}, u32[]{:S(2)}) copy-start(f32[4096]{0:T(1024)} %param.9) | copy-start | bytes 49156
  25.9 29.7 %copy-start.4 = (bf16[512,128]{1,0:T(8,128)(2,1)}, bf16[512,128]{1,0:T(8,128)(2,1)S(1)}, u32[]{:S(2)}) copy-start(bf16[512,128]{1,0:T(8,128)(2,1)S(1)} %get-tuple-element.27.back) | copy-start | bytes 393220
  26.0 46.6 %copy-start.3 = (bf16[128,512]{1,0:T(8,128)(2,1)}, bf16[128,512]{1,0:T(8,128)(2,1)S(1)}, u32[]{:S(2)}) copy-start(bf16[128,512]{1,0:T(8,128)(2,1)S(1)} %get-tuple-element.29.refs_0_) | copy-start | bytes 393220
  26.0 9.7 %collective-permute-start = (bf16[128,512]{1,0:T(8,128)(2,1)S(1)}, bf16[128,512]{1,0:T(8,128)(2,1)S(1)}, u32[]{:S(2)}, u32[]{:S(2)}) collective-permute-start(bf16[128,512]{1,0:T(8,128)(2,1)S(1)} %get-tuple-element.29.refs_0_), channel_id=1, source_target_pairs={{0,1},{1,2},{2,3},{3,4},{4,5},{5,6},{6,7},{7,0},{8,9},{9,10},{10,1... | collective-permute-start | bytes 393224 | tf_op jit(solution)/shard_map/ppermute | solution.py:415
  27.7 8.0 %collective-permute-start.1 = (bf16[128,512]{1,0:T(8,128)(2,1)S(1)}, bf16[128,512]{1,0:T(8,128)(2,1)S(1)}, u32[]{:S(2)}, u32[]{:S(2)}) collective-permute-start(bf16[128,512]{1,0:T(8,128)(2,1)S(1)} %get-tuple-element.29.refs_0_), channel_id=1, source_target_pairs={{0,7},{1,0},{2,1},{3,2},{4,3},{5,4},{6,5},{7,6},{8,15},{9,8},{10,9... | collective-permute-start | bytes 393224 | tf_op jit(solution)/shard_map/ppermute | solution.py:419
  35.6 22.2 %copy-start.12 = (bf16[128,512]{1,0:T(8,128)(2,1)}, bf16[128,512]{1,0:T(8,128)(2,1)S(1)}, u32[]{:S(2)}) copy-start(bf16[128,512]{1,0:T(8,128)(2,1)S(1)} %collective-permute-done.refs_1_) | copy-start | bytes 393220
  35.6 26.5 %copy-start.13 = (bf16[128,512]{1,0:T(8,128)(2,1)}, bf16[128,512]{1,0:T(8,128)(2,1)S(1)}, u32[]{:S(2)}) copy-start(bf16[128,512]{1,0:T(8,128)(2,1)S(1)} %collective-permute-done.1.refs_2_) | copy-start | bytes 393220
  35.6 5.9 %collective-permute-start.2 = (bf16[128,512]{1,0:T(8,128)(2,1)S(1)}, bf16[128,512]{1,0:T(8,128)(2,1)S(1)}, u32[]{:S(2)}, u32[]{:S(2)}) collective-permute-start(bf16[128,512]{1,0:T(8,128)(2,1)S(1)} %collective-permute-done.refs_1_), channel_id=1, source_target_pairs={{0,1},{1,2},{2,3},{3,4},{4,5},{5,6},{6,7},{7,0},{8,9},{9,10},{10,1... | collective-permute-start | bytes 393224 | tf_op jit(solution)/shard_map/ppermute | solution.py:415
  35.9 11.9 %collective-permute-start.18 = (bf16[128,1536]{1,0:T(8,128)(2,1)S(1)}, bf16[128,1536]{1,0:T(8,128)(2,1)S(1)}, u32[]{:S(2)}, u32[]{:S(2)}) collective-permute-start(bf16[128,1536]{1,0:T(8,128)(2,1)S(1)} %shard_map.85.refs_8_), channel_id=1, source_target_pairs={{0,192},{64,0},{128,64},{192,128},{1,193},{65,1},{129,65},{193,129... | collective-permute-start | bytes 1179656 | tf_op jit(solution)/shard_map/ppermute | solution.py:398
  36.3 13.6 %collective-permute-start.10 = (bf16[1536,128]{1,0:T(8,128)(2,1)S(1)}, bf16[1536,128]{1,0:T(8,128)(2,1)S(1)}, u32[]{:S(2)}, u32[]{:S(2)}) collective-permute-start(bf16[1536,128]{1,0:T(8,128)(2,1)S(1)} %copy-done.7), channel_id=1, source_target_pairs={{0,64},{64,128},{128,192},{192,0},{1,65},{65,129},{129,193},{193,1... | collective-permute-start | bytes 1179656 | tf_op jit(solution)/shard_map/ppermute | solution.py:395
  37.4 18.2 %collective-permute-start.17 = (bf16[128,1536]{1,0:T(8,128)(2,1)S(1)}, bf16[128,1536]{1,0:T(8,128)(2,1)S(1)}, u32[]{:S(2)}, u32[]{:S(2)}) collective-permute-start(bf16[128,1536]{1,0:T(8,128)(2,1)S(1)} %shard_map.85.refs_8_), channel_id=1, source_target_pairs={{0,64},{64,128},{128,192},{192,0},{1,65},{65,129},{129,193},{193,1... | collective-permute-start | bytes 1179656 | tf_op jit(solution)/shard_map/ppermute | solution.py:395
  37.5 20.0 %collective-permute-start.11 = (bf16[1536,128]{1,0:T(8,128)(2,1)S(1)}, bf16[1536,128]{1,0:T(8,128)(2,1)S(1)}, u32[]{:S(2)}, u32[]{:S(2)}) collective-permute-start(bf16[1536,128]{1,0:T(8,128)(2,1)S(1)} %copy-done.7), channel_id=1, source_target_pairs={{0,192},{64,0},{128,64},{192,128},{1,193},{65,1},{129,65},{193,129... | collective-permute-start | bytes 1179656 | tf_op jit(solution)/shard_map/ppermute | solution.py:398
  41.5 4.1 %collective-permute-start.3 = (bf16[128,512]{1,0:T(8,128)(2,1)S(1)}, bf16[128,512]{1,0:T(8,128)(2,1)S(1)}, u32[]{:S(2)}, u32[]{:S(2)}) collective-permute-start(bf16[128,512]{1,0:T(8,128)(2,1)S(1)} %collective-permute-done.1.refs_2_), channel_id=1, source_target_pairs={{0,7},{1,0},{2,1},{3,2},{4,3},{5,4},{6,5},{7,6},{8,15},{9,8},{10,9... | collective-permute-start | bytes 393224 | tf_op jit(solution)/shard_map/ppermute | solution.py:419
  45.7 14.6 %collective-permute-start.20 = (bf16[128,1536]{1,0:T(8,128)(2,1)S(1)}, bf16[128,1536]{1,0:T(8,128)(2,1)S(1)}, u32[]{:S(2)}, u32[]{:S(2)}) collective-permute-start(bf16[128,1536]{1,0:T(8,128)(2,1)S(1)} %shard_map.85.refs_8_), channel_id=1, source_target_pairs={{0,8},{8,0},{1,9},{9,1},{2,10},{10,2},{3,11},{11,3},{4,12},{12,4},... | collective-permute-start | bytes 1179656 | tf_op jit(solution)/shard_map/ppermute | solution.py:428
  47.8 9.7 %collective-permute-start.4 = (bf16[128,512]{1,0:T(8,128)(2,1)S(1)}, bf16[128,512]{1,0:T(8,128)(2,1)S(1)}, u32[]{:S(2)}, u32[]{:S(2)}) collective-permute-start(bf16[128,512]{1,0:T(8,128)(2,1)S(1)} %collective-permute-done.2.refs_3_), channel_id=1, source_target_pairs={{0,1},{1,2},{2,3},{3,4},{4,5},{5,6},{6,7},{7,0},{8,9},{9,10},{10,1... | collective-permute-start | bytes 393224 | tf_op jit(solution)/shard_map/ppermute | solution.py:415
  50.0 7.9 %collective-permute-start.5 = (bf16[128,512]{1,0:T(8,128)(2,1)S(1)}, bf16[128,512]{1,0:T(8,128)(2,1)S(1)}, u32[]{:S(2)}, u32[]{:S(2)}) collective-permute-start(bf16[128,512]{1,0:T(8,128)(2,1)S(1)} %collective-permute-done.3.refs_4_), channel_id=1, source_target_pairs={{0,7},{1,0},{2,1},{3,2},{4,3},{5,4},{6,5},{7,6},{8,15},{9,8},{10,9... | collective-permute-start | bytes 393224 | tf_op jit(solution)/shard_map/ppermute | solution.py:419
  55.7 6.5 %collective-permute-start.13 = (bf16[1536,128]{1,0:T(8,128)(2,1)S(1)}, bf16[1536,128]{1,0:T(8,128)(2,1)S(1)}, u32[]{:S(2)}, u32[]{:S(2)}) collective-permute-start(bf16[1536,128]{1,0:T(8,128)(2,1)S(1)} %copy-done.7), channel_id=1, source_target_pairs={{0,8},{8,0},{1,9},{9,1},{2,10},{10,2},{3,11},{11,3},{4,12},{12,4},... | collective-permute-start | bytes 1179656 | tf_op jit(solution)/shard_map/ppermute | solution.py:427
  57.5 10.7 %collective-permute-start.19 = (bf16[128,1536]{1,0:T(8,128)(2,1)S(1)}, bf16[128,1536]{1,0:T(8,128)(2,1)}, u32[]{:S(2)}, u32[]{:S(2)}) collective-permute-start(bf16[128,1536]{1,0:T(8,128)(2,1)S(1)} %collective-permute-done.18.refs_10_), channel_id=1, source_target_pairs={{0,192},{64,0},{128,64},{192,128},{1,193},{65,1},{129,65},{193,129... | collective-permute-start | bytes 1179656 | tf_op jit(solution)/shard_map/ppermute | solution.py:425
  57.5 14.1 %collective-permute-start.22 = (bf16[128,1536]{1,0:T(8,128)(2,1)S(1)}, bf16[128,1536]{1,0:T(8,128)(2,1)}, u32[]{:S(2)}, u32[]{:S(2)}) collective-permute-start(bf16[128,1536]{1,0:T(8,128)(2,1)S(1)} %collective-permute-done.18.refs_10_), channel_id=1, source_target_pairs={{0,8},{8,0},{1,9},{9,1},{2,10},{10,2},{3,11},{11,3},{4,12},{12,4},... | collective-permute-start | bytes 1179656 | tf_op jit(solution)/shard_map/ppermute | solution.py:428
  58.8 11.7 %collective-permute-start.12 = (bf16[1536,128]{1,0:T(8,128)(2,1)S(1)}, bf16[1536,128]{1,0:T(8,128)(2,1)}, u32[]{:S(2)}, u32[]{:S(2)}) collective-permute-start(bf16[1536,128]{1,0:T(8,128)(2,1)S(1)} %collective-permute-done.10.refs_1_), channel_id=1, source_target_pairs={{0,64},{64,128},{128,192},{192,0},{1,65},{65,129},{129,193},{193,1... | collective-permute-start | bytes 1179656 | tf_op jit(solution)/shard_map/ppermute | solution.py:424
  60.3 11.4 %collective-permute-start.6 = (bf16[128,512]{1,0:T(8,128)(2,1)}, bf16[128,512]{1,0:T(8,128)(2,1)S(1)}, u32[]{:S(2)}, u32[]{:S(2)}) collective-permute-start(bf16[128,512]{1,0:T(8,128)(2,1)} %copy-done.16), channel_id=1, source_target_pairs={{0,1},{1,2},{2,3},{3,4},{4,5},{5,6},{6,7},{7,0},{8,9},{9,10},{10,1... | collective-permute-start | bytes 393224 | tf_op jit(solution)/shard_map/ppermute | solution.py:415
  62.2 13.6 %collective-permute-start.14 = (bf16[1536,128]{1,0:T(8,128)(2,1)S(1)}, bf16[1536,128]{1,0:T(8,128)(2,1)S(1)}, u32[]{:S(2)}, u32[]{:S(2)}) collective-permute-start(bf16[1536,128]{1,0:T(8,128)(2,1)S(1)} %collective-permute-done.10.refs_1_), channel_id=1, source_target_pairs={{0,8},{8,0},{1,9},{9,1},{2,10},{10,2},{3,11},{11,3},{4,12},{12,4},... | collective-permute-start | bytes 1179656 | tf_op jit(solution)/shard_map/ppermute | solution.py:427
  68.2 9.2 %collective-permute-start.21 = (bf16[128,1536]{1,0:T(8,128)(2,1)S(1)}, bf16[128,1536]{1,0:T(8,128)(2,1)S(1)}, u32[]{:S(2)}, u32[]{:S(2)}) collective-permute-start(bf16[128,1536]{1,0:T(8,128)(2,1)S(1)} %collective-permute-done.17.refs_9_), channel_id=1, source_target_pairs={{0,8},{8,0},{1,9},{9,1},{2,10},{10,2},{3,11},{11,3},{4,12},{12,4},... | collective-permute-start | bytes 1179656 | tf_op jit(solution)/shard_map/ppermute | solution.py:428
  70.5 9.6 %collective-permute-start.15 = (bf16[1536,128]{1,0:T(8,128)(2,1)S(1)}, bf16[1536,128]{1,0:T(8,128)(2,1)}, u32[]{:S(2)}, u32[]{:S(2)}) collective-permute-start(bf16[1536,128]{1,0:T(8,128)(2,1)S(1)} %collective-permute-done.11.refs_2_), channel_id=1, source_target_pairs={{0,8},{8,0},{1,9},{9,1},{2,10},{10,2},{3,11},{11,3},{4,12},{12,4},... | collective-permute-start | bytes 1179656 | tf_op jit(solution)/shard_map/ppermute | solution.py:427
  71.6 8.5 %collective-permute-start.23 = (bf16[128,1536]{1,0:T(8,128)(2,1)}, bf16[128,1536]{1,0:T(8,128)(2,1)}, u32[]{:S(2)}, u32[]{:S(2)}) collective-permute-start(bf16[128,1536]{1,0:T(8,128)(2,1)} %collective-permute-done.19.refs_11_), channel_id=1, source_target_pairs={{0,8},{8,0},{1,9},{9,1},{2,10},{10,2},{3,11},{11,3},{4,12},{12,4},... | collective-permute-start | bytes 1179656 | tf_op jit(solution)/shard_map/ppermute | solution.py:430
  71.6 8.5 %collective-permute-start.16 = (bf16[1536,128]{1,0:T(8,128)(2,1)}, bf16[1536,128]{1,0:T(8,128)(2,1)}, u32[]{:S(2)}, u32[]{:S(2)}) collective-permute-start(bf16[1536,128]{1,0:T(8,128)(2,1)} %collective-permute-done.12.refs_3_), channel_id=1, source_target_pairs={{0,8},{8,0},{1,9},{9,1},{2,10},{10,2},{3,11},{11,3},{4,12},{12,4},... | collective-permute-start | bytes 1179656 | tf_op jit(solution)/shard_map/ppermute | solution.py:429
  76.5 6.9 %collective-permute-start.8 = (bf16[128,640]{1,0:T(8,128)(2,1)S(1)}, bf16[128,640]{1,0:T(8,128)(2,1)S(1)}, u32[]{:S(2)}, u32[]{:S(2)}) collective-permute-start(bf16[128,640]{1,0:T(8,128)(2,1)S(1)} %shard_map.84.first_q), channel_id=1, source_target_pairs={{0,16},{16,32},{32,48},{48,0},{1,17},{17,33},{33,49},{49,1},{2,18}... | collective-permute-start | bytes 491528 | tf_op jit(solution)/shard_map/ppermute | solution.py:464
  78.1 5.5 %collective-permute-start.9 = (bf16[128,640]{1,0:T(8,128)(2,1)S(1)}, bf16[128,640]{1,0:T(8,128)(2,1)}, u32[]{:S(2)}, u32[]{:S(2)}) collective-permute-start(bf16[128,640]{1,0:T(8,128)(2,1)S(1)} %shard_map.84.first_q), channel_id=1, source_target_pairs={{0,48},{16,0},{32,16},{48,32},{1,49},{17,1},{33,17},{49,33},{2,50}... | collective-permute-start | bytes 491528 | tf_op jit(solution)/shard_map/ppermute | solution.py:464
  80.1 19.8 %collective-permute-start.7 = (bf16[128,640]{1,0:T(8,128)(2,1)S(1)}, bf16[128,640]{1,0:T(8,128)(2,1)S(1)}, u32[]{:S(2)}, u32[]{:S(2)}) collective-permute-start(bf16[128,640]{1,0:T(8,128)(2,1)S(1)} %shard_map.84.first_q), channel_id=1, source_target_pairs={{0,32},{16,48},{32,0},{48,16},{1,33},{17,49},{33,1},{49,17},{2,34}... | collective-permute-start | bytes 491528 | tf_op jit(solution)/shard_map/ppermute | solution.py:465
  112.2 5.8 %collective-permute-start.26 = (bf16[128,640]{1,0:T(8,128)(2,1)S(1)}, bf16[128,640]{1,0:T(8,128)(2,1)S(1)}, u32[]{:S(2)}, u32[]{:S(2)}) collective-permute-start(bf16[128,640]{1,0:T(8,128)(2,1)S(1)} %get-tuple-element.46), channel_id=1, source_target_pairs={{0,32},{16,48},{32,0},{48,16},{1,33},{17,49},{33,1},{49,17},{2,34}... | collective-permute-start | bytes 491528 | tf_op jit(solution)/shard_map/ppermute | solution.py:471
  113.2 6.1 %collective-permute-start.24 = (bf16[128,640]{1,0:T(8,128)(2,1)S(1)}, bf16[128,640]{1,0:T(8,128)(2,1)S(1)}, u32[]{:S(2)}, u32[]{:S(2)}) collective-permute-start(bf16[128,640]{1,0:T(8,128)(2,1)S(1)} %get-tuple-element.44), channel_id=1, source_target_pairs={{0,48},{16,0},{32,16},{48,32},{1,49},{17,1},{33,17},{49,33},{2,50}... | collective-permute-start | bytes 491528 | tf_op jit(solution)/shard_map/ppermute | solution.py:468
  114.3 5.4 %collective-permute-start.25 = (bf16[128,640]{1,0:T(8,128)(2,1)S(1)}, bf16[128,640]{1,0:T(8,128)(2,1)S(1)}, u32[]{:S(2)}, u32[]{:S(2)}) collective-permute-start(bf16[128,640]{1,0:T(8,128)(2,1)S(1)} %get-tuple-element.45), channel_id=1, source_target_pairs={{0,16},{16,32},{32,48},{48,0},{1,17},{17,33},{33,49},{49,1},{2,18}... | collective-permute-start | bytes 491528 | tf_op jit(solution)/shard_map/ppermute | solution.py:469
  (13 other events, 79.1 us)

commit v3 on v2

--- a/solution.py
+++ b/solution.py
@@ -54,9 +54,14 @@
     return place
 
 
-def pack_kernel(shards, count, pos, hidden, out):
+def pack_kernel(shards, count, pos_from, hidden_from, out, pos, hidden, sem):
+    load_pos = pltpu.make_async_copy(pos_from, pos, sem.at[0])
+    load_rows = pltpu.make_async_copy(hidden_from, hidden, sem.at[1])
+    load_pos.start()
+    load_rows.start()
     s, count = seq_place(), count[0]
     slots, tokens, width = pos.shape[0], hidden.shape[0], hidden.shape[1]
+    load_pos.wait()
     where = pos[...].reshape(1, slots)
     block = 128
     for b in range(shards * GROUP // block):
@@ -74,6 +79,8 @@
         live = (kc < slots // shards) & (slot_c < count)
         pick = onehot((iota((block, tokens), 1) == at) & live)
         rows = slice(b * block, (b + 1) * block)
+        if b == 0:
+            load_rows.wait()
         out[rows, :width] = jnp.dot(pick, hidden[...], preferred_element_type=F32).astype(BF)
         token = at + s * tokens
         lane = iota((block, META), 1)
@@ -200,9 +207,10 @@
     for i in range(n):
         start = (shard_ids[i] * tokens).astype(F32)
         bounds.append((below(start)[0], below(start + tokens)[1]))
-    count = jnp.int32(0)
-    clear = count
-    for masked in (False, True):
+    count = jnp.int32(1)
+    cut_off = count
+    steps[0] = n * tiles
+    for masked in (True, False):
         for i in range(n):
             least, most = bounds[i]
             for t in range(tiles):
@@ -210,10 +218,12 @@
                 cut = t * TILE < most
                 here = (t >= least // TILE) & (cut if masked else ~cut)
                 count += here.astype(jnp.int32)
-        if not masked:
-            clear = count
+        if masked:
+            cut_off = count
     for k in range(3):
         steps[count + k] = n * tiles
+    base = count & 1
+    middle = (cut_off - base + 1) // 2
 
     def parts(code):
         none = code >= n * tiles
@@ -255,18 +265,18 @@
 
     def run(done, first, last, masked):
         def pair(j, done):
-            a, b, c = steps[2 * j], steps[2 * j + 1], steps[2 * j + 2]
+            a, b, c = steps[base + 2 * j], steps[base + 2 * j + 1], steps[base + 2 * j + 2]
             done = arrive(done, b, c)
             advance(b, odd, tops.at[1], a, even, tops.at[0], masked)
             advance(c, even, tops.at[0], b, odd, tops.at[1], masked)
             return done
 
-        done = arrive(done, steps[2 * first])
-        advance(steps[2 * first], even, tops.at[0], None, None, None, masked)
+        done = arrive(done, steps[base + 2 * first])
+        advance(steps[base + 2 * first], even, tops.at[0], None, None, None, masked)
         return lax.fori_loop(first, last, pair, done)
 
-    done = run(jnp.int32(0), 0, clear // 2, False)
-    done = run(done, clear // 2, (count + 1) // 2, True)
+    done = run(jnp.int32(0), 0, middle, True)
+    done = run(done, middle, (count - base) // 2, False)
     arrive(done, jnp.int32(n * tiles - 1))
 
     for c, out in enumerate((first_out, second_out)):
@@ -381,22 +391,35 @@
     send = call(
         functools.partial(pack_kernel, shards),
         jax.ShapeDtypeStruct((lanes, width + META), BF),
-        [SM, VM, VM],
+        [SM, HB, HB],
         cand_count,
-        cand_pos,
-        hidden,
+        pltpu.with_memory_space_constraint(cand_pos, pltpu.HBM),
+        pltpu.with_memory_space_constraint(hidden, pltpu.HBM),
+        scratch_shapes=[
+            pltpu.VMEM(cand_pos.shape, jnp.int32),
+            pltpu.VMEM(hidden.shape, BF),
+            pltpu.SemaphoreType.DMA((2,)),
+        ],
     )
     swap = [(0, 1), (1, 0)]
     keys, values, send = lax.optimization_barrier((keys, values, send))
     values = call(turn_kernel, jax.ShapeDtypeStruct(values.shape[::-1], BF), [VM], values)
     got = lax.all_to_all(send.reshape(shards, GROUP, -1), SEQ, 0, 0, tiled=True)
     got = got.reshape(lanes, -1)
-    k_left, v_left = (
-        lax.ppermute(a, SEQ[0], shift(nx, 1)) for a in (keys, values)
-    )
-    k_right, v_right = (
-        lax.ppermute(a, SEQ[0], shift(nx, -1)) for a in (keys, values)
-    )
+    plane = SEQ[:2]
+
+    def mirrored(row, col):
+        return col if row % 2 == 0 else ny - 1 - col
+
+    def move(a, step):
+        pairs = [
+            (r * ny + q, (r + step) % nx * ny + mirrored(r, q)) for r in range(nx) for q in range(ny)
+        ]
+        return lax.ppermute(a, plane, pairs)
+
+    k_left, k_right = move(keys, 1), move(keys, -1)
+    v_left, v_right = move(values, 1), move(values, -1)
+    k_own, v_own = move(keys, 0), move(values, 0)
     rows, meta, back = call(
         compact_kernel,
         (
@@ -423,13 +446,15 @@
 
     k_far = lax.ppermute(k_left, SEQ[0], shift(nx, 1))
     v_far = lax.ppermute(v_right, SEQ[0], shift(nx, -1))
-    near_k, near_v = [keys, k_left, k_right, k_far], [values, v_left, v_right, v_far]
+    near_k, near_v = [k_own, k_left, k_right, k_far], [v_own, v_left, v_right, v_far]
     all_k = near_k + [lax.ppermute(a, SEQ[2], swap) for a in near_k[:3]]
     all_v = near_v + [lax.ppermute(a, SEQ[2], swap) for a in near_v[:3]]
     all_k.append(lax.ppermute(k_far, SEQ[2], swap))
     all_v.append(lax.ppermute(v_far, SEQ[2], swap))
     places = [((x + d) % nx, cc) for cc in (c, 1 - c) for d in (0, nx - 1, 1, 2)]
-    shard_ids = jnp.stack([(px * ny + y) * nc + pc for px, pc in places]).astype(jnp.int32)
+    shard_ids = jnp.stack(
+        [(px * ny + jnp.where(px % 2 == 0, y, ny - 1 - y)) * nc + pc for px, pc in places]
+    ).astype(jnp.int32)
 
     half = HEAD // 2
     freq = jnp.exp(-math.log(ROPE_BASE) * 2.0 * jnp.arange(half, dtype=F32) / HEAD)

time: 175 us -> 183 us (1.046)
  starting transfers between devices: 31 us -> 55 us
  blocking collectives: 72.6 us -> 53.9 us
  waiting for transfers between devices: 27.6 us -> 31.8 us
  local copies, waits for them, and re-layouts: 6.59 us -> 4.56 us
    all_to_all x1 -> x0, blocking collectives: 21.3 us -> none  [body(): got = lax.all_to_all(send.reshape(shards, GROUP, -1), SEQ, 0, 0, tiled=True)]
    all_to_all x0 -> x1, waiting for transfers between devices: none -> 10.2 us  [body(): got = lax.all_to_all(send.reshape(shards, GROUP, -1), SEQ, 0, 0, tiled=True)]
    all_to_all x0 -> x1, starting transfers between devices: none -> 8.59 us  [body(): got = lax.all_to_all(send.reshape(shards, GROUP, -1), SEQ, 0, 0, tiled=True)]
    ppermute x3, starting transfers between devices: 6.2 us -> 12.8 us  [body(): down = lax.ppermute(down, 'head', shift(nz, -1))]
    all_to_all x1, blocking collectives: 27.3 us -> 33.7 us  [body(): arrived = lax.all_to_all(partial, 'head', 0, 0, tiled=True)]
    ppermute x4 -> x6, starting transfers between devices: 4.22 us -> 9.59 us  [move(): return lax.ppermute(a, plane, pairs)]
    all_to_all x1, blocking collectives: 24 us -> 20.2 us  [body(): lax.all_to_all(to_send.reshape(shards, GROUP, width), SEQ, 0, 0, tiled=True)]
    ppermute x3, starting transfers between devices: 3.94 us -> 0.93 us  [body(): all_k = near_k + [lax.ppermute(a, SEQ[2], swap) for a in near_k[:3]]]
  transfers between devices with their start and end apart: 27 -> 30, of which waited for: 11 -> 13; matrix products, arithmetic and copies ran while one was open for 0% -> 0% of each run, Pallas kernels for 10% -> 9%
where the time goes in v3:
time: 183 us; the launch traced here: 182 us
  starting transfers between devices  55 us (30%)
  blocking collectives  53.9 us (29%)
  Pallas kernels  35.3 us (19%)
  waiting for transfers between devices  31.8 us (17%)
  local copies, waits for them, and re-layouts  4.56 us (2%)
    pallas_call x9, Pallas kernels, call(): pl.pallas_call(kernel, out_shape=out, in_specs=specs, out_specs=jax.tree....  35.3 us
    all_to_all x1, blocking collectives, body(): arrived = lax.all_to_all(partial, 'head', 0, 0, tiled=True)  33.7 us
    all_to_all x1, blocking collectives, body(): lax.all_to_all(to_send.reshape(shards, GROUP, width), SEQ, 0, 0, tiled=True)  20.2 us
    ppermute x3, starting transfers between devices, body(): down = lax.ppermute(down, 'head', shift(nz, -1))  12.8 us
    all_to_all x1, waiting for transfers between devices, body(): got = lax.all_to_all(send.reshape(shards, GROUP, -1), SEQ, 0, 0, tiled=True)  10.2 us
    ppermute x6, starting transfers between devices, move(): return lax.ppermute(a, plane, pairs)  9.59 us
    all_to_all x1, starting transfers between devices, body(): got = lax.all_to_all(send.reshape(shards, GROUP, -1), SEQ, 0, 0, tiled=True)  8.59 us
    ppermute x3, starting transfers between devices, body(): all_v = near_v + [lax.ppermute(a, SEQ[2], swap) for a in near_v[:3]]  5.34 us
  transfers between devices with their start and end apart: 30, of which 13 were waited for; matrix products, arithmetic and copies ran while one was open for 0% of the time, Pallas kernels for 9%

profile of v3, /device:TPU:1, one launch (start us, length us, event | category | flops | bytes accessed | tf_op | source)
XLA Modules:
  0.0 182.1 jit_solution(3147320256731023159)
XLA Ops:
  0.7 3.4 %shard_map.82 = bf16[512,640]{1,0:T(8,128)(2,1)} custom-call(s32[1]{0:T(128)S(6)} %copy.9.count, s32[384]{0:T(512)} %pos_from.1, bf16[1536,512]{1,0:T(8,128)(2,1)} %hidden_from.1), custom_call_target="tpu_custom_call" | custom-call | tf_op jit(solution)/shard_map/pallas_call | solution.py:39
  4.1 8.6 %all-to-all-start = ((bf16[32,16,640]{2,1,0:T(8,128)(2,1)}), bf16[32,16,640]{2,1,0:T(8,128)(2,1)S(1)}, u32[]{:S(2)}, u32[]{:S(2)}) async-start(bf16[32,16,640]{2,1,0:T(8,128)(2,1)} %bitcast), calls=%async_computation | async-start | bytes 1310720 | tf_op jit(solution)/shard_map/all_to_all | solution.py:407
  12.8 2.7 %collective-permute-start.20 = (bf16[128,1536]{1,0:T(8,128)(2,1)S(1)}, bf16[128,1536]{1,0:T(8,128)(2,1)S(1)}, u32[]{:S(2)}, u32[]{:S(2)}) collective-permute-start(bf16[128,1536]{1,0:T(8,128)(2,1)S(1)} %shard_map.85), channel_id=1, source_target_pairs={{0,192},{16,208},{32,224},{48,240},{64,48},{80,32},{96,16},{112,0}... | collective-permute-start | bytes 1179656 | tf_op jit(solution)/shard_map/ppermute | solution.py:418
  16.7 10.2 %all-to-all-done = bf16[32,16,640]{2,1,0:T(8,128)(2,1)S(1)} async-done(((bf16[32,16,640]{2,1,0:T(8,128)(2,1)}), bf16[32,16,640]{2,1,0:T(8,128)(2,1)S(1)}, u32[]{:S(2)}, u32[]{:S(2)}) %all-to-all-start) | async-done | bytes 655392 | tf_op jit(solution)/shard_map/all_to_all | solution.py:407
  27.6 1.7 collective-permute-start
  29.3 4.0 %collective-permute-start.1 = (bf16[128,512]{1,0:T(8,128)(2,1)S(1)}, bf16[128,512]{1,0:T(8,128)(2,1)S(1)}, u32[]{:S(2)}, u32[]{:S(2)}) collective-permute-start(bf16[128,512]{1,0:T(8,128)(2,1)S(1)} %get-tuple-element.29.refs_0_), channel_id=1, source_target_pairs={{0,7},{1,0},{2,1},{3,2},{4,3},{5,4},{6,5},{7,6},{8,15},{9,8},{10,9... | collective-permute-start | bytes 393224 | tf_op jit(solution)/shard_map/ppermute | solution.py:442
  33.3 2.9 %collective-permute-done.refs_1_ = bf16[128,512]{1,0:T(8,128)(2,1)S(1)} collective-permute-done((bf16[128,512]{1,0:T(8,128)(2,1)S(1)}, bf16[128,512]{1,0:T(8,128)(2,1)S(1)}, u32[]{:S(2)}, u32[]{:S(2)}) %collective-permute-start) | collective-permute-done | bytes 131104 | tf_op jit(solution)/shard_map/ppermute | solution.py:438
  37.0 2.4 %collective-permute-start.19 = (bf16[128,1536]{1,0:T(8,128)(2,1)S(1)}, bf16[128,1536]{1,0:T(8,128)(2,1)S(1)}, u32[]{:S(2)}, u32[]{:S(2)}) collective-permute-start(bf16[128,1536]{1,0:T(8,128)(2,1)S(1)} %shard_map.85), channel_id=1, source_target_pairs={{0,64},{16,80},{32,96},{48,112},{64,176},{80,160},{96,144},{112,12... | collective-permute-start | bytes 1179656 | tf_op jit(solution)/shard_map/ppermute | solution.py:418
  39.4 2.1 %collective-permute-done.20.refs_10_ = bf16[128,1536]{1,0:T(8,128)(2,1)S(1)} collective-permute-done((bf16[128,1536]{1,0:T(8,128)(2,1)S(1)}, bf16[128,1536]{1,0:T(8,128)(2,1)S(1)}, u32[]{:S(2)}, u32[]{:S(2)}) %collective-permute-start.20) | collective-permute-done | bytes 393248 | tf_op jit(solution)/shard_map/ppermute | solution.py:418
  41.5 1.6 collective-permute-start.10
  44.2 5.4 %collective-permute-start.3 = (bf16[128,512]{1,0:T(8,128)(2,1)S(1)}, bf16[128,512]{1,0:T(8,128)(2,1)S(1)}, u32[]{:S(2)}, u32[]{:S(2)}) collective-permute-start(bf16[128,512]{1,0:T(8,128)(2,1)S(1)} %collective-permute-done.1.refs_2_), channel_id=1, source_target_pairs={{0,7},{1,0},{2,1},{3,2},{4,3},{5,4},{6,5},{7,6},{8,15},{9,8},{10,9... | collective-permute-start | bytes 393224 | tf_op jit(solution)/shard_map/ppermute | solution.py:442
  49.6 1.9 %collective-permute-done.3.refs_4_ = bf16[128,512]{1,0:T(8,128)(2,1)S(1)} collective-permute-done((bf16[128,512]{1,0:T(8,128)(2,1)S(1)}, bf16[128,512]{1,0:T(8,128)(2,1)S(1)}, u32[]{:S(2)}, u32[]{:S(2)}) %collective-permute-start.3) | collective-permute-done | bytes 131104 | tf_op jit(solution)/shard_map/ppermute | solution.py:442
  53.6 3.4 %collective-permute-start.5 = (bf16[128,512]{1,0:T(8,128)(2,1)S(1)}, bf16[128,512]{1,0:T(8,128)(2,1)S(1)}, u32[]{:S(2)}, u32[]{:S(2)}) collective-permute-start(bf16[128,512]{1,0:T(8,128)(2,1)S(1)} %collective-permute-done.3.refs_4_), channel_id=1, source_target_pairs={{0,7},{1,0},{2,1},{3,2},{4,3},{5,4},{6,5},{7,6},{8,15},{9,8},{10,9... | collective-permute-start | bytes 393224 | tf_op jit(solution)/shard_map/ppermute | solution.py:442
  58.7 2.9 %collective-permute-start.24 = (bf16[128,1536]{1,0:T(8,128)(2,1)S(1)}, bf16[128,1536]{1,0:T(8,128)(2,1)}, u32[]{:S(2)}, u32[]{:S(2)}) collective-permute-start(bf16[128,1536]{1,0:T(8,128)(2,1)S(1)} %collective-permute-done.20.refs_10_), channel_id=1, source_target_pairs={{0,8},{8,0},{1,9},{9,1},{2,10},{10,2},{3,11},{11,3},{4,12},{12,4},... | collective-permute-start | bytes 1179656 | tf_op jit(solution)/shard_map/ppermute | solution.py:451
  63.2 3.2 %collective-permute-done.21.refs_11_ = bf16[128,1536]{1,0:T(8,128)(2,1)} collective-permute-done((bf16[128,1536]{1,0:T(8,128)(2,1)S(1)}, bf16[128,1536]{1,0:T(8,128)(2,1)}, u32[]{:S(2)}, u32[]{:S(2)}) %collective-permute-start.21) | collective-permute-done | bytes 393248 | tf_op jit(solution)/shard_map/ppermute | solution.py:448
  66.5 2.3 %collective-permute-start.6 = (bf16[128,512]{1,0:T(8,128)(2,1)}, bf16[128,512]{1,0:T(8,128)(2,1)S(1)}, u32[]{:S(2)}, u32[]{:S(2)}) collective-permute-start(bf16[128,512]{1,0:T(8,128)(2,1)} %copy-done.13), channel_id=1, source_target_pairs={{0,1},{1,2},{2,3},{3,4},{4,5},{5,6},{6,7},{7,0},{8,9},{9,10},{10,1... | collective-permute-start | bytes 393224 | tf_op jit(solution)/shard_map/ppermute | solution.py:438
  68.8 2.1 %collective-permute-start.23 = (bf16[128,1536]{1,0:T(8,128)(2,1)S(1)}, bf16[128,1536]{1,0:T(8,128)(2,1)S(1)}, u32[]{:S(2)}, u32[]{:S(2)}) collective-permute-start(bf16[128,1536]{1,0:T(8,128)(2,1)S(1)} %collective-permute-done.19.refs_9_), channel_id=1, source_target_pairs={{0,8},{8,0},{1,9},{9,1},{2,10},{10,2},{3,11},{11,3},{4,12},{12,4},... | collective-permute-start | bytes 1179656 | tf_op jit(solution)/shard_map/ppermute | solution.py:451
  72.1 2.5 %collective-permute-start.17 = (bf16[1536,128]{1,0:T(8,128)(2,1)S(1)}, bf16[1536,128]{1,0:T(8,128)(2,1)}, u32[]{:S(2)}, u32[]{:S(2)}) collective-permute-start(bf16[1536,128]{1,0:T(8,128)(2,1)S(1)} %collective-permute-done.13.refs_3_), channel_id=1, source_target_pairs={{0,8},{8,0},{1,9},{9,1},{2,10},{10,2},{3,11},{11,3},{4,12},{12,4},... | collective-permute-start | bytes 1179656 | tf_op jit(solution)/shard_map/ppermute | solution.py:452
  75.1 3.2 %shard_map.84.first_q = bf16[128,640]{1,0:T(8,128)(2,1)S(1)} custom-call(s32[1]{0:T(128)} %bitcast.10.z, bf16[128,128]{1,0:T(8,128)(2,1)S(1)} %get-tuple-element.28.meta, f32[1,4096]{1,0:T(1,128)S(1)} %bitcast.17, f32[128,128]{1,0:T(8,128)S(1)} %get-tuple-element.50.cosine, f32[128,128]{1,0:T(8,128)S(1)} %get-tuple-element.51.sine, ...), custom_call_target="tpu_custom_call" | custom-call | tf_op jit(solution)/shard_map/pallas_call | solution.py:39
  80.8 1.7 collective-permute-start.9
  82.6 1.5 collective-permute-start.7
  84.1 2.0 %collective-permute-done.8.first_q = bf16[128,640]{1,0:T(8,128)(2,1)S(1)} collective-permute-done((bf16[128,640]{1,0:T(8,128)(2,1)S(1)}, bf16[128,640]{1,0:T(8,128)(2,1)S(1)}, u32[]{:S(2)}, u32[]{:S(2)}) %collective-permute-start.8) | collective-permute-done | bytes 163872 | tf_op jit(solution)/shard_map/ppermute | solution.py:489
  88.3 12.8 %shard_map.86 = (bf16[128,640]{1,0:T(8,128)(2,1)S(1)}, bf16[128,640]{1,0:T(8,128)(2,1)S(1)}, bf16[8,1536,128]{2,1,0:T(8,128)(2,1)S(1)}, bf16[8,144,1536]{2,1,0:T(8,128)(2,1)S(1)}) custom-call(s32[8]{0:T(128)S(1)} %stack.35.shard_ids, bf16[128,640]{1,0:T(8,128)(2,1)S(1)} %collective-permute-done.8.first_q, ...), custom_call_target="tpu_custom_call" | custom-call | flops 10000000000 | bytes 7000000 | tf_op jit(solution)/shard_map/pallas_call | solution.py:39
  101.1 11.3 %shard_map.87 = (bf16[128,640]{1,0:T(8,128)(2,1)S(1)}, bf16[128,640]{1,0:T(8,128)(2,1)S(1)}) custom-call(s32[8]{0:T(128)S(1)} %stack.35.shard_ids, bf16[128,640]{1,0:T(8,128)(2,1)S(1)} %shard_map.84.first_q, bf16[128,640]{1,0:T(8,128)(2,1)S(1)} %collective-permute-done.7.second_q, bf16[8,1536,128]{2,1,0:T(8,128)(2,1)S(1)} %get-tuple-element.41.refs_0_, ...), custom_call_target="tpu_custom_call" | custom-call | flops 10000000000 | bytes 7000000 | tf_op jit(solution)/shard_map/pallas_call | solution.py:39
  112.4 3.7 %collective-permute-start.28 = (bf16[128,640]{1,0:T(8,128)(2,1)S(1)}, bf16[128,640]{1,0:T(8,128)(2,1)S(1)}, u32[]{:S(2)}, u32[]{:S(2)}) collective-permute-start(bf16[128,640]{1,0:T(8,128)(2,1)S(1)} %get-tuple-element.46), channel_id=1, source_target_pairs={{0,32},{16,48},{32,0},{48,16},{1,33},{17,49},{33,1},{49,17},{2,34}... | collective-permute-start | bytes 491528 | tf_op jit(solution)/shard_map/ppermute | solution.py:496
  117.6 1.2 collective-permute-done.28.refs_3_
  118.8 3.1 %collective-permute-done.26.refs_1_ = bf16[128,640]{1,0:T(8,128)(2,1)S(1)} collective-permute-done((bf16[128,640]{1,0:T(8,128)(2,1)S(1)}, bf16[128,640]{1,0:T(8,128)(2,1)S(1)}, u32[]{:S(2)}, u32[]{:S(2)}) %collective-permute-start.26) | collective-permute-done | bytes 163872 | tf_op jit(solution)/shard_map/ppermute | solution.py:493
  122.0 2.3 %collective-permute-done.27.refs_2_ = bf16[128,640]{1,0:T(8,128)(2,1)S(1)} collective-permute-done((bf16[128,640]{1,0:T(8,128)(2,1)S(1)}, bf16[128,640]{1,0:T(8,128)(2,1)S(1)}, u32[]{:S(2)}, u32[]{:S(2)}) %collective-permute-start.27) | collective-permute-done | bytes 163872 | tf_op jit(solution)/shard_map/ppermute | solution.py:494
  124.3 1.4 shard_map.88
  125.7 33.7 %all_to_all.15.parts = bf16[8,128,512]{2,1,0:T(8,128)(2,1)S(1)} all-to-all(bf16[8,128,512]{2,1,0:T(8,128)(2,1)S(1)} %shard_map.88), channel_id=1, replica_groups=mesh['seq_0'=4,'seq_1'=4,'seq_2'=2,'head'=8] {'head'}, dimensions={0} | all-to-all | bytes 2097152 | tf_op jit(solution)/shard_map/all_to_all | solution.py:505
  159.4 1.3 shard_map.89
  160.7 20.2 %all_to_all.16 = bf16[32,16,512]{2,1,0:T(8,128)(2,1)S(1)} all-to-all(bf16[32,16,512]{2,1,0:T(8,128)(2,1)S(1)} %bitcast.14), channel_id=1, replica_groups=mesh['seq_0'=4,'seq_1'=4,'seq_2'=2,'head'=8] {'seq_0','seq_1','seq_2'}, dimensions={0} | all-to-all | bytes 1048576 | tf_op jit(solution)/shard_map/all_to_all | solution.py:509
  (75 shorter events, 18.3 us)
Async XLA Ops:
  4.1 22.8 %all-to-all-start = ((bf16[32,16,640]{2,1,0:T(8,128)(2,1)}), bf16[32,16,640]{2,1,0:T(8,128)(2,1)S(1)}, u32[]{:S(2)}, u32[]{:S(2)}) async-start(bf16[32,16,640]{2,1,0:T(8,128)(2,1)} %bitcast), calls=%async_computation | async-start | bytes 1310720 | tf_op jit(solution)/shard_map/all_to_all | solution.py:407
  12.8 28.7 %collective-permute-start.20 = (bf16[128,1536]{1,0:T(8,128)(2,1)S(1)}, bf16[128,1536]{1,0:T(8,128)(2,1)S(1)}, u32[]{:S(2)}, u32[]{:S(2)}) collective-permute-start(bf16[128,1536]{1,0:T(8,128)(2,1)S(1)} %shard_map.85), channel_id=1, source_target_pairs={{0,192},{16,208},{32,224},{48,240},{64,48},{80,32},{96,16},{112,0}... | collective-permute-start | bytes 1179656 | tf_op jit(solution)/shard_map/ppermute | solution.py:418
  15.5 27.6 %collective-permute-start.11 = (bf16[1536,128]{1,0:T(8,128)(2,1)}, bf16[1536,128]{1,0:T(8,128)(2,1)S(1)}, u32[]{:S(2)}, u32[]{:S(2)}) collective-permute-start(bf16[1536,128]{1,0:T(8,128)(2,1)} %param.12), channel_id=1, source_target_pairs={{0,64},{16,80},{32,96},{48,112},{64,176},{80,160},{96,144},{112,12... | collective-permute-start | bytes 1179656 | tf_op jit(solution)/shard_map/ppermute | solution.py:418
  26.8 48.2 %copy-start.4 = (f32[4096]{0:T(1024)S(1)}, f32[4096]{0:T(1024)}, u32[]{:S(2)}) copy-start(f32[4096]{0:T(1024)} %param.9) | copy-start | bytes 49156
  27.6 73.5 %copy-start.3 = (bf16[512,128]{1,0:T(8,128)(2,1)}, bf16[512,128]{1,0:T(8,128)(2,1)S(1)}, u32[]{:S(2)}) copy-start(bf16[512,128]{1,0:T(8,128)(2,1)S(1)} %get-tuple-element.27.back) | copy-start | bytes 393220
  27.6 8.7 %collective-permute-start = (bf16[128,512]{1,0:T(8,128)(2,1)S(1)}, bf16[128,512]{1,0:T(8,128)(2,1)S(1)}, u32[]{:S(2)}, u32[]{:S(2)}) collective-permute-start(bf16[128,512]{1,0:T(8,128)(2,1)S(1)} %get-tuple-element.29.refs_0_), channel_id=1, source_target_pairs={{0,1},{1,2},{2,3},{3,4},{4,5},{5,6},{6,7},{7,0},{8,9},{9,10},{10,1... | collective-permute-start | bytes 393224 | tf_op jit(solution)/shard_map/ppermute | solution.py:438
  29.3 7.0 %collective-permute-start.1 = (bf16[128,512]{1,0:T(8,128)(2,1)S(1)}, bf16[128,512]{1,0:T(8,128)(2,1)S(1)}, u32[]{:S(2)}, u32[]{:S(2)}) collective-permute-start(bf16[128,512]{1,0:T(8,128)(2,1)S(1)} %get-tuple-element.29.refs_0_), channel_id=1, source_target_pairs={{0,7},{1,0},{2,1},{3,2},{4,3},{5,4},{6,5},{7,6},{8,15},{9,8},{10,9... | collective-permute-start | bytes 393224 | tf_op jit(solution)/shard_map/ppermute | solution.py:442
  36.3 7.9 %collective-permute-start.2 = (bf16[128,512]{1,0:T(8,128)(2,1)S(1)}, bf16[128,512]{1,0:T(8,128)(2,1)S(1)}, u32[]{:S(2)}, u32[]{:S(2)}) collective-permute-start(bf16[128,512]{1,0:T(8,128)(2,1)S(1)} %collective-permute-done.refs_1_), channel_id=1, source_target_pairs={{0,1},{1,2},{2,3},{3,4},{4,5},{5,6},{6,7},{7,0},{8,9},{9,10},{10,1... | collective-permute-start | bytes 393224 | tf_op jit(solution)/shard_map/ppermute | solution.py:438
  36.3 15.5 %collective-permute-start.18 = (bf16[128,1536]{1,0:T(8,128)(2,1)S(1)}, bf16[128,1536]{1,0:T(8,128)(2,1)S(1)}, u32[]{:S(2)}, u32[]{:S(2)}) collective-permute-start(bf16[128,1536]{1,0:T(8,128)(2,1)S(1)} %shard_map.85), channel_id=1, source_target_pairs={{0,0},{16,16},{32,32},{48,48},{64,112},{80,96},{96,80},{112,64},{1... | collective-permute-start | bytes 1179656 | tf_op jit(solution)/shard_map/ppermute | solution.py:418
  37.0 16.5 %collective-permute-start.19 = (bf16[128,1536]{1,0:T(8,128)(2,1)S(1)}, bf16[128,1536]{1,0:T(8,128)(2,1)S(1)}, u32[]{:S(2)}, u32[]{:S(2)}) collective-permute-start(bf16[128,1536]{1,0:T(8,128)(2,1)S(1)} %shard_map.85), channel_id=1, source_target_pairs={{0,64},{16,80},{32,96},{48,112},{64,176},{80,160},{96,144},{112,12... | collective-permute-start | bytes 1179656 | tf_op jit(solution)/shard_map/ppermute | solution.py:418
  41.5 15.4 %collective-permute-start.10 = (bf16[1536,128]{1,0:T(8,128)(2,1)}, bf16[1536,128]{1,0:T(8,128)(2,1)S(1)}, u32[]{:S(2)}, u32[]{:S(2)}) collective-permute-start(bf16[1536,128]{1,0:T(8,128)(2,1)} %param.12), channel_id=1, source_target_pairs={{0,0},{16,16},{32,32},{48,48},{64,112},{80,96},{96,80},{112,64},{1... | collective-permute-start | bytes 1179656 | tf_op jit(solution)/shard_map/ppermute | solution.py:418
  43.2 15.5 %collective-permute-start.12 = (bf16[1536,128]{1,0:T(8,128)(2,1)}, bf16[1536,128]{1,0:T(8,128)(2,1)S(1)}, u32[]{:S(2)}, u32[]{:S(2)}) collective-permute-start(bf16[1536,128]{1,0:T(8,128)(2,1)} %param.12), channel_id=1, source_target_pairs={{0,192},{16,208},{32,224},{48,240},{64,48},{80,32},{96,16},{112,0}... | collective-permute-start | bytes 1179656 | tf_op jit(solution)/shard_map/ppermute | solution.py:418
  44.2 7.3 %collective-permute-start.3 = (bf16[128,512]{1,0:T(8,128)(2,1)S(1)}, bf16[128,512]{1,0:T(8,128)(2,1)S(1)}, u32[]{:S(2)}, u32[]{:S(2)}) collective-permute-start(bf16[128,512]{1,0:T(8,128)(2,1)S(1)} %collective-permute-done.1.refs_2_), channel_id=1, source_target_pairs={{0,7},{1,0},{2,1},{3,2},{4,3},{5,4},{6,5},{7,6},{8,15},{9,8},{10,9... | collective-permute-start | bytes 393224 | tf_op jit(solution)/shard_map/ppermute | solution.py:442
  51.5 15.0 %collective-permute-start.21 = (bf16[128,1536]{1,0:T(8,128)(2,1)S(1)}, bf16[128,1536]{1,0:T(8,128)(2,1)}, u32[]{:S(2)}, u32[]{:S(2)}) collective-permute-start(bf16[128,1536]{1,0:T(8,128)(2,1)S(1)} %collective-permute-done.20.refs_10_), channel_id=1, source_target_pairs={{0,192},{64,0},{128,64},{192,128},{1,193},{65,1},{129,65},{193,129... | collective-permute-start | bytes 1179656 | tf_op jit(solution)/shard_map/ppermute | solution.py:448
  51.9 9.7 %collective-permute-start.4 = (bf16[128,512]{1,0:T(8,128)(2,1)S(1)}, bf16[128,512]{1,0:T(8,128)(2,1)S(1)}, u32[]{:S(2)}, u32[]{:S(2)}) collective-permute-start(bf16[128,512]{1,0:T(8,128)(2,1)S(1)} %collective-permute-done.2.refs_3_), channel_id=1, source_target_pairs={{0,1},{1,2},{2,3},{3,4},{4,5},{5,6},{6,7},{7,0},{8,9},{9,10},{10,1... | collective-permute-start | bytes 393224 | tf_op jit(solution)/shard_map/ppermute | solution.py:438
  53.6 8.4 %collective-permute-start.5 = (bf16[128,512]{1,0:T(8,128)(2,1)S(1)}, bf16[128,512]{1,0:T(8,128)(2,1)S(1)}, u32[]{:S(2)}, u32[]{:S(2)}) collective-permute-start(bf16[128,512]{1,0:T(8,128)(2,1)S(1)} %collective-permute-done.3.refs_4_), channel_id=1, source_target_pairs={{0,7},{1,0},{2,1},{3,2},{4,3},{5,4},{6,5},{7,6},{8,15},{9,8},{10,9... | collective-permute-start | bytes 393224 | tf_op jit(solution)/shard_map/ppermute | solution.py:442
  57.0 11.8 %collective-permute-start.13 = (bf16[1536,128]{1,0:T(8,128)(2,1)S(1)}, bf16[1536,128]{1,0:T(8,128)(2,1)S(1)}, u32[]{:S(2)}, u32[]{:S(2)}) collective-permute-start(bf16[1536,128]{1,0:T(8,128)(2,1)S(1)} %collective-permute-done.11.refs_1_), channel_id=1, source_target_pairs={{0,64},{64,128},{128,192},{192,0},{1,65},{65,129},{129,193},{193,1... | collective-permute-start | bytes 1179656 | tf_op jit(solution)/shard_map/ppermute | solution.py:447
  58.7 12.2 %collective-permute-start.24 = (bf16[128,1536]{1,0:T(8,128)(2,1)S(1)}, bf16[128,1536]{1,0:T(8,128)(2,1)}, u32[]{:S(2)}, u32[]{:S(2)}) collective-permute-start(bf16[128,1536]{1,0:T(8,128)(2,1)S(1)} %collective-permute-done.20.refs_10_), channel_id=1, source_target_pairs={{0,8},{8,0},{1,9},{9,1},{2,10},{10,2},{3,11},{11,3},{4,12},{12,4},... | collective-permute-start | bytes 1179656 | tf_op jit(solution)/shard_map/ppermute | solution.py:451
  61.6 9.6 %collective-permute-start.15 = (bf16[1536,128]{1,0:T(8,128)(2,1)S(1)}, bf16[1536,128]{1,0:T(8,128)(2,1)}, u32[]{:S(2)}, u32[]{:S(2)}) collective-permute-start(bf16[1536,128]{1,0:T(8,128)(2,1)S(1)} %collective-permute-done.11.refs_1_), channel_id=1, source_target_pairs={{0,8},{8,0},{1,9},{9,1},{2,10},{10,2},{3,11},{11,3},{4,12},{12,4},... | collective-permute-start | bytes 1179656 | tf_op jit(solution)/shard_map/ppermute | solution.py:450
  62.9 8.8 %collective-permute-start.22 = (bf16[128,1536]{1,0:T(8,128)(2,1)S(1)}, bf16[128,1536]{1,0:T(8,128)(2,1)}, u32[]{:S(2)}, u32[]{:S(2)}) collective-permute-start(bf16[128,1536]{1,0:T(8,128)(2,1)S(1)} %collective-permute-done.18.refs_8_), channel_id=1, source_target_pairs={{0,8},{8,0},{1,9},{9,1},{2,10},{10,2},{3,11},{11,3},{4,12},{12,4},... | collective-permute-start | bytes 1179656 | tf_op jit(solution)/shard_map/ppermute | solution.py:451
  66.5 5.6 %collective-permute-start.6 = (bf16[128,512]{1,0:T(8,128)(2,1)}, bf16[128,512]{1,0:T(8,128)(2,1)S(1)}, u32[]{:S(2)}, u32[]{:S(2)}) collective-permute-start(bf16[128,512]{1,0:T(8,128)(2,1)} %copy-done.13), channel_id=1, source_target_pairs={{0,1},{1,2},{2,3},{3,4},{4,5},{5,6},{6,7},{7,0},{8,9},{9,10},{10,1... | collective-permute-start | bytes 393224 | tf_op jit(solution)/shard_map/ppermute | solution.py:438
  68.8 9.5 %collective-permute-start.23 = (bf16[128,1536]{1,0:T(8,128)(2,1)S(1)}, bf16[128,1536]{1,0:T(8,128)(2,1)S(1)}, u32[]{:S(2)}, u32[]{:S(2)}) collective-permute-start(bf16[128,1536]{1,0:T(8,128)(2,1)S(1)} %collective-permute-done.19.refs_9_), channel_id=1, source_target_pairs={{0,8},{8,0},{1,9},{9,1},{2,10},{10,2},{3,11},{11,3},{4,12},{12,4},... | collective-permute-start | bytes 1179656 | tf_op jit(solution)/shard_map/ppermute | solution.py:451
  70.9 9.2 %collective-permute-start.14 = (bf16[1536,128]{1,0:T(8,128)(2,1)S(1)}, bf16[1536,128]{1,0:T(8,128)(2,1)S(1)}, u32[]{:S(2)}, u32[]{:S(2)}) collective-permute-start(bf16[1536,128]{1,0:T(8,128)(2,1)S(1)} %collective-permute-done.10.refs_0_), channel_id=1, source_target_pairs={{0,8},{8,0},{1,9},{9,1},{2,10},{10,2},{3,11},{11,3},{4,12},{12,4},... | collective-permute-start | bytes 1179656 | tf_op jit(solution)/shard_map/ppermute | solution.py:450
  71.2 11.4 %collective-permute-start.16 = (bf16[1536,128]{1,0:T(8,128)(2,1)S(1)}, bf16[1536,128]{1,0:T(8,128)(2,1)}, u32[]{:S(2)}, u32[]{:S(2)}) collective-permute-start(bf16[1536,128]{1,0:T(8,128)(2,1)S(1)} %collective-permute-done.12.refs_2_), channel_id=1, source_target_pairs={{0,8},{8,0},{1,9},{9,1},{2,10},{10,2},{3,11},{11,3},{4,12},{12,4},... | collective-permute-start | bytes 1179656 | tf_op jit(solution)/shard_map/ppermute | solution.py:450
  71.7 12.4 %collective-permute-start.25 = (bf16[128,1536]{1,0:T(8,128)(2,1)}, bf16[128,1536]{1,0:T(8,128)(2,1)}, u32[]{:S(2)}, u32[]{:S(2)}) collective-permute-start(bf16[128,1536]{1,0:T(8,128)(2,1)} %collective-permute-done.21.refs_11_), channel_id=1, source_target_pairs={{0,8},{8,0},{1,9},{9,1},{2,10},{10,2},{3,11},{11,3},{4,12},{12,4},... | collective-permute-start | bytes 1179656 | tf_op jit(solution)/shard_map/ppermute | solution.py:453
  72.1 11.9 %collective-permute-start.17 = (bf16[1536,128]{1,0:T(8,128)(2,1)S(1)}, bf16[1536,128]{1,0:T(8,128)(2,1)}, u32[]{:S(2)}, u32[]{:S(2)}) collective-permute-start(bf16[1536,128]{1,0:T(8,128)(2,1)S(1)} %collective-permute-done.13.refs_3_), channel_id=1, source_target_pairs={{0,8},{8,0},{1,9},{9,1},{2,10},{10,2},{3,11},{11,3},{4,12},{12,4},... | collective-permute-start | bytes 1179656 | tf_op jit(solution)/shard_map/ppermute | solution.py:452
  79.0 7.0 %collective-permute-start.8 = (bf16[128,640]{1,0:T(8,128)(2,1)S(1)}, bf16[128,640]{1,0:T(8,128)(2,1)S(1)}, u32[]{:S(2)}, u32[]{:S(2)}) collective-permute-start(bf16[128,640]{1,0:T(8,128)(2,1)S(1)} %shard_map.84.first_q), channel_id=1, source_target_pairs={{0,16},{16,32},{32,48},{48,0},{1,17},{17,33},{33,49},{49,1},{2,18}... | collective-permute-start | bytes 491528 | tf_op jit(solution)/shard_map/ppermute | solution.py:489
  80.8 5.5 %collective-permute-start.9 = (bf16[128,640]{1,0:T(8,128)(2,1)S(1)}, bf16[128,640]{1,0:T(8,128)(2,1)S(1)}, u32[]{:S(2)}, u32[]{:S(2)}) collective-permute-start(bf16[128,640]{1,0:T(8,128)(2,1)S(1)} %shard_map.84.first_q), channel_id=1, source_target_pairs={{0,48},{16,0},{32,16},{48,32},{1,49},{17,1},{33,17},{49,33},{2,50}... | collective-permute-start | bytes 491528 | tf_op jit(solution)/shard_map/ppermute | solution.py:489
  82.6 18.5 %collective-permute-start.7 = (bf16[128,640]{1,0:T(8,128)(2,1)S(1)}, bf16[128,640]{1,0:T(8,128)(2,1)S(1)}, u32[]{:S(2)}, u32[]{:S(2)}) collective-permute-start(bf16[128,640]{1,0:T(8,128)(2,1)S(1)} %shard_map.84.first_q), channel_id=1, source_target_pairs={{0,32},{16,48},{32,0},{48,16},{1,33},{17,49},{33,1},{49,17},{2,34}... | collective-permute-start | bytes 491528 | tf_op jit(solution)/shard_map/ppermute | solution.py:490
  112.4 6.4 %collective-permute-start.28 = (bf16[128,640]{1,0:T(8,128)(2,1)S(1)}, bf16[128,640]{1,0:T(8,128)(2,1)S(1)}, u32[]{:S(2)}, u32[]{:S(2)}) collective-permute-start(bf16[128,640]{1,0:T(8,128)(2,1)S(1)} %get-tuple-element.46), channel_id=1, source_target_pairs={{0,32},{16,48},{32,0},{48,16},{1,33},{17,49},{33,1},{49,17},{2,34}... | collective-permute-start | bytes 491528 | tf_op jit(solution)/shard_map/ppermute | solution.py:496
  116.1 5.9 %collective-permute-start.26 = (bf16[128,640]{1,0:T(8,128)(2,1)S(1)}, bf16[128,640]{1,0:T(8,128)(2,1)S(1)}, u32[]{:S(2)}, u32[]{:S(2)}) collective-permute-start(bf16[128,640]{1,0:T(8,128)(2,1)S(1)} %get-tuple-element.44), channel_id=1, source_target_pairs={{0,48},{16,0},{32,16},{48,32},{1,49},{17,1},{33,17},{49,33},{2,50}... | collective-permute-start | bytes 491528 | tf_op jit(solution)/shard_map/ppermute | solution.py:493
  117.2 7.1 %collective-permute-start.27 = (bf16[128,640]{1,0:T(8,128)(2,1)S(1)}, bf16[128,640]{1,0:T(8,128)(2,1)S(1)}, u32[]{:S(2)}, u32[]{:S(2)}) collective-permute-start(bf16[128,640]{1,0:T(8,128)(2,1)S(1)} %get-tuple-element.45), channel_id=1, source_target_pairs={{0,16},{16,32},{32,48},{48,0},{1,17},{17,33},{33,49},{49,1},{2,18}... | collective-permute-start | bytes 491528 | tf_op jit(solution)/shard_map/ppermute | solution.py:494
  (13 other events, 204.1 us)

commit v4 on v2

--- a/solution.py
+++ b/solution.py
@@ -200,9 +200,10 @@
     for i in range(n):
         start = (shard_ids[i] * tokens).astype(F32)
         bounds.append((below(start)[0], below(start + tokens)[1]))
-    count = jnp.int32(0)
-    clear = count
-    for masked in (False, True):
+    count = jnp.int32(1)
+    cut_off = count
+    steps[0] = n * tiles
+    for masked in (True, False):
         for i in range(n):
             least, most = bounds[i]
             for t in range(tiles):
@@ -210,10 +211,12 @@
                 cut = t * TILE < most
                 here = (t >= least // TILE) & (cut if masked else ~cut)
                 count += here.astype(jnp.int32)
-        if not masked:
-            clear = count
+        if masked:
+            cut_off = count
     for k in range(3):
         steps[count + k] = n * tiles
+    base = count & 1
+    middle = (cut_off - base + 1) // 2
 
     def parts(code):
         none = code >= n * tiles
@@ -255,18 +258,18 @@
 
     def run(done, first, last, masked):
         def pair(j, done):
-            a, b, c = steps[2 * j], steps[2 * j + 1], steps[2 * j + 2]
+            a, b, c = steps[base + 2 * j], steps[base + 2 * j + 1], steps[base + 2 * j + 2]
             done = arrive(done, b, c)
             advance(b, odd, tops.at[1], a, even, tops.at[0], masked)
             advance(c, even, tops.at[0], b, odd, tops.at[1], masked)
             return done
 
-        done = arrive(done, steps[2 * first])
-        advance(steps[2 * first], even, tops.at[0], None, None, None, masked)
+        done = arrive(done, steps[base + 2 * first])
+        advance(steps[base + 2 * first], even, tops.at[0], None, None, None, masked)
         return lax.fori_loop(first, last, pair, done)
 
-    done = run(jnp.int32(0), 0, clear // 2, False)
-    done = run(done, clear // 2, (count + 1) // 2, True)
+    done = run(jnp.int32(0), 0, middle, True)
+    done = run(done, middle, (count - base) // 2, False)
     arrive(done, jnp.int32(n * tiles - 1))
 
     for c, out in enumerate((first_out, second_out)):
@@ -419,7 +422,6 @@
             down = lax.ppermute(down, "head", shift(nz, -1))
             slices.append(down)
             order.append(k)
-            up, down = lax.optimization_barrier((up, down))
 
     k_far = lax.ppermute(k_left, SEQ[0], shift(nx, 1))
     v_far = lax.ppermute(v_right, SEQ[0], shift(nx, -1))

time: 175 us -> 173 us (0.989)
  blocking collectives: 72.6 us -> 50.5 us
  starting transfers between devices: 31 us -> 49.1 us
    all_to_all x1 -> x0, blocking collectives: 21.3 us -> none  [body(): got = lax.all_to_all(send.reshape(shards, GROUP, -1), SEQ, 0, 0, tiled=True)]
    ppermute x2, waiting for transfers between devices: 0.01 us -> 10.8 us  [body(): lax.ppermute(a, SEQ[0], shift(nx, -1))]
    all_to_all x0 -> x1, starting transfers between devices: none -> 8.58 us  [body(): got = lax.all_to_all(send.reshape(shards, GROUP, -1), SEQ, 0, 0, tiled=True)]
    ppermute x1, waiting for transfers between devices: 5.01 us -> 0.01 us  [body(): v_far = lax.ppermute(v_right, SEQ[0], shift(nx, -1))]
    ppermute x4, starting transfers between devices: 5.81 us -> 1.65 us  [body(): up = lax.ppermute(up, 'head', shift(nz, 1))]
    ppermute x1, starting transfers between devices: 0.51 us -> 4.38 us  [body(): all_k.append(lax.ppermute(k_far, SEQ[2], swap))]
    ppermute x3, starting transfers between devices: 6.2 us -> 9.29 us  [body(): down = lax.ppermute(down, 'head', shift(nz, -1))]
    ppermute x3, waiting for transfers between devices: 2.88 us -> 0.01 us  [body(): down = lax.ppermute(down, 'head', shift(nz, -1))]
  transfers between devices with their start and end apart: 27 -> 28, of which waited for: 11 -> 10; matrix products, arithmetic and copies ran while one was open for 0% -> 0% of each run, Pallas kernels for 10% -> 10%
where the time goes in v4:
time: 173 us
  blocking collectives  50.5 us (29%)
  starting transfers between devices  49.1 us (28%)
  Pallas kernels  36.7 us (21%)
  waiting for transfers between devices  28.6 us (17%)
  local copies, waits for them, and re-layouts  6.34 us (4%)
    pallas_call x9, Pallas kernels, call(): pl.pallas_call(kernel, out_shape=out, in_specs=specs, out_specs=jax.tree....  36.7 us
    all_to_all x1, blocking collectives, body(): arrived = lax.all_to_all(partial, 'head', 0, 0, tiled=True)  28.1 us
    all_to_all x1, blocking collectives, body(): lax.all_to_all(to_send.reshape(shards, GROUP, width), SEQ, 0, 0, tiled=True)  22.4 us
    ppermute x2, waiting for transfers between devices, body(): lax.ppermute(a, SEQ[0], shift(nx, -1))  10.8 us
    ppermute x3, starting transfers between devices, body(): down = lax.ppermute(down, 'head', shift(nz, -1))  9.29 us
    all_to_all x1, starting transfers between devices, body(): got = lax.all_to_all(send.reshape(shards, GROUP, -1), SEQ, 0, 0, tiled=True)  8.58 us
    ppermute x2, waiting for transfers between devices, body(): lax.ppermute(a, SEQ[0], shift(nx, 1))  6.8 us
    unnamed x32, local copies, waits for them, and re-layouts  6.26 us
  transfers between devices with their start and end apart: 28, of which 10 were waited for; matrix products, arithmetic and copies ran while one was open for 0% of the time, Pallas kernels for 10%

profile of v4, /device:TPU:1, one launch (start us, length us, event | category | flops | bytes accessed | tf_op | source)
XLA Modules:
  0.0 172.8 jit_solution(18163459093317643140)
XLA Ops:
  0.7 1.4 copy-done.1
  2.7 2.1 %shard_map.82 = bf16[512,640]{1,0:T(8,128)(2,1)} custom-call(s32[1]{0:T(128)S(6)} %copy.9.count, s32[384]{0:T(512)S(1)} %copy-done.6, bf16[1536,512]{1,0:T(8,128)(2,1)S(1)} %copy-done.1), custom_call_target="tpu_custom_call" | custom-call | tf_op jit(solution)/shard_map/pallas_call | solution.py:39
  4.8 8.6 %all-to-all-start = ((bf16[32,16,640]{2,1,0:T(8,128)(2,1)}), bf16[32,16,640]{2,1,0:T(8,128)(2,1)S(1)}, u32[]{:S(2)}, u32[]{:S(2)}) async-start(bf16[32,16,640]{2,1,0:T(8,128)(2,1)} %bitcast), calls=%async_computation | async-start | bytes 1310720 | tf_op jit(solution)/shard_map/all_to_all | solution.py:395
  13.6 2.7 %collective-permute-start.18 = (bf16[128,1536]{1,0:T(8,128)(2,1)S(1)}, bf16[128,1536]{1,0:T(8,128)(2,1)S(1)}, u32[]{:S(2)}, u32[]{:S(2)}) collective-permute-start(bf16[128,1536]{1,0:T(8,128)(2,1)S(1)} %shard_map.85.refs_8_), channel_id=1, source_target_pairs={{0,192},{64,0},{128,64},{192,128},{1,193},{65,1},{129,65},{193,129... | collective-permute-start | bytes 1179656 | tf_op jit(solution)/shard_map/ppermute | solution.py:401
  16.5 2.5 %collective-permute-start.11 = (bf16[1536,128]{1,0:T(8,128)(2,1)S(1)}, bf16[1536,128]{1,0:T(8,128)(2,1)S(1)}, u32[]{:S(2)}, u32[]{:S(2)}) collective-permute-start(bf16[1536,128]{1,0:T(8,128)(2,1)S(1)} %copy-done.7), channel_id=1, source_target_pairs={{0,192},{64,0},{128,64},{192,128},{1,193},{65,1},{129,65},{193,129... | collective-permute-start | bytes 1179656 | tf_op jit(solution)/shard_map/ppermute | solution.py:401
  19.0 1.2 collective-permute-start.20
  20.2 10.8 %collective-permute-done.18.refs_10_ = bf16[128,1536]{1,0:T(8,128)(2,1)S(1)} collective-permute-done((bf16[128,1536]{1,0:T(8,128)(2,1)S(1)}, bf16[128,1536]{1,0:T(8,128)(2,1)S(1)}, u32[]{:S(2)}, u32[]{:S(2)}) %collective-permute-start.18) | collective-permute-done | bytes 393248 | tf_op jit(solution)/shard_map/ppermute | solution.py:401
  31.0 1.5 collective-permute-start.13
  33.9 6.8 %collective-permute-done.10.refs_1_ = bf16[1536,128]{1,0:T(8,128)(2,1)S(1)} collective-permute-done((bf16[1536,128]{1,0:T(8,128)(2,1)S(1)}, bf16[1536,128]{1,0:T(8,128)(2,1)S(1)}, u32[]{:S(2)}, u32[]{:S(2)}) %collective-permute-start.10) | collective-permute-done | bytes 393248 | tf_op jit(solution)/shard_map/ppermute | solution.py:398
  40.7 1.6 collective-permute-start
  42.3 3.9 %collective-permute-start.1 = (bf16[128,512]{1,0:T(8,128)(2,1)S(1)}, bf16[128,512]{1,0:T(8,128)(2,1)S(1)}, u32[]{:S(2)}, u32[]{:S(2)}) collective-permute-start(bf16[128,512]{1,0:T(8,128)(2,1)S(1)} %get-tuple-element.24.refs_0_), channel_id=1, source_target_pairs={{0,7},{1,0},{2,1},{3,2},{4,3},{5,4},{6,5},{7,6},{8,15},{9,8},{10,9... | collective-permute-start | bytes 393224 | tf_op jit(solution)/shard_map/ppermute | solution.py:422
  46.2 2.9 %collective-permute-done.refs_1_ = bf16[128,512]{1,0:T(8,128)(2,1)S(1)} collective-permute-done((bf16[128,512]{1,0:T(8,128)(2,1)S(1)}, bf16[128,512]{1,0:T(8,128)(2,1)S(1)}, u32[]{:S(2)}, u32[]{:S(2)}) %collective-permute-start) | collective-permute-done | bytes 131104 | tf_op jit(solution)/shard_map/ppermute | solution.py:418
  50.7 2.6 %collective-permute-start.3 = (bf16[128,512]{1,0:T(8,128)(2,1)S(1)}, bf16[128,512]{1,0:T(8,128)(2,1)}, u32[]{:S(2)}, u32[]{:S(2)}) collective-permute-start(bf16[128,512]{1,0:T(8,128)(2,1)S(1)} %collective-permute-done.1.refs_2_), channel_id=1, source_target_pairs={{0,7},{1,0},{2,1},{3,2},{4,3},{5,4},{6,5},{7,6},{8,15},{9,8},{10,9... | collective-permute-start | bytes 393224 | tf_op jit(solution)/shard_map/ppermute | solution.py:422
  54.2 2.9 %collective-permute-start.22 = (bf16[128,1536]{1,0:T(8,128)(2,1)S(1)}, bf16[128,1536]{1,0:T(8,128)(2,1)}, u32[]{:S(2)}, u32[]{:S(2)}) collective-permute-start(bf16[128,1536]{1,0:T(8,128)(2,1)S(1)} %collective-permute-done.18.refs_10_), channel_id=1, source_target_pairs={{0,8},{8,0},{1,9},{9,1},{2,10},{10,2},{3,11},{11,3},{4,12},{12,4},... | collective-permute-start | bytes 1179656 | tf_op jit(solution)/shard_map/ppermute | solution.py:430
  57.2 2.8 %collective-permute-start.5 = (bf16[128,512]{1,0:T(8,128)(2,1)}, bf16[128,512]{1,0:T(8,128)(2,1)S(1)}, u32[]{:S(2)}, u32[]{:S(2)}) collective-permute-start(bf16[128,512]{1,0:T(8,128)(2,1)} %collective-permute-done.3.refs_4_), channel_id=1, source_target_pairs={{0,7},{1,0},{2,1},{3,2},{4,3},{5,4},{6,5},{7,6},{8,15},{9,8},{10,9... | collective-permute-start | bytes 393224 | tf_op jit(solution)/shard_map/ppermute | solution.py:422
  60.0 3.3 %collective-permute-start.14 = (bf16[1536,128]{1,0:T(8,128)(2,1)S(1)}, bf16[1536,128]{1,0:T(8,128)(2,1)S(1)}, u32[]{:S(2)}, u32[]{:S(2)}) collective-permute-start(bf16[1536,128]{1,0:T(8,128)(2,1)S(1)} %collective-permute-done.10.refs_1_), channel_id=1, source_target_pairs={{0,8},{8,0},{1,9},{9,1},{2,10},{10,2},{3,11},{11,3},{4,12},{12,4},... | collective-permute-start | bytes 1179656 | tf_op jit(solution)/shard_map/ppermute | solution.py:429
  65.2 4.4 %collective-permute-start.16 = (bf16[1536,128]{1,0:T(8,128)(2,1)}, bf16[1536,128]{1,0:T(8,128)(2,1)}, u32[]{:S(2)}, u32[]{:S(2)}) collective-permute-start(bf16[1536,128]{1,0:T(8,128)(2,1)} %collective-permute-done.12.refs_3_), channel_id=1, source_target_pairs={{0,8},{8,0},{1,9},{9,1},{2,10},{10,2},{3,11},{11,3},{4,12},{12,4},... | collective-permute-start | bytes 1179656 | tf_op jit(solution)/shard_map/ppermute | solution.py:431
  70.0 3.2 %shard_map.84.first_q = bf16[128,640]{1,0:T(8,128)(2,1)S(1)} custom-call(s32[1]{0:T(128)} %bitcast.10.z, bf16[128,128]{1,0:T(8,128)(2,1)S(1)} %get-tuple-element.23.meta, f32[1,4096]{1,0:T(1,128)S(1)} %bitcast.17, f32[128,128]{1,0:T(8,128)S(1)} %get-tuple-element.40.cosine, f32[128,128]{1,0:T(8,128)S(1)} %get-tuple-element.41.sine, ...), custom_call_target="tpu_custom_call" | custom-call | tf_op jit(solution)/shard_map/pallas_call | solution.py:39
  74.0 1.2 collective-permute-start.8
  75.9 1.5 collective-permute-start.9
  77.5 1.8 %collective-permute-start.7 = (bf16[128,640]{1,0:T(8,128)(2,1)S(1)}, bf16[128,640]{1,0:T(8,128)(2,1)S(1)}, u32[]{:S(2)}, u32[]{:S(2)}) collective-permute-start(bf16[128,640]{1,0:T(8,128)(2,1)S(1)} %shard_map.84.first_q), channel_id=1, source_target_pairs={{0,32},{16,48},{32,0},{48,16},{1,33},{17,49},{33,1},{49,17},{2,34}... | collective-permute-start | bytes 491528 | tf_op jit(solution)/shard_map/ppermute | solution.py:467
  79.3 1.6 collective-permute-done.8.first_q
  83.4 14.0 %shard_map.86 = (bf16[128,640]{1,0:T(8,128)(2,1)S(1)}, bf16[128,640]{1,0:T(8,128)(2,1)S(1)}, bf16[8,1536,128]{2,1,0:T(8,128)(2,1)S(1)}, bf16[8,144,1536]{2,1,0:T(8,128)(2,1)S(1)}) custom-call(s32[8]{0:T(128)S(1)} %stack.35.shard_ids, bf16[128,640]{1,0:T(8,128)(2,1)S(1)} %collective-permute-done.8.first_q, ...), custom_call_target="tpu_custom_call" | custom-call | flops 10000000000 | bytes 7000000 | tf_op jit(solution)/shard_map/pallas_call | solution.py:39
  97.5 12.7 %shard_map.87 = (bf16[128,640]{1,0:T(8,128)(2,1)S(1)}, bf16[128,640]{1,0:T(8,128)(2,1)S(1)}) custom-call(s32[8]{0:T(128)S(1)} %stack.35.shard_ids, bf16[128,640]{1,0:T(8,128)(2,1)S(1)} %shard_map.84.first_q, bf16[128,640]{1,0:T(8,128)(2,1)S(1)} %collective-permute-done.7.second_q, bf16[8,1536,128]{2,1,0:T(8,128)(2,1)S(1)} %get-tuple-element.31.refs_0_, ...), custom_call_target="tpu_custom_call" | custom-call | flops 10000000000 | bytes 7000000 | tf_op jit(solution)/shard_map/pallas_call | solution.py:39
  110.2 1.7 collective-permute-start.26
  113.4 2.6 %collective-permute-done.26.refs_3_ = bf16[128,640]{1,0:T(8,128)(2,1)S(1)} collective-permute-done((bf16[128,640]{1,0:T(8,128)(2,1)S(1)}, bf16[128,640]{1,0:T(8,128)(2,1)S(1)}, u32[]{:S(2)}, u32[]{:S(2)}) %collective-permute-start.26) | collective-permute-done | bytes 163872 | tf_op jit(solution)/shard_map/ppermute | solution.py:473
  116.5 1.9 %collective-permute-done.25.refs_2_ = bf16[128,640]{1,0:T(8,128)(2,1)S(1)} collective-permute-done((bf16[128,640]{1,0:T(8,128)(2,1)S(1)}, bf16[128,640]{1,0:T(8,128)(2,1)S(1)}, u32[]{:S(2)}, u32[]{:S(2)}) %collective-permute-start.25) | collective-permute-done | bytes 163872 | tf_op jit(solution)/shard_map/ppermute | solution.py:471
  118.4 1.4 shard_map.88
  119.8 28.1 %all_to_all.15.parts = bf16[8,128,512]{2,1,0:T(8,128)(2,1)S(1)} all-to-all(bf16[8,128,512]{2,1,0:T(8,128)(2,1)S(1)} %shard_map.88), channel_id=1, replica_groups=mesh['seq_0'=4,'seq_1'=4,'seq_2'=2,'head'=8] {'head'}, dimensions={0} | all-to-all | bytes 2097152 | tf_op jit(solution)/shard_map/all_to_all | solution.py:482
  147.9 1.3 shard_map.89
  149.2 22.4 %all_to_all.16 = bf16[32,16,512]{2,1,0:T(8,128)(2,1)S(1)} all-to-all(bf16[32,16,512]{2,1,0:T(8,128)(2,1)S(1)} %bitcast.14), channel_id=1, replica_groups=mesh['seq_0'=4,'seq_1'=4,'seq_2'=2,'head'=8] {'seq_0','seq_1','seq_2'}, dimensions={0} | all-to-all | bytes 1048576 | tf_op jit(solution)/shard_map/all_to_all | solution.py:486
  171.6 1.1 shard_map.90
  (73 shorter events, 13.2 us)
Async XLA Ops:
  4.8 27.7 %all-to-all-start = ((bf16[32,16,640]{2,1,0:T(8,128)(2,1)}), bf16[32,16,640]{2,1,0:T(8,128)(2,1)S(1)}, u32[]{:S(2)}, u32[]{:S(2)}) async-start(bf16[32,16,640]{2,1,0:T(8,128)(2,1)} %bitcast), calls=%async_computation | async-start | bytes 1310720 | tf_op jit(solution)/shard_map/all_to_all | solution.py:395
  13.6 17.4 %collective-permute-start.18 = (bf16[128,1536]{1,0:T(8,128)(2,1)S(1)}, bf16[128,1536]{1,0:T(8,128)(2,1)S(1)}, u32[]{:S(2)}, u32[]{:S(2)}) collective-permute-start(bf16[128,1536]{1,0:T(8,128)(2,1)S(1)} %shard_map.85.refs_8_), channel_id=1, source_target_pairs={{0,192},{64,0},{128,64},{192,128},{1,193},{65,1},{129,65},{193,129... | collective-permute-start | bytes 1179656 | tf_op jit(solution)/shard_map/ppermute | solution.py:401
  16.3 26.1 %collective-permute-start.17 = (bf16[128,1536]{1,0:T(8,128)(2,1)S(1)}, bf16[128,1536]{1,0:T(8,128)(2,1)S(1)}, u32[]{:S(2)}, u32[]{:S(2)}) collective-permute-start(bf16[128,1536]{1,0:T(8,128)(2,1)S(1)} %shard_map.85.refs_8_), channel_id=1, source_target_pairs={{0,64},{64,128},{128,192},{192,0},{1,65},{65,129},{129,193},{193,1... | collective-permute-start | bytes 1179656 | tf_op jit(solution)/shard_map/ppermute | solution.py:398
  16.3 24.4 %collective-permute-start.10 = (bf16[1536,128]{1,0:T(8,128)(2,1)S(1)}, bf16[1536,128]{1,0:T(8,128)(2,1)S(1)}, u32[]{:S(2)}, u32[]{:S(2)}) collective-permute-start(bf16[1536,128]{1,0:T(8,128)(2,1)S(1)} %copy-done.7), channel_id=1, source_target_pairs={{0,64},{64,128},{128,192},{192,0},{1,65},{65,129},{129,193},{193,1... | collective-permute-start | bytes 1179656 | tf_op jit(solution)/shard_map/ppermute | solution.py:398
  16.5 32.7 %collective-permute-start.11 = (bf16[1536,128]{1,0:T(8,128)(2,1)S(1)}, bf16[1536,128]{1,0:T(8,128)(2,1)S(1)}, u32[]{:S(2)}, u32[]{:S(2)}) collective-permute-start(bf16[1536,128]{1,0:T(8,128)(2,1)S(1)} %copy-done.7), channel_id=1, source_target_pairs={{0,192},{64,0},{128,64},{192,128},{1,193},{65,1},{129,65},{193,129... | collective-permute-start | bytes 1179656 | tf_op jit(solution)/shard_map/ppermute | solution.py:401
  19.0 30.8 %collective-permute-start.20 = (bf16[128,1536]{1,0:T(8,128)(2,1)S(1)}, bf16[128,1536]{1,0:T(8,128)(2,1)}, u32[]{:S(2)}, u32[]{:S(2)}) collective-permute-start(bf16[128,1536]{1,0:T(8,128)(2,1)S(1)} %shard_map.85.refs_8_), channel_id=1, source_target_pairs={{0,8},{8,0},{1,9},{9,1},{2,10},{10,2},{3,11},{11,3},{4,12},{12,4},... | collective-permute-start | bytes 1179656 | tf_op jit(solution)/shard_map/ppermute | solution.py:430
  31.0 23.2 %collective-permute-start.13 = (bf16[1536,128]{1,0:T(8,128)(2,1)S(1)}, bf16[1536,128]{1,0:T(8,128)(2,1)}, u32[]{:S(2)}, u32[]{:S(2)}) collective-permute-start(bf16[1536,128]{1,0:T(8,128)(2,1)S(1)} %copy-done.7), channel_id=1, source_target_pairs={{0,8},{8,0},{1,9},{9,1},{2,10},{10,2},{3,11},{11,3},{4,12},{12,4},... | collective-permute-start | bytes 1179656 | tf_op jit(solution)/shard_map/ppermute | solution.py:429
  32.5 37.5 %copy-start.5 = (f32[4096]{0:T(1024)S(1)}, f32[4096]{0:T(1024)}, u32[]{:S(2)}) copy-start(f32[4096]{0:T(1024)} %param.9) | copy-start | bytes 49156
  33.9 36.1 %copy-start.3 = (bf16[128,512]{1,0:T(8,128)(2,1)}, bf16[128,512]{1,0:T(8,128)(2,1)S(1)}, u32[]{:S(2)}) copy-start(bf16[128,512]{1,0:T(8,128)(2,1)S(1)} %get-tuple-element.24.refs_0_) | copy-start | bytes 393220
  40.7 8.5 %collective-permute-start = (bf16[128,512]{1,0:T(8,128)(2,1)S(1)}, bf16[128,512]{1,0:T(8,128)(2,1)S(1)}, u32[]{:S(2)}, u32[]{:S(2)}) collective-permute-start(bf16[128,512]{1,0:T(8,128)(2,1)S(1)} %get-tuple-element.24.refs_0_), channel_id=1, source_target_pairs={{0,1},{1,2},{2,3},{3,4},{4,5},{5,6},{6,7},{7,0},{8,9},{9,10},{10,1... | collective-permute-start | bytes 393224 | tf_op jit(solution)/shard_map/ppermute | solution.py:418
  42.3 8.4 %collective-permute-start.1 = (bf16[128,512]{1,0:T(8,128)(2,1)S(1)}, bf16[128,512]{1,0:T(8,128)(2,1)S(1)}, u32[]{:S(2)}, u32[]{:S(2)}) collective-permute-start(bf16[128,512]{1,0:T(8,128)(2,1)S(1)} %get-tuple-element.24.refs_0_), channel_id=1, source_target_pairs={{0,7},{1,0},{2,1},{3,2},{4,3},{5,4},{6,5},{7,6},{8,15},{9,8},{10,9... | collective-permute-start | bytes 393224 | tf_op jit(solution)/shard_map/ppermute | solution.py:422
  49.2 20.8 %copy-start.12 = (bf16[128,512]{1,0:T(8,128)(2,1)}, bf16[128,512]{1,0:T(8,128)(2,1)S(1)}, u32[]{:S(2)}) copy-start(bf16[128,512]{1,0:T(8,128)(2,1)S(1)} %collective-permute-done.refs_1_) | copy-start | bytes 393220
  49.2 5.0 %collective-permute-start.2 = (bf16[128,512]{1,0:T(8,128)(2,1)S(1)}, bf16[128,512]{1,0:T(8,128)(2,1)S(1)}, u32[]{:S(2)}, u32[]{:S(2)}) collective-permute-start(bf16[128,512]{1,0:T(8,128)(2,1)S(1)} %collective-permute-done.refs_1_), channel_id=1, source_target_pairs={{0,1},{1,2},{2,3},{3,4},{4,5},{5,6},{6,7},{7,0},{8,9},{9,10},{10,1... | collective-permute-start | bytes 393224 | tf_op jit(solution)/shard_map/ppermute | solution.py:418
  49.2 10.8 %collective-permute-start.19 = (bf16[128,1536]{1,0:T(8,128)(2,1)S(1)}, bf16[128,1536]{1,0:T(8,128)(2,1)S(1)}, u32[]{:S(2)}, u32[]{:S(2)}) collective-permute-start(bf16[128,1536]{1,0:T(8,128)(2,1)S(1)} %collective-permute-done.18.refs_10_), channel_id=1, source_target_pairs={{0,192},{64,0},{128,64},{192,128},{1,193},{65,1},{129,65},{193,129... | collective-permute-start | bytes 1179656 | tf_op jit(solution)/shard_map/ppermute | solution.py:427
  49.8 13.5 %collective-permute-start.12 = (bf16[1536,128]{1,0:T(8,128)(2,1)S(1)}, bf16[1536,128]{1,0:T(8,128)(2,1)}, u32[]{:S(2)}, u32[]{:S(2)}) collective-permute-start(bf16[1536,128]{1,0:T(8,128)(2,1)S(1)} %collective-permute-done.10.refs_1_), channel_id=1, source_target_pairs={{0,64},{64,128},{128,192},{192,0},{1,65},{65,129},{129,193},{193,1... | collective-permute-start | bytes 1179656 | tf_op jit(solution)/shard_map/ppermute | solution.py:426
  50.7 6.4 %collective-permute-start.3 = (bf16[128,512]{1,0:T(8,128)(2,1)S(1)}, bf16[128,512]{1,0:T(8,128)(2,1)}, u32[]{:S(2)}, u32[]{:S(2)}) collective-permute-start(bf16[128,512]{1,0:T(8,128)(2,1)S(1)} %collective-permute-done.1.refs_2_), channel_id=1, source_target_pairs={{0,7},{1,0},{2,1},{3,2},{4,3},{5,4},{6,5},{7,6},{8,15},{9,8},{10,9... | collective-permute-start | bytes 393224 | tf_op jit(solution)/shard_map/ppermute | solution.py:422
  54.2 5.7 %collective-permute-start.4 = (bf16[128,512]{1,0:T(8,128)(2,1)S(1)}, bf16[128,512]{1,0:T(8,128)(2,1)}, u32[]{:S(2)}, u32[]{:S(2)}) collective-permute-start(bf16[128,512]{1,0:T(8,128)(2,1)S(1)} %collective-permute-done.2.refs_3_), channel_id=1, source_target_pairs={{0,1},{1,2},{2,3},{3,4},{4,5},{5,6},{6,7},{7,0},{8,9},{9,10},{10,1... | collective-permute-start | bytes 393224 | tf_op jit(solution)/shard_map/ppermute | solution.py:418
  54.2 9.4 %collective-permute-start.22 = (bf16[128,1536]{1,0:T(8,128)(2,1)S(1)}, bf16[128,1536]{1,0:T(8,128)(2,1)}, u32[]{:S(2)}, u32[]{:S(2)}) collective-permute-start(bf16[128,1536]{1,0:T(8,128)(2,1)S(1)} %collective-permute-done.18.refs_10_), channel_id=1, source_target_pairs={{0,8},{8,0},{1,9},{9,1},{2,10},{10,2},{3,11},{11,3},{4,12},{12,4},... | collective-permute-start | bytes 1179656 | tf_op jit(solution)/shard_map/ppermute | solution.py:430
  57.2 6.9 %collective-permute-start.5 = (bf16[128,512]{1,0:T(8,128)(2,1)}, bf16[128,512]{1,0:T(8,128)(2,1)S(1)}, u32[]{:S(2)}, u32[]{:S(2)}) collective-permute-start(bf16[128,512]{1,0:T(8,128)(2,1)} %collective-permute-done.3.refs_4_), channel_id=1, source_target_pairs={{0,7},{1,0},{2,1},{3,2},{4,3},{5,4},{6,5},{7,6},{8,15},{9,8},{10,9... | collective-permute-start | bytes 393224 | tf_op jit(solution)/shard_map/ppermute | solution.py:422
  59.9 5.2 %collective-permute-start.6 = (bf16[128,512]{1,0:T(8,128)(2,1)}, bf16[128,512]{1,0:T(8,128)(2,1)S(1)}, u32[]{:S(2)}, u32[]{:S(2)}) collective-permute-start(bf16[128,512]{1,0:T(8,128)(2,1)} %collective-permute-done.4.refs_5_), channel_id=1, source_target_pairs={{0,1},{1,2},{2,3},{3,4},{4,5},{5,6},{6,7},{7,0},{8,9},{9,10},{10,1... | collective-permute-start | bytes 393224 | tf_op jit(solution)/shard_map/ppermute | solution.py:418
  60.0 13.3 %collective-permute-start.14 = (bf16[1536,128]{1,0:T(8,128)(2,1)S(1)}, bf16[1536,128]{1,0:T(8,128)(2,1)S(1)}, u32[]{:S(2)}, u32[]{:S(2)}) collective-permute-start(bf16[1536,128]{1,0:T(8,128)(2,1)S(1)} %collective-permute-done.10.refs_1_), channel_id=1, source_target_pairs={{0,8},{8,0},{1,9},{9,1},{2,10},{10,2},{3,11},{11,3},{4,12},{12,4},... | collective-permute-start | bytes 1179656 | tf_op jit(solution)/shard_map/ppermute | solution.py:429
  63.3 11.9 %collective-permute-start.21 = (bf16[128,1536]{1,0:T(8,128)(2,1)S(1)}, bf16[128,1536]{1,0:T(8,128)(2,1)S(1)}, u32[]{:S(2)}, u32[]{:S(2)}) collective-permute-start(bf16[128,1536]{1,0:T(8,128)(2,1)S(1)} %collective-permute-done.17.refs_9_), channel_id=1, source_target_pairs={{0,8},{8,0},{1,9},{9,1},{2,10},{10,2},{3,11},{11,3},{4,12},{12,4},... | collective-permute-start | bytes 1179656 | tf_op jit(solution)/shard_map/ppermute | solution.py:430
  63.6 13.9 %collective-permute-start.15 = (bf16[1536,128]{1,0:T(8,128)(2,1)S(1)}, bf16[1536,128]{1,0:T(8,128)(2,1)}, u32[]{:S(2)}, u32[]{:S(2)}) collective-permute-start(bf16[1536,128]{1,0:T(8,128)(2,1)S(1)} %collective-permute-done.11.refs_2_), channel_id=1, source_target_pairs={{0,8},{8,0},{1,9},{9,1},{2,10},{10,2},{3,11},{11,3},{4,12},{12,4},... | collective-permute-start | bytes 1179656 | tf_op jit(solution)/shard_map/ppermute | solution.py:429
  64.1 15.3 %collective-permute-start.23 = (bf16[128,1536]{1,0:T(8,128)(2,1)S(1)}, bf16[128,1536]{1,0:T(8,128)(2,1)}, u32[]{:S(2)}, u32[]{:S(2)}) collective-permute-start(bf16[128,1536]{1,0:T(8,128)(2,1)S(1)} %collective-permute-done.19.refs_11_), channel_id=1, source_target_pairs={{0,8},{8,0},{1,9},{9,1},{2,10},{10,2},{3,11},{11,3},{4,12},{12,4},... | collective-permute-start | bytes 1179656 | tf_op jit(solution)/shard_map/ppermute | solution.py:432
  65.2 14.2 %collective-permute-start.16 = (bf16[1536,128]{1,0:T(8,128)(2,1)}, bf16[1536,128]{1,0:T(8,128)(2,1)}, u32[]{:S(2)}, u32[]{:S(2)}) collective-permute-start(bf16[1536,128]{1,0:T(8,128)(2,1)} %collective-permute-done.12.refs_3_), channel_id=1, source_target_pairs={{0,8},{8,0},{1,9},{9,1},{2,10},{10,2},{3,11},{11,3},{4,12},{12,4},... | collective-permute-start | bytes 1179656 | tf_op jit(solution)/shard_map/ppermute | solution.py:431
  74.0 7.0 %collective-permute-start.8 = (bf16[128,640]{1,0:T(8,128)(2,1)S(1)}, bf16[128,640]{1,0:T(8,128)(2,1)S(1)}, u32[]{:S(2)}, u32[]{:S(2)}) collective-permute-start(bf16[128,640]{1,0:T(8,128)(2,1)S(1)} %shard_map.84.first_q), channel_id=1, source_target_pairs={{0,16},{16,32},{32,48},{48,0},{1,17},{17,33},{33,49},{49,1},{2,18}... | collective-permute-start | bytes 491528 | tf_op jit(solution)/shard_map/ppermute | solution.py:466
  75.9 5.5 %collective-permute-start.9 = (bf16[128,640]{1,0:T(8,128)(2,1)S(1)}, bf16[128,640]{1,0:T(8,128)(2,1)S(1)}, u32[]{:S(2)}, u32[]{:S(2)}) collective-permute-start(bf16[128,640]{1,0:T(8,128)(2,1)S(1)} %shard_map.84.first_q), channel_id=1, source_target_pairs={{0,48},{16,0},{32,16},{48,32},{1,49},{17,1},{33,17},{49,33},{2,50}... | collective-permute-start | bytes 491528 | tf_op jit(solution)/shard_map/ppermute | solution.py:466
  77.5 19.9 %collective-permute-start.7 = (bf16[128,640]{1,0:T(8,128)(2,1)S(1)}, bf16[128,640]{1,0:T(8,128)(2,1)S(1)}, u32[]{:S(2)}, u32[]{:S(2)}) collective-permute-start(bf16[128,640]{1,0:T(8,128)(2,1)S(1)} %shard_map.84.first_q), channel_id=1, source_target_pairs={{0,32},{16,48},{32,0},{48,16},{1,33},{17,49},{33,1},{49,17},{2,34}... | collective-permute-start | bytes 491528 | tf_op jit(solution)/shard_map/ppermute | solution.py:467
  97.4 20.9 %copy-start = (bf16[512,4096]{1,0:T(8,128)(2,1)S(1)}, bf16[512,4096]{1,0:T(8,128)(2,1)}, u32[]{:S(2)}) copy-start(bf16[512,4096]{1,0:T(8,128)(2,1)} %weight.3) | copy-start | bytes 12582916
  110.2 5.8 %collective-permute-start.26 = (bf16[128,640]{1,0:T(8,128)(2,1)S(1)}, bf16[128,640]{1,0:T(8,128)(2,1)S(1)}, u32[]{:S(2)}, u32[]{:S(2)}) collective-permute-start(bf16[128,640]{1,0:T(8,128)(2,1)S(1)} %get-tuple-element.36), channel_id=1, source_target_pairs={{0,32},{16,48},{32,0},{48,16},{1,33},{17,49},{33,1},{49,17},{2,34}... | collective-permute-start | bytes 491528 | tf_op jit(solution)/shard_map/ppermute | solution.py:473
  111.9 4.5 %collective-permute-start.24 = (bf16[128,640]{1,0:T(8,128)(2,1)S(1)}, bf16[128,640]{1,0:T(8,128)(2,1)S(1)}, u32[]{:S(2)}, u32[]{:S(2)}) collective-permute-start(bf16[128,640]{1,0:T(8,128)(2,1)S(1)} %get-tuple-element.34), channel_id=1, source_target_pairs={{0,48},{16,0},{32,16},{48,32},{1,49},{17,1},{33,17},{49,33},{2,50}... | collective-permute-start | bytes 491528 | tf_op jit(solution)/shard_map/ppermute | solution.py:470
  113.0 5.4 %collective-permute-start.25 = (bf16[128,640]{1,0:T(8,128)(2,1)S(1)}, bf16[128,640]{1,0:T(8,128)(2,1)S(1)}, u32[]{:S(2)}, u32[]{:S(2)}) collective-permute-start(bf16[128,640]{1,0:T(8,128)(2,1)S(1)} %get-tuple-element.35), channel_id=1, source_target_pairs={{0,16},{16,32},{32,48},{48,0},{1,17},{17,33},{33,49},{49,1},{2,18}... | collective-permute-start | bytes 491528 | tf_op jit(solution)/shard_map/ppermute | solution.py:471
  (12 other events, 61.3 us)
